TPU v7x, 128 devices: a whole 4x4x4 slice. The times are simulated.
128 devices in a mesh: own: 16 (over y, z), red: 8 (over x, core).
Axes of the slice: x: 4, y: 4, z: 4, core: 2. Of those that a mesh axis runs over, the one named last changes fastest.
Arguments:
- amp_tiles: bfloat16 [8192, 128, 128], P(('own', 'red')), may hold values from -6 to 6
- int_tiles: bfloat16 [8192, 128, 128], P(('own', 'red')), may hold values from -0.0625 to 0.0625
- requests: int32 [16, 8, 16, 2, 8], P('own', 'red'), may hold values from -1 to 63, as said below
- tri_amp: int32 [512, 8, 64], P('own', 'red'), may hold values from 0 to 127, as said below
- tri_int: int32 [512, 8, 64], P('own', 'red'), may hold values from 0 to 127, as said below
- tri_count: int32 [512, 8], P('own', 'red'), may hold values from 1 to 64, as said below
Outputs:
- residual: float32 [512, 128, 128], P(('own', 'red'))
Inputs may be any that keep to these rules, and one draw needn't show every extreme that they name: -1 marks an empty slot and live slots come first; the live numbers in one row of 8 slots are distinct; every owner device has 8 live amplitude requests to some holder and 8 live integral requests to some holder. tri_amp[t, r, k] // 8 is a holder h and tri_amp[t, r, k] % 8 is below the number of live amplitude requests of the owner of t, on red index r, to h. `tri_int`: likewise for the integral requests. `tri_count`: on every owner and red index some residual tile has 64 live triples.
All inputs are finite; a program needn't handle non-finite values.
Results may differ from a plain program's by a relative error of at most 0.0003.
Values may be sent and summed in bfloat16 or wider, within the bound.
No kernel may reach another device: no remote copies, remote signals or barrier semaphores. Data moves between devices by JAX's collectives and lax.ppermute only.
A program may use at most 128 MiB of HBM per device.

v0:
```python
import functools

import jax
import jax.numpy as jnp
from jax import lax
from jax.experimental import pallas as pl
from jax.experimental.pallas import tpu as pltpu
from jax.sharding import PartitionSpec as P

GROUP = 4
UNROLL = 4
PACK_STEPS = 4


def pack_body(lists, asked, *refs):
    stores, outs = refs[:2], refs[2:]
    cap = asked.shape[1] // 2
    last = stores[0].shape[0] - 1
    peers = outs[0].shape[0]
    first = pl.program_id(0) * peers
    for peer in range(peers):
        for out, picks in zip(outs, lists):
            for pos, (kind, slot) in enumerate(picks):
                tile = jnp.clip(asked[first + peer, kind * cap + slot], 0, last)
                out[peer, pos] = stores[kind][tile]


def pack(lists, asked, stores):
    peers = asked.shape[0]
    tile = stores[0].shape[1:]
    whole = pl.BlockSpec(stores[0].shape, lambda i: (0, 0, 0))
    return pl.pallas_call(
        functools.partial(pack_body, lists),
        grid=(PACK_STEPS,),
        in_specs=[pl.BlockSpec(memory_space=pltpu.SMEM), whole, whole],
        out_specs=[
            pl.BlockSpec((peers // PACK_STEPS, len(picks)) + tile, lambda i: (i, 0, 0, 0)) for picks in lists
        ],
        out_shape=[jax.ShapeDtypeStruct((peers, len(picks)) + tile, stores[0].dtype) for picks in lists],
    )(asked, *stores)


def group_dot(lefts, rights):
    return lax.dot_general(
        jnp.concatenate(lefts, axis=1),
        jnp.concatenate(rights, axis=1),
        (((1,), (1,)), ((), ())),
        preferred_element_type=jnp.float32,
    )


def contract(bounds, left_at, right_at, table, ends, left, right, acc, first, part):
    places = acc.shape[0]
    begin, finish = bounds[first // places], bounds[first // places + 1]

    def full_step(i, carry):
        sums = []
        for u in range(UNROLL):
            g = begin + i * UNROLL + u
            row, base = table[0, g], table[1, g]
            lefts = [left[left_at[row, base + j]] for j in range(GROUP)]
            rights = [right[right_at[row, base + j]] for j in range(GROUP)]
            sums.append(group_dot(lefts, rights))
        for u in range(UNROLL):
            g = begin + i * UNROLL + u
            place = jnp.minimum(table[2, g] - first, places - 1)
            acc[place] = acc[place] + jnp.where(g < finish, sums[u], 0.0)
        return carry

    lax.fori_loop(0, (finish - begin + UNROLL - 1) // UNROLL, full_step, 0)

    def rest_step(i, carry):
        sums = []
        for u in range(UNROLL):
            place = first + i * UNROLL + u
            row, stop = ends[0, place], ends[1, place]
            base = stop - ends[2, place] % GROUP
            lefts, rights = [], []
            for j in range(GROUP):
                tile = left[left_at[row, base + j]]
                lefts.append(jnp.where(base + j < stop, tile, jnp.zeros_like(tile)))
                rights.append(right[right_at[row, base + j]])
            sums.append(group_dot(lefts, rights))
        for u in range(UNROLL):
            place = i * UNROLL + u
            acc[place] = acc[place] + sums[u]
        return carry

    lax.fori_loop(0, places // UNROLL, rest_step, 0)


def flatten(ref):
    return ref.reshape((ref.shape[0] * ref.shape[1],) + ref.shape[2:])


def first_body(bounds, left_at, right_at, table, ends, got, out):
    out[...] = jnp.zeros(out.shape, out.dtype)
    flat = flatten(got)
    contract(bounds, left_at, right_at, table, ends, flat, flat, out, 0, 0)


def second_body(first, bounds, left_at, right_at, table, ends, got, rest, before, other, mine, acc):
    places = acc.shape[0]
    acc[...] = before[pl.ds(first, places)]
    contract(bounds, left_at, right_at, table, ends, flatten(got), flatten(rest), acc, first, 1)
    other[...] = acc[pl.ds(0, places // 2)]
    mine[...] = acc[pl.ds(places // 2, places // 2)]


def group_table(order, start, stop, slots):
    rows = start.shape[0]
    at = order[:, None] == jnp.arange(rows)[None, :]

    def in_order(values):
        return jnp.sum(jnp.where(at, values[None, :], 0), axis=1)

    start, stop = in_order(start), in_order(stop)
    size = (stop - start) // GROUP
    end = jnp.sum(jnp.where(jnp.arange(rows)[:, None] >= jnp.arange(rows)[None, :], size[None, :], 0), axis=1)
    limit = rows * (slots // GROUP) + 2 * UNROLL
    number = jnp.arange(limit, dtype=jnp.int32)[:, None]
    passed = number >= end[None, :]
    place = jnp.minimum(jnp.sum(passed.astype(jnp.int32), axis=1), rows - 1)
    opened = jnp.max(jnp.where(passed, end[None, :], 0), axis=1)
    mine = place[:, None] == jnp.arange(rows)[None, :]

    def of_place(values):
        return jnp.sum(jnp.where(mine, values[None, :], 0), axis=1)

    base = of_place(start) + (number[:, 0] - opened) * GROUP
    base = jnp.where(number[:, 0] < end[-1], base, slots)
    table = jnp.stack([of_place(order), base, place]).astype(jnp.int32)
    ends = jnp.stack([order, stop, stop - start]).astype(jnp.int32)
    return end.astype(jnp.int32), table, ends


def body(amp_tiles, int_tiles, requests, tri_amp, tri_int, tri_count):
    wanted = requests[0, 0]
    peers, kinds, cap = wanted.shape
    rows, slots = tri_amp.shape[0], tri_amp.shape[2]
    tile = amp_tiles.shape[1:]
    cut = cap // 2
    red = lax.axis_size("red")
    share = rows // red
    steps = red // 2
    me = lax.axis_index("red")

    wanted, me = lax.optimization_barrier((wanted, me))
    asked = lax.all_to_all(wanted.reshape(peers, kinds * cap), "own", split_axis=0, concat_axis=0, tiled=True)
    first_list = tuple((0, s) for s in range(cap)) + tuple((1, s) for s in range(cut))
    second_list = tuple((1, s) for s in range(cut, cap))
    asked, me = lax.optimization_barrier((asked, me))
    send_first, send_second = pack((first_list, second_list), asked, (amp_tiles, int_tiles))
    got_first = lax.all_to_all(send_first, "own", split_axis=0, concat_axis=0, tiled=True)
    got_first, send_second, tri_amp, tri_int, tri_count, me = lax.optimization_barrier(
        (got_first, send_second, tri_amp, tri_int, tri_count, me)
    )
    got_second = lax.all_to_all(send_second, "own", split_axis=0, concat_axis=0, tiled=True)

    amp_pos, int_pos = tri_amp[:, 0], tri_int[:, 0]
    count = tri_count[:, 0]
    alive = lax.broadcasted_iota(jnp.int32, (rows, slots), 1) < count[:, None]
    is_low = int_pos % cap < cut
    key = jnp.where(alive, jnp.where(is_low, 0, 1), 2)
    code = lax.sort((key * peers * cap + amp_pos) * peers * cap + int_pos, dimension=1)
    low = jnp.sum((alive & is_low).astype(jnp.int32), axis=1)
    amp_pos = (code // (peers * cap)) % (peers * cap)
    int_pos = code % (peers * cap)
    pad = ((0, 0), (0, GROUP))
    width = cap + cut
    holder, slot = int_pos // cap, int_pos % cap
    left_at = jnp.pad((amp_pos // cap) * width + amp_pos % cap, pad)
    right_at = jnp.where(slot < cut, holder * width + cap + slot, holder * (cap - cut) + slot - cut)
    right_at = jnp.pad(jnp.where(code < 2 * (peers * cap) ** 2, right_at, 0), pad)

    place = jnp.arange(rows, dtype=jnp.int32)
    step, side = place // (2 * share), (place // share) % 2
    order = (((me // 2 + step) % steps) * 2 + jnp.where(side == 0, 1 - me % 2, me % 2)) * share + place % share
    first_end, first_table, first_ends = group_table(order, jnp.zeros_like(low), low, slots)
    second_end, second_table, second_ends = group_table(order, low, count, slots)
    first_bounds = jnp.pad(first_end[rows - 1 :], (1, 0))
    second_bounds = jnp.pad(second_end[2 * share - 1 :: 2 * share], (1, 0))

    smem = pl.BlockSpec(memory_space=pltpu.SMEM)
    vmem = pl.BlockSpec(memory_space=pltpu.VMEM)
    params = pltpu.CompilerParams(vmem_limit_bytes=24 * 2**20)
    before = pl.pallas_call(
        first_body,
        in_specs=[smem] * 5 + [vmem],
        out_specs=vmem,
        out_shape=jax.ShapeDtypeStruct((rows,) + tile, jnp.float32),
        compiler_params=params,
    )(first_bounds, left_at, right_at, first_table, first_ends, got_first)

    def second(step):
        half = jax.ShapeDtypeStruct((share,) + tile, jnp.float32)
        return pl.pallas_call(
            functools.partial(second_body, step * 2 * share),
            in_specs=[smem] * 5 + [vmem] * 3,
            out_specs=[vmem, vmem],
            out_shape=[half, half],
            scratch_shapes=[pltpu.VMEM((2 * share,) + tile, jnp.float32)],
            compiler_params=params,
        )(second_bounds, left_at, right_at, second_table, second_ends, got_first, got_second, before)

    swap = [(i, i ^ 1) for i in range(red)]
    arrived = []
    for step in [steps // 2] + [s for s in range(1, steps) if s != steps // 2]:
        other, mine = second(step)
        block = mine + lax.ppermute(other, "red", swap)
        arrived.append(lax.ppermute(block, "red", [(i, ((i // 2 + step) % steps) * 2 + i % 2) for i in range(red)]))
    other, mine = second(0)
    total = mine + lax.ppermute(other, "red", swap)
    for block in arrived:
        total = total + block
    return total


def solution(mesh):
    placed = (
        P(("own", "red"), None, None),
        P(("own", "red"), None, None),
        P("own", "red", None, None, None),
        P("own", "red", None),
        P("own", "red", None),
        P("own", "red"),
    )
    return jax.shard_map(
        body, mesh=mesh, in_specs=placed, out_specs=P(("own", "red"), None, None), check_vma=False
    )
```

profile of v0, /device:TPU:1, one launch (start us, length us, event | category | flops | bytes accessed | tf_op | source)
XLA Modules:
  0.0 171.7 jit_solution(6155977381569046195)
XLA Ops:
  0.0 0.8 copy.22
  0.8 14.9 %all_to_all.22 = s32[16,1,16]{2,1,0:T(1,128)} all-to-all(s32[16,1,16]{2,1,0:T(1,128)S(1)} %copy.22), channel_id=1, replica_groups=mesh['own'=16,'red'=8] {'own'}, dimensions={0} | all-to-all | bytes 2048 | tf_op jit(solution)/shard_map/all_to_all | solution.py:149
  15.7 5.9 %shard_map.64 = (bf16[16,12,128,128]{3,2,1,0:T(8,128)(2,1)}, bf16[16,4,128,128]{3,2,1,0:T(8,128)(2,1)}) custom-call(s32[16,16]{1,0:T(8,128)} %bitcast.12, bf16[64,128,128]{2,1,0:T(8,128)(2,1)} %refs_0_.1, bf16[64,128,128]{2,1,0:T(8,128)(2,1)} %refs_1_.1), custom_call_target="tpu_custom_call" | custom-call | tf_op jit(solution)/shard_map/pallas_call | solution.py:32
  21.6 75.9 %all_to_all.23.got = bf16[16,12,128,128]{3,2,1,0:T(8,128)(2,1)} all-to-all(bf16[16,12,128,128]{3,2,1,0:T(8,128)(2,1)} %get-tuple-element.30), channel_id=1, replica_groups=mesh['own'=16,'red'=8] {'own'}, dimensions={0} | all-to-all | bytes 12582912 | tf_op jit(solution)/shard_map/all_to_all | solution.py:154
  97.5 0.1 multiply_add_fusion
  97.5 0.2 convert_reduce_fusion.2
  97.7 3.7 %all-to-all-start.2 = ((bf16[16,4,128,128]{3,2,1,0:T(8,128)(2,1)}), bf16[16,4,128,128]{3,2,1,0:T(8,128)(2,1)S(1)}, u32[]{:S(2)}, u32[]{:S(2)}) async-start(bf16[16,4,128,128]{3,2,1,0:T(8,128)(2,1)} %get-tuple-element.39), calls=%async_computation.2 | async-start | bytes 4194304 | tf_op jit(solution)/shard_map/all_to_all | solution.py:158
  101.5 0.2 select_reduce_fusion.7
  101.7 0.1 select_reduce_fusion.5
  101.8 0.6 slice.11
  102.4 0.1 slice.10
  102.5 0.6 slice.12
  103.0 0.1 select_reduce_fusion
  103.2 0.1 select_reduce_fusion.2
  103.3 0.1 select_reduce_fusion.4
  103.4 0.6 pad.18.bounds
  104.1 0.1 copy.23
  104.2 1.0 sort.14
  105.2 0.1 copy.24
  105.3 0.1 select_select_fusion
  105.4 0.1 pad.15.bounds
  105.4 0.6 compare_select_fusion
  106.1 2.8 %copy-done = bf16[16,12,128,128]{3,2,1,0:T(8,128)(2,1)S(1)} copy-done((bf16[16,12,128,128]{3,2,1,0:T(8,128)(2,1)S(1)}, bf16[16,12,128,128]{3,2,1,0:T(8,128)(2,1)}, u32[]{:S(2)}) %copy-start) | copy-done | bytes 6291480
  108.9 8.2 %shard_map.65.before = f32[32,128,128]{2,1,0:T(8,128)S(1)} custom-call(s32[2]{0:T(128)S(1)} %pad.18.bounds, s32[32,68]{1,0:T(8,128)S(1)} %pad.16.left_at, s32[32,68]{1,0:T(8,128)S(1)} %pad.17.right_at, s32[3,520]{1,0:T(4,128)S(1)} %pad_add_fusion.1.table, s32[3,32]{1,0:T(4,128)S(1)} %get-tuple-element.61.ends, bf16[16,12,128,128]{3,2,1,0:T(8,128)(2,1)S(1)} %copy-done), custom_call_target="tpu_custom_call" | custom-call | tf_op jit(solution)/shard_map/pallas_call | solution.py:187
  117.1 1.3 copy-done.2
  118.4 0.6 compare_select_fusion.1
  119.0 7.9 %all-to-all-done.2.rest = bf16[16,4,128,128]{3,2,1,0:T(8,128)(2,1)S(1)} async-done(((bf16[16,4,128,128]{3,2,1,0:T(8,128)(2,1)}), bf16[16,4,128,128]{3,2,1,0:T(8,128)(2,1)S(1)}, u32[]{:S(2)}, u32[]{:S(2)}) %all-to-all-start.2) | async-done | bytes 2097184 | tf_op jit(solution)/shard_map/all_to_all | solution.py:158
  127.0 2.8 %copy-done.1 = bf16[16,12,128,128]{3,2,1,0:T(8,128)(2,1)S(1)} copy-done((bf16[16,12,128,128]{3,2,1,0:T(8,128)(2,1)S(1)}, bf16[16,12,128,128]{3,2,1,0:T(8,128)(2,1)}, u32[]{:S(2)}) %copy-start.1) | copy-done | bytes 6291480
  129.8 1.6 copy-done.3
  131.4 2.0 %shard_map.67 = (f32[4,128,128]{2,1,0:T(8,128)S(1)}, f32[4,128,128]{2,1,0:T(8,128)S(1)}) custom-call(s32[5]{0:T(128)S(1)} %pad.15.bounds, s32[32,68]{1,0:T(8,128)S(1)} %pad.16.left_at, s32[32,68]{1,0:T(8,128)S(1)} %pad.17.right_at, s32[3,520]{1,0:T(4,128)S(1)} %pad_add_fusion.table, s32[3,32]{1,0:T(4,128)S(1)} %get-tuple-element.62.ends, ...), custom_call_target="tpu_custom_call" | custom-call | tf_op jit(solution)/shard_map/pallas_call | solution.py:197
  133.4 5.8 %collective-permute-start.1 = (f32[4,128,128]{2,1,0:T(8,128)S(1)}, f32[4,128,128]{2,1,0:T(8,128)S(1)}, u32[]{:S(2)}, u32[]{:S(2)}) collective-permute-start(f32[4,128,128]{2,1,0:T(8,128)S(1)} %get-tuple-element.43), channel_id=1, source_target_pairs={{0,1},{1,0},{2,3},{3,2},{4,5},{5,4},{6,7},{7,6},{8,9},{9,8},{10,11... | collective-permute-start | bytes 786440 | tf_op jit(solution)/shard_map/ppermute | solution.py:210
  139.1 2.3 %shard_map.68 = (f32[4,128,128]{2,1,0:T(8,128)S(1)}, f32[4,128,128]{2,1,0:T(8,128)S(1)}) custom-call(s32[5]{0:T(128)S(1)} %pad.15.bounds, s32[32,68]{1,0:T(8,128)S(1)} %pad.16.left_at, s32[32,68]{1,0:T(8,128)S(1)} %pad.17.right_at, s32[3,520]{1,0:T(4,128)S(1)} %pad_add_fusion.table, s32[3,32]{1,0:T(4,128)S(1)} %get-tuple-element.62.ends, ...), custom_call_target="tpu_custom_call" | custom-call | tf_op jit(solution)/shard_map/pallas_call | solution.py:197
  141.5 0.4 collective-permute-start.3
  141.9 2.3 %shard_map.69 = (f32[4,128,128]{2,1,0:T(8,128)S(1)}, f32[4,128,128]{2,1,0:T(8,128)S(1)}) custom-call(s32[5]{0:T(128)S(1)} %pad.15.bounds, s32[32,68]{1,0:T(8,128)S(1)} %pad.16.left_at, s32[32,68]{1,0:T(8,128)S(1)} %pad.17.right_at, s32[3,520]{1,0:T(4,128)S(1)} %pad_add_fusion.table, s32[3,32]{1,0:T(4,128)S(1)} %get-tuple-element.62.ends, ...), custom_call_target="tpu_custom_call" | custom-call | tf_op jit(solution)/shard_map/pallas_call | solution.py:197
  144.2 0.6 collective-permute-start.5
  144.8 2.3 %shard_map.66 = (f32[4,128,128]{2,1,0:T(8,128)S(1)}, f32[4,128,128]{2,1,0:T(8,128)S(1)}) custom-call(s32[5]{0:T(128)S(1)} %pad.15.bounds, s32[32,68]{1,0:T(8,128)S(1)} %pad.16.left_at, s32[32,68]{1,0:T(8,128)S(1)} %pad.17.right_at, s32[3,520]{1,0:T(4,128)S(1)} %pad_add_fusion.table, s32[3,32]{1,0:T(4,128)S(1)} %get-tuple-element.62.ends, ...), custom_call_target="tpu_custom_call" | custom-call | tf_op jit(solution)/shard_map/pallas_call | solution.py:197
  147.1 0.4 collective-permute-start
  147.5 0.0 collective-permute-done.1
  147.6 4.7 %collective-permute-start.2 = (f32[4,128,128]{2,1,0:T(8,128)S(1)}, f32[4,128,128]{2,1,0:T(8,128)S(1)}, u32[]{:S(2)}, u32[]{:S(2)}) collective-permute-start(f32[4,128,128]{2,1,0:T(8,128)S(1)} %add.273), channel_id=1, source_target_pairs={{0,4},{1,5},{2,6},{3,7},{4,0},{5,1},{6,2},{7,3},{8,12},{9,13},{10,... | collective-permute-start | bytes 786440 | tf_op jit(solution)/shard_map/ppermute | solution.py:211
  152.3 0.0 collective-permute-done.3
  152.3 6.9 %collective-permute-start.4 = (f32[4,128,128]{2,1,0:T(8,128)S(1)}, f32[4,128,128]{2,1,0:T(8,128)S(1)}, u32[]{:S(2)}, u32[]{:S(2)}) collective-permute-start(f32[4,128,128]{2,1,0:T(8,128)S(1)} %add.275), channel_id=1, source_target_pairs={{0,2},{1,3},{2,4},{3,5},{4,6},{5,7},{6,0},{7,1},{8,10},{9,11},{10,... | collective-permute-start | bytes 786440 | tf_op jit(solution)/shard_map/ppermute | solution.py:211
  159.2 0.0 collective-permute-done.5
  159.3 2.5 %collective-permute-start.6 = (f32[4,128,128]{2,1,0:T(8,128)S(1)}, f32[4,128,128]{2,1,0:T(8,128)S(1)}, u32[]{:S(2)}, u32[]{:S(2)}) collective-permute-start(f32[4,128,128]{2,1,0:T(8,128)S(1)} %add.277), channel_id=1, source_target_pairs={{0,6},{1,7},{2,0},{3,1},{4,2},{5,3},{6,4},{7,5},{8,14},{9,15},{10,... | collective-permute-start | bytes 786440 | tf_op jit(solution)/shard_map/ppermute | solution.py:211
  161.7 0.0 collective-permute-done
  161.7 0.0 collective-permute-done.2
  161.7 5.8 %collective-permute-done.4 = f32[4,128,128]{2,1,0:T(8,128)S(1)} collective-permute-done((f32[4,128,128]{2,1,0:T(8,128)S(1)}, f32[4,128,128]{2,1,0:T(8,128)S(1)}, u32[]{:S(2)}, u32[]{:S(2)}) %collective-permute-start.4) | collective-permute-done | bytes 262176 | tf_op jit(solution)/shard_map/ppermute | solution.py:211
  167.5 3.4 %collective-permute-done.6 = f32[4,128,128]{2,1,0:T(8,128)S(1)} collective-permute-done((f32[4,128,128]{2,1,0:T(8,128)S(1)}, f32[4,128,128]{2,1,0:T(8,128)S(1)}, u32[]{:S(2)}, u32[]{:S(2)}) %collective-permute-start.6) | collective-permute-done | bytes 262176 | tf_op jit(solution)/shard_map/ppermute | solution.py:211
  170.9 0.8 add_add_fusion
  (28 shorter events, 0.2 us)
Async XLA Ops:
  21.5 75.9 %copy-start.4 = (s32[32,1,64]{2,1,0:T(1,128)S(1)}, s32[32,1,64]{2,1,0:T(1,128)}, u32[]{:S(2)}) copy-start(s32[32,1,64]{2,1,0:T(1,128)} %param.10) | copy-start | bytes 24580
  21.5 75.9 %copy-start.5 = (s32[32,1,64]{2,1,0:T(1,128)S(1)}, s32[32,1,64]{2,1,0:T(1,128)}, u32[]{:S(2)}) copy-start(s32[32,1,64]{2,1,0:T(1,128)} %param.9) | copy-start | bytes 24580
  21.5 75.9 %copy-start.6 = (s32[32,1]{0,1:T(1,128)S(1)}, s32[32,1]{0,1:T(1,128)}, u32[]{:S(2)}) copy-start(s32[32,1]{0,1:T(1,128)} %param.11) | copy-start | bytes 388
  97.7 29.3 %all-to-all-start.2 = ((bf16[16,4,128,128]{3,2,1,0:T(8,128)(2,1)}), bf16[16,4,128,128]{3,2,1,0:T(8,128)(2,1)S(1)}, u32[]{:S(2)}, u32[]{:S(2)}) async-start(bf16[16,4,128,128]{3,2,1,0:T(8,128)(2,1)} %get-tuple-element.39), calls=%async_computation.2 | async-start | bytes 4194304 | tf_op jit(solution)/shard_map/all_to_all | solution.py:158
  106.1 2.8 %copy-start = (bf16[16,12,128,128]{3,2,1,0:T(8,128)(2,1)S(1)}, bf16[16,12,128,128]{3,2,1,0:T(8,128)(2,1)}, u32[]{:S(2)}) copy-start(bf16[16,12,128,128]{3,2,1,0:T(8,128)(2,1)} %all_to_all.23.got) | copy-start | bytes 18874372
  117.1 1.3 copy-start.2
  127.0 2.8 %copy-start.1 = (bf16[16,12,128,128]{3,2,1,0:T(8,128)(2,1)S(1)}, bf16[16,12,128,128]{3,2,1,0:T(8,128)(2,1)}, u32[]{:S(2)}) copy-start(bf16[16,12,128,128]{3,2,1,0:T(8,128)(2,1)} %all_to_all.23.got) | copy-start | bytes 18874372
  129.8 1.6 copy-start.3
  133.4 14.1 %collective-permute-start.1 = (f32[4,128,128]{2,1,0:T(8,128)S(1)}, f32[4,128,128]{2,1,0:T(8,128)S(1)}, u32[]{:S(2)}, u32[]{:S(2)}) collective-permute-start(f32[4,128,128]{2,1,0:T(8,128)S(1)} %get-tuple-element.43), channel_id=1, source_target_pairs={{0,1},{1,0},{2,3},{3,2},{4,5},{5,4},{6,7},{7,6},{8,9},{9,8},{10,11... | collective-permute-start | bytes 786440 | tf_op jit(solution)/shard_map/ppermute | solution.py:210
  141.5 10.8 %collective-permute-start.3 = (f32[4,128,128]{2,1,0:T(8,128)S(1)}, f32[4,128,128]{2,1,0:T(8,128)S(1)}, u32[]{:S(2)}, u32[]{:S(2)}) collective-permute-start(f32[4,128,128]{2,1,0:T(8,128)S(1)} %get-tuple-element.45), channel_id=1, source_target_pairs={{0,1},{1,0},{2,3},{3,2},{4,5},{5,4},{6,7},{7,6},{8,9},{9,8},{10,11... | collective-permute-start | bytes 786440 | tf_op jit(solution)/shard_map/ppermute | solution.py:210
  144.2 15.0 %collective-permute-start.5 = (f32[4,128,128]{2,1,0:T(8,128)S(1)}, f32[4,128,128]{2,1,0:T(8,128)S(1)}, u32[]{:S(2)}, u32[]{:S(2)}) collective-permute-start(f32[4,128,128]{2,1,0:T(8,128)S(1)} %get-tuple-element.47), channel_id=1, source_target_pairs={{0,1},{1,0},{2,3},{3,2},{4,5},{5,4},{6,7},{7,6},{8,9},{9,8},{10,11... | collective-permute-start | bytes 786440 | tf_op jit(solution)/shard_map/ppermute | solution.py:210
  147.1 14.6 %collective-permute-start = (f32[4,128,128]{2,1,0:T(8,128)S(1)}, f32[4,128,128]{2,1,0:T(8,128)S(1)}, u32[]{:S(2)}, u32[]{:S(2)}) collective-permute-start(f32[4,128,128]{2,1,0:T(8,128)S(1)} %get-tuple-element.41), channel_id=1, source_target_pairs={{0,1},{1,0},{2,3},{3,2},{4,5},{5,4},{6,7},{7,6},{8,9},{9,8},{10,11... | collective-permute-start | bytes 786440 | tf_op jit(solution)/shard_map/ppermute | solution.py:213
  147.6 14.2 %collective-permute-start.2 = (f32[4,128,128]{2,1,0:T(8,128)S(1)}, f32[4,128,128]{2,1,0:T(8,128)S(1)}, u32[]{:S(2)}, u32[]{:S(2)}) collective-permute-start(f32[4,128,128]{2,1,0:T(8,128)S(1)} %add.273), channel_id=1, source_target_pairs={{0,4},{1,5},{2,6},{3,7},{4,0},{5,1},{6,2},{7,3},{8,12},{9,13},{10,... | collective-permute-start | bytes 786440 | tf_op jit(solution)/shard_map/ppermute | solution.py:211
  152.3 15.2 %collective-permute-start.4 = (f32[4,128,128]{2,1,0:T(8,128)S(1)}, f32[4,128,128]{2,1,0:T(8,128)S(1)}, u32[]{:S(2)}, u32[]{:S(2)}) collective-permute-start(f32[4,128,128]{2,1,0:T(8,128)S(1)} %add.275), channel_id=1, source_target_pairs={{0,2},{1,3},{2,4},{3,5},{4,6},{5,7},{6,0},{7,1},{8,10},{9,11},{10,... | collective-permute-start | bytes 786440 | tf_op jit(solution)/shard_map/ppermute | solution.py:211
  159.3 11.7 %collective-permute-start.6 = (f32[4,128,128]{2,1,0:T(8,128)S(1)}, f32[4,128,128]{2,1,0:T(8,128)S(1)}, u32[]{:S(2)}, u32[]{:S(2)}) collective-permute-start(f32[4,128,128]{2,1,0:T(8,128)S(1)} %add.277), channel_id=1, source_target_pairs={{0,6},{1,7},{2,0},{3,1},{4,2},{5,3},{6,4},{7,5},{8,14},{9,15},{10,... | collective-permute-start | bytes 786440 | tf_op jit(solution)/shard_map/ppermute | solution.py:211
where the time goes:
time: 173 us; the launch traced here: 172 us
  blocking collectives  90.8 us (52%)
  starting transfers between devices  25 us (14%)
  Pallas kernels  23 us (13%)
  waiting for transfers between devices  17.2 us (10%)
  local copies, waits for them, and re-layouts  11.4 us (7%)
  other arithmetic  4.07 us (2%)
    all_to_all x1, blocking collectives, body(): lax.all_to_all(send_first, 'own', split_axis=0, concat_axis=0, tiled=True)  75.9 us
    all_to_all x1, blocking collectives, body(): lax.all_to_all(wanted.reshape(peers, kinds * cap), 'own', split_axis=0, c...  14.9 us
    ppermute x3, starting transfers between devices, body(): lax.ppermute(block, 'red', [(i, (i // 2 + step) % steps * 2 + i % 2) for...  14.1 us
    ppermute x3, waiting for transfers between devices, body(): lax.ppermute(block, 'red', [(i, (i // 2 + step) % steps * 2 + i % 2) for...  9.22 us
    pallas_call x4, Pallas kernels, second(): pl.pallas_call(functools.partial(second_body, step * 2 * share), in_specs...  8.95 us
    unnamed x14, local copies, waits for them, and re-layouts  8.5 us
    pallas_call x1, Pallas kernels, body(): pl.pallas_call(first_body, in_specs=[smem] * 5 + [vmem], out_specs=vmem,...  8.2 us
    all_to_all x1, waiting for transfers between devices, body(): lax.all_to_all(send_second, 'own', split_axis=0, concat_axis=0, tiled=True)  7.95 us
  transfers between devices with their start and end apart: 8, of which 3 were waited for; matrix products, arithmetic and copies ran while one was open for 3% of the time, Pallas kernels for 9%

commit v1 on v0

--- a/solution.py
+++ b/solution.py
@@ -49,7 +49,7 @@
     )
 
 
-def contract(bounds, left_at, right_at, table, ends, left, right, acc, first, part):
+def contract(bounds, left_at, right_at, table, ends, left, right, acc, first):
     places = acc.shape[0]
     begin, finish = bounds[first // places], bounds[first // places + 1]
 
@@ -96,13 +96,13 @@
 def first_body(bounds, left_at, right_at, table, ends, got, out):
     out[...] = jnp.zeros(out.shape, out.dtype)
     flat = flatten(got)
-    contract(bounds, left_at, right_at, table, ends, flat, flat, out, 0, 0)
+    contract(bounds, left_at, right_at, table, ends, flat, flat, out, 0)
 
 
 def second_body(first, bounds, left_at, right_at, table, ends, got, rest, before, other, mine, acc):
     places = acc.shape[0]
     acc[...] = before[pl.ds(first, places)]
-    contract(bounds, left_at, right_at, table, ends, flatten(got), flatten(rest), acc, first, 1)
+    contract(bounds, left_at, right_at, table, ends, flatten(got), flatten(rest), acc, first)
     other[...] = acc[pl.ds(0, places // 2)]
     mine[...] = acc[pl.ds(places // 2, places // 2)]
 
@@ -204,16 +204,23 @@
         )(second_bounds, left_at, right_at, second_table, second_ends, got_first, got_second, before)
 
     swap = [(i, i ^ 1) for i in range(red)]
+
+    def met(step):
+        other, mine = second(step)
+        return mine + lax.ppermute(other, "red", swap)
+
     arrived = []
-    for step in [steps // 2] + [s for s in range(1, steps) if s != steps // 2]:
-        other, mine = second(step)
-        block = mine + lax.ppermute(other, "red", swap)
+    for step in far_first(steps)[:-1]:
+        block = met(step)
         arrived.append(lax.ppermute(block, "red", [(i, ((i // 2 + step) % steps) * 2 + i % 2) for i in range(red)]))
-    other, mine = second(0)
-    total = mine + lax.ppermute(other, "red", swap)
+    total = met(0)
     for block in arrived:
         total = total + block
     return total
+
+
+def far_first(steps):
+    return [steps // 2] + [s for s in range(1, steps) if s != steps // 2] + [0]
 
 
 def solution(mesh):
@@ -225,6 +232,5 @@
         P("own", "red", None),
         P("own", "red"),
     )
-    return jax.shard_map(
-        body, mesh=mesh, in_specs=placed, out_specs=P(("own", "red"), None, None), check_vma=False
-    )
+
+    return jax.shard_map(body, mesh=mesh, in_specs=placed, out_specs=P(("own", "red"), None, None), check_vma=False)

time: 173 us -> 172 us (level)
  starting transfers between devices: 25 us -> 21.2 us
  waiting for transfers between devices: 17.2 us -> 19.8 us
    ppermute x3, starting transfers between devices: 14.1 us -> 3.21 us  [body(): lax.ppermute(block, 'red', [(i, (i // 2 + step) % steps * 2 + i % 2) for...]
    ppermute x4, starting transfers between devices: 7.18 us -> 14.2 us  [met(): return mine + lax.ppermute(other, 'red', swap)]
    ppermute x3, waiting for transfers between devices: 9.22 us -> 12.2 us  [body(): lax.ppermute(block, 'red', [(i, (i // 2 + step) % steps * 2 + i % 2) for...]
where the time goes in v1:
time: 172 us; the launch traced here: 171 us
  blocking collectives  90.8 us (53%)
  Pallas kernels  23.6 us (14%)
  starting transfers between devices  21.2 us (12%)
  waiting for transfers between devices  19.8 us (12%)
  local copies, waits for them, and re-layouts  11.4 us (7%)
  other arithmetic  4.07 us (2%)
    all_to_all x1, blocking collectives, body(): lax.all_to_all(send_first, 'own', split_axis=0, concat_axis=0, tiled=True)  75.9 us
    all_to_all x1, blocking collectives, body(): lax.all_to_all(wanted.reshape(peers, kinds * cap), 'own', split_axis=0, c...  14.9 us
    ppermute x4, starting transfers between devices, met(): return mine + lax.ppermute(other, 'red', swap)  14.2 us
    ppermute x3, waiting for transfers between devices, body(): lax.ppermute(block, 'red', [(i, (i // 2 + step) % steps * 2 + i % 2) for...  12.2 us
    pallas_call x4, Pallas kernels, second(): pl.pallas_call(functools.partial(second_body, step * 2 * share), in_specs...  9.26 us
    pallas_call x1, Pallas kernels, body(): pl.pallas_call(first_body, in_specs=[smem] * 5 + [vmem], out_specs=vmem,...  8.52 us
    unnamed x14, local copies, waits for them, and re-layouts  8.5 us
    all_to_all x1, waiting for transfers between devices, body(): lax.all_to_all(send_second, 'own', split_axis=0, concat_axis=0, tiled=True)  7.62 us
  transfers between devices with their start and end apart: 8, of which 3 were waited for; matrix products, arithmetic and copies ran while one was open for 3% of the time, Pallas kernels for 9%

profile of v1, /device:TPU:1, one launch (start us, length us, event | category | flops | bytes accessed | tf_op | source)
XLA Modules:
  0.0 171.2 jit_solution(6155977381569046195)
XLA Ops:
  0.0 0.8 copy.22
  0.8 14.9 %all_to_all.22 = s32[16,1,16]{2,1,0:T(1,128)} all-to-all(s32[16,1,16]{2,1,0:T(1,128)S(1)} %copy.22), channel_id=1, replica_groups=mesh['own'=16,'red'=8] {'own'}, dimensions={0} | all-to-all | bytes 2048 | tf_op jit(solution)/shard_map/all_to_all | solution.py:149
  15.7 5.9 %shard_map.64 = (bf16[16,12,128,128]{3,2,1,0:T(8,128)(2,1)}, bf16[16,4,128,128]{3,2,1,0:T(8,128)(2,1)}) custom-call(s32[16,16]{1,0:T(8,128)} %bitcast.12, bf16[64,128,128]{2,1,0:T(8,128)(2,1)} %refs_0_.1, bf16[64,128,128]{2,1,0:T(8,128)(2,1)} %refs_1_.1), custom_call_target="tpu_custom_call" | custom-call | tf_op jit(solution)/shard_map/pallas_call | solution.py:32
  21.6 75.9 %all_to_all.23.got = bf16[16,12,128,128]{3,2,1,0:T(8,128)(2,1)} all-to-all(bf16[16,12,128,128]{3,2,1,0:T(8,128)(2,1)} %get-tuple-element.30), channel_id=1, replica_groups=mesh['own'=16,'red'=8] {'own'}, dimensions={0} | all-to-all | bytes 12582912 | tf_op jit(solution)/shard_map/all_to_all | solution.py:154
  97.5 0.1 multiply_add_fusion
  97.5 0.2 convert_reduce_fusion.2
  97.7 3.7 %all-to-all-start.2 = ((bf16[16,4,128,128]{3,2,1,0:T(8,128)(2,1)}), bf16[16,4,128,128]{3,2,1,0:T(8,128)(2,1)S(1)}, u32[]{:S(2)}, u32[]{:S(2)}) async-start(bf16[16,4,128,128]{3,2,1,0:T(8,128)(2,1)} %get-tuple-element.39), calls=%async_computation.2 | async-start | bytes 4194304 | tf_op jit(solution)/shard_map/all_to_all | solution.py:158
  101.5 0.2 select_reduce_fusion.7
  101.7 0.1 select_reduce_fusion.5
  101.8 0.6 slice.11
  102.4 0.1 slice.10
  102.5 0.6 slice.12
  103.0 0.1 select_reduce_fusion
  103.2 0.1 select_reduce_fusion.2
  103.3 0.1 select_reduce_fusion.4
  103.4 0.6 pad.18.bounds
  104.1 0.1 copy.23
  104.2 1.0 sort.14
  105.2 0.1 copy.24
  105.3 0.1 select_select_fusion
  105.4 0.1 pad.15.bounds
  105.4 0.6 compare_select_fusion
  106.1 2.8 %copy-done = bf16[16,12,128,128]{3,2,1,0:T(8,128)(2,1)S(1)} copy-done((bf16[16,12,128,128]{3,2,1,0:T(8,128)(2,1)S(1)}, bf16[16,12,128,128]{3,2,1,0:T(8,128)(2,1)}, u32[]{:S(2)}) %copy-start) | copy-done | bytes 6291480
  108.9 8.5 %shard_map.65.before = f32[32,128,128]{2,1,0:T(8,128)S(1)} custom-call(s32[2]{0:T(128)S(1)} %pad.18.bounds, s32[32,68]{1,0:T(8,128)S(1)} %pad.16.left_at, s32[32,68]{1,0:T(8,128)S(1)} %pad.17.right_at, s32[3,520]{1,0:T(4,128)S(1)} %pad_add_fusion.1.table, s32[3,32]{1,0:T(4,128)S(1)} %get-tuple-element.61.ends, bf16[16,12,128,128]{3,2,1,0:T(8,128)(2,1)S(1)} %copy-done), custom_call_target="tpu_custom_call" | custom-call | tf_op jit(solution)/shard_map/pallas_call | solution.py:187
  117.4 1.3 copy-done.2
  118.8 0.6 compare_select_fusion.1
  119.4 7.6 %all-to-all-done.2.rest = bf16[16,4,128,128]{3,2,1,0:T(8,128)(2,1)S(1)} async-done(((bf16[16,4,128,128]{3,2,1,0:T(8,128)(2,1)}), bf16[16,4,128,128]{3,2,1,0:T(8,128)(2,1)S(1)}, u32[]{:S(2)}, u32[]{:S(2)}) %all-to-all-start.2) | async-done | bytes 2097184 | tf_op jit(solution)/shard_map/all_to_all | solution.py:158
  127.0 2.8 %copy-done.1 = bf16[16,12,128,128]{3,2,1,0:T(8,128)(2,1)S(1)} copy-done((bf16[16,12,128,128]{3,2,1,0:T(8,128)(2,1)S(1)}, bf16[16,12,128,128]{3,2,1,0:T(8,128)(2,1)}, u32[]{:S(2)}) %copy-start.1) | copy-done | bytes 6291480
  129.8 1.6 copy-done.3
  131.4 2.6 %shard_map.67 = (f32[4,128,128]{2,1,0:T(8,128)S(1)}, f32[4,128,128]{2,1,0:T(8,128)S(1)}) custom-call(s32[5]{0:T(128)S(1)} %pad.15.bounds, s32[32,68]{1,0:T(8,128)S(1)} %pad.16.left_at, s32[32,68]{1,0:T(8,128)S(1)} %pad.17.right_at, s32[3,520]{1,0:T(4,128)S(1)} %pad_add_fusion.table, s32[3,32]{1,0:T(4,128)S(1)} %get-tuple-element.62.ends, ...), custom_call_target="tpu_custom_call" | custom-call | tf_op jit(solution)/shard_map/pallas_call | solution.py:197
  134.0 9.8 %collective-permute-start.1 = (f32[4,128,128]{2,1,0:T(8,128)S(1)}, f32[4,128,128]{2,1,0:T(8,128)S(1)}, u32[]{:S(2)}, u32[]{:S(2)}) collective-permute-start(f32[4,128,128]{2,1,0:T(8,128)S(1)} %get-tuple-element.43), channel_id=1, source_target_pairs={{0,1},{1,0},{2,3},{3,2},{4,5},{5,4},{6,7},{7,6},{8,9},{9,8},{10,11... | collective-permute-start | bytes 786440 | tf_op jit(solution)/shard_map/ppermute | solution.py:210
  143.8 2.0 %shard_map.68 = (f32[4,128,128]{2,1,0:T(8,128)S(1)}, f32[4,128,128]{2,1,0:T(8,128)S(1)}) custom-call(s32[5]{0:T(128)S(1)} %pad.15.bounds, s32[32,68]{1,0:T(8,128)S(1)} %pad.16.left_at, s32[32,68]{1,0:T(8,128)S(1)} %pad.17.right_at, s32[3,520]{1,0:T(4,128)S(1)} %pad_add_fusion.table, s32[3,32]{1,0:T(4,128)S(1)} %get-tuple-element.62.ends, ...), custom_call_target="tpu_custom_call" | custom-call | tf_op jit(solution)/shard_map/pallas_call | solution.py:197
  145.8 2.0 %collective-permute-start.3 = (f32[4,128,128]{2,1,0:T(8,128)S(1)}, f32[4,128,128]{2,1,0:T(8,128)S(1)}, u32[]{:S(2)}, u32[]{:S(2)}) collective-permute-start(f32[4,128,128]{2,1,0:T(8,128)S(1)} %get-tuple-element.45), channel_id=1, source_target_pairs={{0,1},{1,0},{2,3},{3,2},{4,5},{5,4},{6,7},{7,6},{8,9},{9,8},{10,11... | collective-permute-start | bytes 786440 | tf_op jit(solution)/shard_map/ppermute | solution.py:210
  147.8 2.3 %shard_map.69 = (f32[4,128,128]{2,1,0:T(8,128)S(1)}, f32[4,128,128]{2,1,0:T(8,128)S(1)}) custom-call(s32[5]{0:T(128)S(1)} %pad.15.bounds, s32[32,68]{1,0:T(8,128)S(1)} %pad.16.left_at, s32[32,68]{1,0:T(8,128)S(1)} %pad.17.right_at, s32[3,520]{1,0:T(4,128)S(1)} %pad_add_fusion.table, s32[3,32]{1,0:T(4,128)S(1)} %get-tuple-element.62.ends, ...), custom_call_target="tpu_custom_call" | custom-call | tf_op jit(solution)/shard_map/pallas_call | solution.py:197
  150.1 1.4 collective-permute-start.5
  151.5 2.3 %shard_map.66 = (f32[4,128,128]{2,1,0:T(8,128)S(1)}, f32[4,128,128]{2,1,0:T(8,128)S(1)}) custom-call(s32[5]{0:T(128)S(1)} %pad.15.bounds, s32[32,68]{1,0:T(8,128)S(1)} %pad.16.left_at, s32[32,68]{1,0:T(8,128)S(1)} %pad.17.right_at, s32[3,520]{1,0:T(4,128)S(1)} %pad_add_fusion.table, s32[3,32]{1,0:T(4,128)S(1)} %get-tuple-element.62.ends, ...), custom_call_target="tpu_custom_call" | custom-call | tf_op jit(solution)/shard_map/pallas_call | solution.py:197
  153.8 1.1 collective-permute-start
  154.9 0.0 collective-permute-done.1
  154.9 0.4 collective-permute-start.2
  155.3 0.0 collective-permute-done.3
  155.4 0.1 collective-permute-start.4
  155.4 0.0 collective-permute-done.5
  155.5 2.7 %collective-permute-start.6 = (f32[4,128,128]{2,1,0:T(8,128)S(1)}, f32[4,128,128]{2,1,0:T(8,128)S(1)}, u32[]{:S(2)}, u32[]{:S(2)}) collective-permute-start(f32[4,128,128]{2,1,0:T(8,128)S(1)} %add.277), channel_id=1, source_target_pairs={{0,6},{1,7},{2,0},{3,1},{4,2},{5,3},{6,4},{7,5},{8,14},{9,15},{10,... | collective-permute-start | bytes 786440 | tf_op jit(solution)/shard_map/ppermute | solution.py:215
  158.2 0.0 collective-permute-done
  158.2 6.2 %collective-permute-done.2 = f32[4,128,128]{2,1,0:T(8,128)S(1)} collective-permute-done((f32[4,128,128]{2,1,0:T(8,128)S(1)}, f32[4,128,128]{2,1,0:T(8,128)S(1)}, u32[]{:S(2)}, u32[]{:S(2)}) %collective-permute-start.2) | collective-permute-done | bytes 262176 | tf_op jit(solution)/shard_map/ppermute | solution.py:215
  164.4 6.0 %collective-permute-done.4 = f32[4,128,128]{2,1,0:T(8,128)S(1)} collective-permute-done((f32[4,128,128]{2,1,0:T(8,128)S(1)}, f32[4,128,128]{2,1,0:T(8,128)S(1)}, u32[]{:S(2)}, u32[]{:S(2)}) %collective-permute-start.4) | collective-permute-done | bytes 262176 | tf_op jit(solution)/shard_map/ppermute | solution.py:215
  170.4 0.0 collective-permute-done.6
  170.4 0.8 add_add_fusion
  (28 shorter events, 0.2 us)
Async XLA Ops:
  21.5 75.9 %copy-start.4 = (s32[32,1,64]{2,1,0:T(1,128)S(1)}, s32[32,1,64]{2,1,0:T(1,128)}, u32[]{:S(2)}) copy-start(s32[32,1,64]{2,1,0:T(1,128)} %param.10) | copy-start | bytes 24580
  21.5 75.9 %copy-start.5 = (s32[32,1,64]{2,1,0:T(1,128)S(1)}, s32[32,1,64]{2,1,0:T(1,128)}, u32[]{:S(2)}) copy-start(s32[32,1,64]{2,1,0:T(1,128)} %param.9) | copy-start | bytes 24580
  21.5 75.9 %copy-start.6 = (s32[32,1]{0,1:T(1,128)S(1)}, s32[32,1]{0,1:T(1,128)}, u32[]{:S(2)}) copy-start(s32[32,1]{0,1:T(1,128)} %param.11) | copy-start | bytes 388
  97.7 29.3 %all-to-all-start.2 = ((bf16[16,4,128,128]{3,2,1,0:T(8,128)(2,1)}), bf16[16,4,128,128]{3,2,1,0:T(8,128)(2,1)S(1)}, u32[]{:S(2)}, u32[]{:S(2)}) async-start(bf16[16,4,128,128]{3,2,1,0:T(8,128)(2,1)} %get-tuple-element.39), calls=%async_computation.2 | async-start | bytes 4194304 | tf_op jit(solution)/shard_map/all_to_all | solution.py:158
  106.1 2.8 %copy-start = (bf16[16,12,128,128]{3,2,1,0:T(8,128)(2,1)S(1)}, bf16[16,12,128,128]{3,2,1,0:T(8,128)(2,1)}, u32[]{:S(2)}) copy-start(bf16[16,12,128,128]{3,2,1,0:T(8,128)(2,1)} %all_to_all.23.got) | copy-start | bytes 18874372
  117.4 1.3 copy-start.2
  127.0 2.8 %copy-start.1 = (bf16[16,12,128,128]{3,2,1,0:T(8,128)(2,1)S(1)}, bf16[16,12,128,128]{3,2,1,0:T(8,128)(2,1)}, u32[]{:S(2)}) copy-start(bf16[16,12,128,128]{3,2,1,0:T(8,128)(2,1)} %all_to_all.23.got) | copy-start | bytes 18874372
  129.8 1.6 copy-start.3
  134.0 20.9 %collective-permute-start.1 = (f32[4,128,128]{2,1,0:T(8,128)S(1)}, f32[4,128,128]{2,1,0:T(8,128)S(1)}, u32[]{:S(2)}, u32[]{:S(2)}) collective-permute-start(f32[4,128,128]{2,1,0:T(8,128)S(1)} %get-tuple-element.43), channel_id=1, source_target_pairs={{0,1},{1,0},{2,3},{3,2},{4,5},{5,4},{6,7},{7,6},{8,9},{9,8},{10,11... | collective-permute-start | bytes 786440 | tf_op jit(solution)/shard_map/ppermute | solution.py:210
  145.8 9.5 %collective-permute-start.3 = (f32[4,128,128]{2,1,0:T(8,128)S(1)}, f32[4,128,128]{2,1,0:T(8,128)S(1)}, u32[]{:S(2)}, u32[]{:S(2)}) collective-permute-start(f32[4,128,128]{2,1,0:T(8,128)S(1)} %get-tuple-element.45), channel_id=1, source_target_pairs={{0,1},{1,0},{2,3},{3,2},{4,5},{5,4},{6,7},{7,6},{8,9},{9,8},{10,11... | collective-permute-start | bytes 786440 | tf_op jit(solution)/shard_map/ppermute | solution.py:210
  150.1 5.3 %collective-permute-start.5 = (f32[4,128,128]{2,1,0:T(8,128)S(1)}, f32[4,128,128]{2,1,0:T(8,128)S(1)}, u32[]{:S(2)}, u32[]{:S(2)}) collective-permute-start(f32[4,128,128]{2,1,0:T(8,128)S(1)} %get-tuple-element.47), channel_id=1, source_target_pairs={{0,1},{1,0},{2,3},{3,2},{4,5},{5,4},{6,7},{7,6},{8,9},{9,8},{10,11... | collective-permute-start | bytes 786440 | tf_op jit(solution)/shard_map/ppermute | solution.py:210
  153.8 4.4 %collective-permute-start = (f32[4,128,128]{2,1,0:T(8,128)S(1)}, f32[4,128,128]{2,1,0:T(8,128)S(1)}, u32[]{:S(2)}, u32[]{:S(2)}) collective-permute-start(f32[4,128,128]{2,1,0:T(8,128)S(1)} %get-tuple-element.41), channel_id=1, source_target_pairs={{0,1},{1,0},{2,3},{3,2},{4,5},{5,4},{6,7},{7,6},{8,9},{9,8},{10,11... | collective-permute-start | bytes 786440 | tf_op jit(solution)/shard_map/ppermute | solution.py:210
  154.9 9.5 %collective-permute-start.2 = (f32[4,128,128]{2,1,0:T(8,128)S(1)}, f32[4,128,128]{2,1,0:T(8,128)S(1)}, u32[]{:S(2)}, u32[]{:S(2)}) collective-permute-start(f32[4,128,128]{2,1,0:T(8,128)S(1)} %add.273), channel_id=1, source_target_pairs={{0,4},{1,5},{2,6},{3,7},{4,0},{5,1},{6,2},{7,3},{8,12},{9,13},{10,... | collective-permute-start | bytes 786440 | tf_op jit(solution)/shard_map/ppermute | solution.py:215
  155.4 15.0 %collective-permute-start.4 = (f32[4,128,128]{2,1,0:T(8,128)S(1)}, f32[4,128,128]{2,1,0:T(8,128)S(1)}, u32[]{:S(2)}, u32[]{:S(2)}) collective-permute-start(f32[4,128,128]{2,1,0:T(8,128)S(1)} %add.275), channel_id=1, source_target_pairs={{0,2},{1,3},{2,4},{3,5},{4,6},{5,7},{6,0},{7,1},{8,10},{9,11},{10,... | collective-permute-start | bytes 786440 | tf_op jit(solution)/shard_map/ppermute | solution.py:215
  155.5 14.9 %collective-permute-start.6 = (f32[4,128,128]{2,1,0:T(8,128)S(1)}, f32[4,128,128]{2,1,0:T(8,128)S(1)}, u32[]{:S(2)}, u32[]{:S(2)}) collective-permute-start(f32[4,128,128]{2,1,0:T(8,128)S(1)} %add.277), channel_id=1, source_target_pairs={{0,6},{1,7},{2,0},{3,1},{4,2},{5,3},{6,4},{7,5},{8,14},{9,15},{10,... | collective-permute-start | bytes 786440 | tf_op jit(solution)/shard_map/ppermute | solution.py:215

commit v2 on v1

--- a/solution.py
+++ b/solution.py
@@ -99,12 +99,16 @@
     contract(bounds, left_at, right_at, table, ends, flat, flat, out, 0)
 
 
-def second_body(first, bounds, left_at, right_at, table, ends, got, rest, before, other, mine, acc):
+def second_body(first, bounds, left_at, right_at, table, ends, got, rest, before, other, mine, acc, old, sem):
     places = acc.shape[0]
-    acc[...] = before[pl.ds(first, places)]
+    copy = pltpu.make_async_copy(before.at[pl.ds(first, places)], old, sem)
+    copy.start()
+    acc[...] = jnp.zeros(acc.shape, acc.dtype)
     contract(bounds, left_at, right_at, table, ends, flatten(got), flatten(rest), acc, first)
-    other[...] = acc[pl.ds(0, places // 2)]
-    mine[...] = acc[pl.ds(places // 2, places // 2)]
+    copy.wait()
+    for half, out in enumerate((other, mine)):
+        span = pl.ds(half * (places // 2), places // 2)
+        out[...] = acc[span] + old[span]
 
 
 def group_table(order, start, stop, slots):
@@ -192,35 +196,39 @@
         compiler_params=params,
     )(first_bounds, left_at, right_at, first_table, first_ends, got_first)
 
+    before = pltpu.with_memory_space_constraint(before, pltpu.HBM)
+
     def second(step):
         half = jax.ShapeDtypeStruct((share,) + tile, jnp.float32)
         return pl.pallas_call(
             functools.partial(second_body, step * 2 * share),
-            in_specs=[smem] * 5 + [vmem] * 3,
+            in_specs=[smem] * 5 + [vmem] * 2 + [pl.BlockSpec(memory_space=pltpu.HBM)],
             out_specs=[vmem, vmem],
             out_shape=[half, half],
-            scratch_shapes=[pltpu.VMEM((2 * share,) + tile, jnp.float32)],
+            scratch_shapes=[pltpu.VMEM((2 * share,) + tile, jnp.float32)] * 2 + [pltpu.SemaphoreType.DMA(())],
             compiler_params=params,
         )(second_bounds, left_at, right_at, second_table, second_ends, got_first, got_second, before)
 
     swap = [(i, i ^ 1) for i in range(red)]
 
-    def met(step):
+    def met(step, spans=(slice(None),), extra=0.0):
         other, mine = second(step)
-        return mine + lax.ppermute(other, "red", swap)
-
-    arrived = []
-    for step in far_first(steps)[:-1]:
-        block = met(step)
-        arrived.append(lax.ppermute(block, "red", [(i, ((i // 2 + step) % steps) * 2 + i % 2) for i in range(red)]))
-    total = met(0)
-    for block in arrived:
-        total = total + block
-    return total
-
-
-def far_first(steps):
-    return [steps // 2] + [s for s in range(1, steps) if s != steps // 2] + [0]
+        theirs = lax.ppermute(other, "red", swap)
+        return [mine[span] + theirs[span] + extra for span in spans]
+
+    def send(value, distance):
+        return lax.ppermute(value, "red", [(i, ((i // 2 + distance) % steps) * 2 + i % 2) for i in range(red)])
+
+    half = share // 2
+    far_low, far_high = met(2, (slice(0, half), slice(half, share)))
+    from_left = send(far_low, 1)
+    from_right = send(far_high, -1)
+    still = ((0, 0), (0, 0))
+    (right,) = met(1, extra=jnp.pad(from_left, ((0, share - half), *still)))
+    from_left = send(right, 1)
+    (left,) = met(3, extra=jnp.pad(from_right, ((half, 0), *still)))
+    from_right = send(left, -1)
+    return met(0)[0] + from_left + from_right
 
 
 def solution(mesh):

time: 172 us -> 171 us (level); the launches traced: 171 us -> 168 us
  waiting for transfers between devices: 19.8 us -> 14.3 us
  starting transfers between devices: 21.2 us -> 24.9 us
    ppermute x7 -> x8, waiting for transfers between devices: 12.2 us -> 6.68 us  [the longest x4 6.67 us: send(): lax.ppermute(value, 'red', [(i, (i // 2 + distance) % steps * 2 + i % 2)...]
    ppermute x7 -> x8, starting transfers between devices: 17.4 us -> 21.1 us  [the longest x4 13.8 us: met(): theirs = lax.ppermute(other, 'red', swap)]
    unnamed x14 -> x12, local copies, waits for them, and re-layouts: 8.5 us -> 6.91 us
  transfers between devices with their start and end apart: 8 -> 9, of which waited for: 3 -> 4; matrix products, arithmetic and copies ran while one was open for 3% -> 3% of each run, Pallas kernels for 9% -> 9%
where the time goes in v2:
time: 171 us; the launch traced here: 168 us
  blocking collectives  90.8 us (53%)
  starting transfers between devices  24.9 us (15%)
  Pallas kernels  24.2 us (14%)
  waiting for transfers between devices  14.3 us (8%)
  local copies, waits for them, and re-layouts  9.82 us (6%)
  other arithmetic  4.07 us (2%)
    all_to_all x1, blocking collectives, body(): lax.all_to_all(send_first, 'own', split_axis=0, concat_axis=0, tiled=True)  75.9 us
    all_to_all x1, blocking collectives, body(): lax.all_to_all(wanted.reshape(peers, kinds * cap), 'own', split_axis=0, c...  14.9 us
    ppermute x4, starting transfers between devices, met(): theirs = lax.ppermute(other, 'red', swap)  13.8 us
    pallas_call x4, Pallas kernels, second(): pl.pallas_call(functools.partial(second_body, step * 2 * share), in_specs...  9.82 us
    pallas_call x1, Pallas kernels, body(): pl.pallas_call(first_body, in_specs=[smem] * 5 + [vmem], out_specs=vmem,...  8.49 us
    all_to_all x1, waiting for transfers between devices, body(): lax.all_to_all(send_second, 'own', split_axis=0, concat_axis=0, tiled=True)  7.66 us
    ppermute x4, starting transfers between devices, send(): lax.ppermute(value, 'red', [(i, (i // 2 + distance) % steps * 2 + i % 2)...  7.3 us
    unnamed x12, local copies, waits for them, and re-layouts  6.91 us
  transfers between devices with their start and end apart: 9, of which 4 were waited for; matrix products, arithmetic and copies ran while one was open for 3% of the time, Pallas kernels for 9%

profile of v2, /device:TPU:1, one launch (start us, length us, event | category | flops | bytes accessed | tf_op | source)
XLA Modules:
  0.0 168.3 jit_solution(7000894709267544512)
XLA Ops:
  0.0 0.8 copy.22
  0.8 14.9 %all_to_all.22 = s32[16,1,16]{2,1,0:T(1,128)} all-to-all(s32[16,1,16]{2,1,0:T(1,128)S(1)} %copy.22), channel_id=1, replica_groups=mesh['own'=16,'red'=8] {'own'}, dimensions={0} | all-to-all | bytes 2048 | tf_op jit(solution)/shard_map/all_to_all | solution.py:153
  15.7 5.9 %shard_map.64 = (bf16[16,12,128,128]{3,2,1,0:T(8,128)(2,1)}, bf16[16,4,128,128]{3,2,1,0:T(8,128)(2,1)}) custom-call(s32[16,16]{1,0:T(8,128)} %bitcast.12, bf16[64,128,128]{2,1,0:T(8,128)(2,1)} %refs_0_.1, bf16[64,128,128]{2,1,0:T(8,128)(2,1)} %refs_1_.1), custom_call_target="tpu_custom_call" | custom-call | tf_op jit(solution)/shard_map/pallas_call | solution.py:32
  21.6 75.9 %all_to_all.23.got = bf16[16,12,128,128]{3,2,1,0:T(8,128)(2,1)} all-to-all(bf16[16,12,128,128]{3,2,1,0:T(8,128)(2,1)} %get-tuple-element.30), channel_id=1, replica_groups=mesh['own'=16,'red'=8] {'own'}, dimensions={0} | all-to-all | bytes 12582912 | tf_op jit(solution)/shard_map/all_to_all | solution.py:158
  97.5 0.1 multiply_add_fusion
  97.5 0.2 convert_reduce_fusion.2
  97.7 3.7 %all-to-all-start.2 = ((bf16[16,4,128,128]{3,2,1,0:T(8,128)(2,1)}), bf16[16,4,128,128]{3,2,1,0:T(8,128)(2,1)S(1)}, u32[]{:S(2)}, u32[]{:S(2)}) async-start(bf16[16,4,128,128]{3,2,1,0:T(8,128)(2,1)} %get-tuple-element.39), calls=%async_computation.2 | async-start | bytes 4194304 | tf_op jit(solution)/shard_map/all_to_all | solution.py:162
  101.5 0.2 select_reduce_fusion.7
  101.7 0.1 select_reduce_fusion.5
  101.8 0.6 slice.23
  102.4 0.1 slice.22
  102.5 0.6 slice.24
  103.0 0.1 select_reduce_fusion
  103.2 0.1 select_reduce_fusion.2
  103.3 0.1 select_reduce_fusion.4
  103.4 0.6 pad.26.bounds
  104.1 0.1 copy.23
  104.2 1.0 sort.14
  105.2 0.1 copy.24
  105.3 0.1 select_select_fusion
  105.4 0.1 pad.23.bounds
  105.4 0.6 compare_select_fusion
  106.1 2.8 %copy-done = bf16[16,12,128,128]{3,2,1,0:T(8,128)(2,1)S(1)} copy-done((bf16[16,12,128,128]{3,2,1,0:T(8,128)(2,1)S(1)}, bf16[16,12,128,128]{3,2,1,0:T(8,128)(2,1)}, u32[]{:S(2)}) %copy-start) | copy-done | bytes 6291480
  108.9 8.5 %shard_map.65.before = f32[32,128,128]{2,1,0:T(8,128)S(1)} custom-call(s32[2]{0:T(128)S(1)} %pad.26.bounds, s32[32,68]{1,0:T(8,128)S(1)} %pad.24.left_at, s32[32,68]{1,0:T(8,128)S(1)} %pad.25.right_at, s32[3,520]{1,0:T(4,128)S(1)} %pad_add_fusion.3.table, s32[3,32]{1,0:T(4,128)S(1)} %get-tuple-element.63.ends, bf16[16,12,128,128]{3,2,1,0:T(8,128)(2,1)S(1)} %copy-done), custom_call_target="tpu_custom_call" | custom-call | tf_op jit(solution)/shard_map/pallas_call | solution.py:191
  117.4 1.3 copy-done.2
  118.7 0.6 compare_select_fusion.1
  119.3 7.7 %all-to-all-done.2.rest = bf16[16,4,128,128]{3,2,1,0:T(8,128)(2,1)S(1)} async-done(((bf16[16,4,128,128]{3,2,1,0:T(8,128)(2,1)}), bf16[16,4,128,128]{3,2,1,0:T(8,128)(2,1)S(1)}, u32[]{:S(2)}, u32[]{:S(2)}) %all-to-all-start.2) | async-done | bytes 2097184 | tf_op jit(solution)/shard_map/all_to_all | solution.py:162
  127.0 2.8 %copy-done.1 = bf16[16,12,128,128]{3,2,1,0:T(8,128)(2,1)S(1)} copy-done((bf16[16,12,128,128]{3,2,1,0:T(8,128)(2,1)S(1)}, bf16[16,12,128,128]{3,2,1,0:T(8,128)(2,1)}, u32[]{:S(2)}) %copy-start.1) | copy-done | bytes 6291480
  129.8 2.7 %shard_map.68 = (f32[4,128,128]{2,1,0:T(8,128)S(1)}, f32[4,128,128]{2,1,0:T(8,128)S(1)}) custom-call(s32[5]{0:T(128)S(1)} %pad.23.bounds, s32[32,68]{1,0:T(8,128)S(1)} %pad.24.left_at, s32[32,68]{1,0:T(8,128)S(1)} %pad.25.right_at, s32[3,520]{1,0:T(4,128)S(1)} %pad_add_fusion.2.table, s32[3,32]{1,0:T(4,128)S(1)} %get-tuple-element.64.ends, ...), custom_call_target="tpu_custom_call" | custom-call | tf_op jit(solution)/shard_map/pallas_call | solution.py:203
  132.5 9.8 %collective-permute-start.2 = (f32[4,128,128]{2,1,0:T(8,128)S(1)}, f32[4,128,128]{2,1,0:T(8,128)S(1)}, u32[]{:S(2)}, u32[]{:S(2)}) collective-permute-start(f32[4,128,128]{2,1,0:T(8,128)S(1)} %get-tuple-element.45), channel_id=1, source_target_pairs={{0,1},{1,0},{2,3},{3,2},{4,5},{5,4},{6,7},{7,6},{8,9},{9,8},{10,11... | collective-permute-start | bytes 786440 | tf_op jit(solution)/shard_map/ppermute | solution.py:216
  142.2 2.4 %shard_map.67 = (f32[4,128,128]{2,1,0:T(8,128)S(1)}, f32[4,128,128]{2,1,0:T(8,128)S(1)}) custom-call(s32[5]{0:T(128)S(1)} %pad.23.bounds, s32[32,68]{1,0:T(8,128)S(1)} %pad.24.left_at, s32[32,68]{1,0:T(8,128)S(1)} %pad.25.right_at, s32[3,520]{1,0:T(4,128)S(1)} %pad_add_fusion.2.table, s32[3,32]{1,0:T(4,128)S(1)} %get-tuple-element.64.ends, ...), custom_call_target="tpu_custom_call" | custom-call | tf_op jit(solution)/shard_map/pallas_call | solution.py:203
  144.6 1.7 collective-permute-start.1
  146.3 0.0 collective-permute-done.2
  146.3 0.1 collective-permute-start.3
  146.4 2.4 %shard_map.69 = (f32[4,128,128]{2,1,0:T(8,128)S(1)}, f32[4,128,128]{2,1,0:T(8,128)S(1)}) custom-call(s32[5]{0:T(128)S(1)} %pad.23.bounds, s32[32,68]{1,0:T(8,128)S(1)} %pad.24.left_at, s32[32,68]{1,0:T(8,128)S(1)} %pad.25.right_at, s32[3,520]{1,0:T(4,128)S(1)} %pad_add_fusion.2.table, s32[3,32]{1,0:T(4,128)S(1)} %get-tuple-element.64.ends, ...), custom_call_target="tpu_custom_call" | custom-call | tf_op jit(solution)/shard_map/pallas_call | solution.py:203
  148.8 1.4 collective-permute-start.5
  150.1 2.4 %shard_map.66 = (f32[4,128,128]{2,1,0:T(8,128)S(1)}, f32[4,128,128]{2,1,0:T(8,128)S(1)}) custom-call(s32[5]{0:T(128)S(1)} %pad.23.bounds, s32[32,68]{1,0:T(8,128)S(1)} %pad.24.left_at, s32[32,68]{1,0:T(8,128)S(1)} %pad.25.right_at, s32[3,520]{1,0:T(4,128)S(1)} %pad_add_fusion.2.table, s32[3,32]{1,0:T(4,128)S(1)} %get-tuple-element.64.ends, ...), custom_call_target="tpu_custom_call" | custom-call | tf_op jit(solution)/shard_map/pallas_call | solution.py:203
  152.5 1.0 collective-permute-start
  153.6 3.7 %collective-permute-start.6 = (f32[2,128,128]{2,1,0:T(8,128)S(1)}, f32[2,128,128]{2,1,0:T(8,128)S(1)}, u32[]{:S(2)}, u32[]{:S(2)}) collective-permute-start(f32[2,128,128]{2,1,0:T(8,128)S(1)} %get-tuple-element.60), channel_id=1, source_target_pairs={{0,6},{1,7},{2,0},{3,1},{4,2},{5,3},{6,4},{7,5},{8,14},{9,15},{10,... | collective-permute-start | bytes 393224 | tf_op jit(solution)/shard_map/ppermute | solution.py:220
  157.2 0.0 collective-permute-done.1
  157.2 0.0 collective-permute-done.3
  157.3 0.1 collective-permute-start.4
  157.4 0.0 collective-permute-done.5
  157.4 2.3 %collective-permute-done.6 = f32[2,128,128]{2,1,0:T(8,128)S(1)} collective-permute-done((f32[2,128,128]{2,1,0:T(8,128)S(1)}, f32[2,128,128]{2,1,0:T(8,128)S(1)}, u32[]{:S(2)}, u32[]{:S(2)}) %collective-permute-start.6) | collective-permute-done | bytes 131104 | tf_op jit(solution)/shard_map/ppermute | solution.py:220
  159.7 3.5 %collective-permute-start.7 = (f32[4,128,128]{2,1,0:T(8,128)S(1)}, f32[4,128,128]{2,1,0:T(8,128)S(1)}, u32[]{:S(2)}, u32[]{:S(2)}) collective-permute-start(f32[4,128,128]{2,1,0:T(8,128)S(1)} %pad_add_fusion), channel_id=1, source_target_pairs={{0,6},{1,7},{2,0},{3,1},{4,2},{5,3},{6,4},{7,5},{8,14},{9,15},{10,... | collective-permute-start | bytes 786440 | tf_op jit(solution)/shard_map/ppermute | solution.py:220
  163.2 2.5 %collective-permute-done.4 = f32[4,128,128]{2,1,0:T(8,128)S(1)} collective-permute-done((f32[4,128,128]{2,1,0:T(8,128)S(1)}, f32[4,128,128]{2,1,0:T(8,128)S(1)}, u32[]{:S(2)}, u32[]{:S(2)}) %collective-permute-start.4) | collective-permute-done | bytes 262176 | tf_op jit(solution)/shard_map/ppermute | solution.py:220
  165.7 1.8 %collective-permute-done.7 = f32[4,128,128]{2,1,0:T(8,128)S(1)} collective-permute-done((f32[4,128,128]{2,1,0:T(8,128)S(1)}, f32[4,128,128]{2,1,0:T(8,128)S(1)}, u32[]{:S(2)}, u32[]{:S(2)}) %collective-permute-start.7) | collective-permute-done | bytes 262176 | tf_op jit(solution)/shard_map/ppermute | solution.py:220
  167.6 0.8 add_add_fusion
  (28 shorter events, 0.3 us)
Async XLA Ops:
  21.5 75.9 %copy-start.3 = (s32[32,1,64]{2,1,0:T(1,128)S(1)}, s32[32,1,64]{2,1,0:T(1,128)}, u32[]{:S(2)}) copy-start(s32[32,1,64]{2,1,0:T(1,128)} %param.10) | copy-start | bytes 24580
  21.5 75.9 %copy-start.4 = (s32[32,1,64]{2,1,0:T(1,128)S(1)}, s32[32,1,64]{2,1,0:T(1,128)}, u32[]{:S(2)}) copy-start(s32[32,1,64]{2,1,0:T(1,128)} %param.9) | copy-start | bytes 24580
  21.5 75.9 %copy-start.5 = (s32[32,1]{0,1:T(1,128)S(1)}, s32[32,1]{0,1:T(1,128)}, u32[]{:S(2)}) copy-start(s32[32,1]{0,1:T(1,128)} %param.11) | copy-start | bytes 388
  97.7 29.3 %all-to-all-start.2 = ((bf16[16,4,128,128]{3,2,1,0:T(8,128)(2,1)}), bf16[16,4,128,128]{3,2,1,0:T(8,128)(2,1)S(1)}, u32[]{:S(2)}, u32[]{:S(2)}) async-start(bf16[16,4,128,128]{3,2,1,0:T(8,128)(2,1)} %get-tuple-element.39), calls=%async_computation.2 | async-start | bytes 4194304 | tf_op jit(solution)/shard_map/all_to_all | solution.py:162
  106.1 2.8 %copy-start = (bf16[16,12,128,128]{3,2,1,0:T(8,128)(2,1)S(1)}, bf16[16,12,128,128]{3,2,1,0:T(8,128)(2,1)}, u32[]{:S(2)}) copy-start(bf16[16,12,128,128]{3,2,1,0:T(8,128)(2,1)} %all_to_all.23.got) | copy-start | bytes 18874372
  117.4 1.3 copy-start.2
  127.0 2.8 %copy-start.1 = (bf16[16,12,128,128]{3,2,1,0:T(8,128)(2,1)S(1)}, bf16[16,12,128,128]{3,2,1,0:T(8,128)(2,1)}, u32[]{:S(2)}) copy-start(bf16[16,12,128,128]{3,2,1,0:T(8,128)(2,1)} %all_to_all.23.got) | copy-start | bytes 18874372
  132.5 13.8 %collective-permute-start.2 = (f32[4,128,128]{2,1,0:T(8,128)S(1)}, f32[4,128,128]{2,1,0:T(8,128)S(1)}, u32[]{:S(2)}, u32[]{:S(2)}) collective-permute-start(f32[4,128,128]{2,1,0:T(8,128)S(1)} %get-tuple-element.45), channel_id=1, source_target_pairs={{0,1},{1,0},{2,3},{3,2},{4,5},{5,4},{6,7},{7,6},{8,9},{9,8},{10,11... | collective-permute-start | bytes 786440 | tf_op jit(solution)/shard_map/ppermute | solution.py:216
  144.6 12.6 %collective-permute-start.1 = (f32[4,128,128]{2,1,0:T(8,128)S(1)}, f32[4,128,128]{2,1,0:T(8,128)S(1)}, u32[]{:S(2)}, u32[]{:S(2)}) collective-permute-start(f32[4,128,128]{2,1,0:T(8,128)S(1)} %get-tuple-element.43), channel_id=1, source_target_pairs={{0,1},{1,0},{2,3},{3,2},{4,5},{5,4},{6,7},{7,6},{8,9},{9,8},{10,11... | collective-permute-start | bytes 786440 | tf_op jit(solution)/shard_map/ppermute | solution.py:216
  146.3 10.9 %collective-permute-start.3 = (f32[2,128,128]{2,1,0:T(8,128)S(1)}, f32[2,128,128]{2,1,0:T(8,128)S(1)}, u32[]{:S(2)}, u32[]{:S(2)}) collective-permute-start(f32[2,128,128]{2,1,0:T(8,128)S(1)} %get-tuple-element.59), channel_id=1, source_target_pairs={{0,2},{1,3},{2,4},{3,5},{4,6},{5,7},{6,0},{7,1},{8,10},{9,11},{10,... | collective-permute-start | bytes 393224 | tf_op jit(solution)/shard_map/ppermute | solution.py:220
  148.8 8.6 %collective-permute-start.5 = (f32[4,128,128]{2,1,0:T(8,128)S(1)}, f32[4,128,128]{2,1,0:T(8,128)S(1)}, u32[]{:S(2)}, u32[]{:S(2)}) collective-permute-start(f32[4,128,128]{2,1,0:T(8,128)S(1)} %get-tuple-element.47), channel_id=1, source_target_pairs={{0,1},{1,0},{2,3},{3,2},{4,5},{5,4},{6,7},{7,6},{8,9},{9,8},{10,11... | collective-permute-start | bytes 786440 | tf_op jit(solution)/shard_map/ppermute | solution.py:216
  152.5 10.7 %collective-permute-start = (f32[4,128,128]{2,1,0:T(8,128)S(1)}, f32[4,128,128]{2,1,0:T(8,128)S(1)}, u32[]{:S(2)}, u32[]{:S(2)}) collective-permute-start(f32[4,128,128]{2,1,0:T(8,128)S(1)} %get-tuple-element.41), channel_id=1, source_target_pairs={{0,1},{1,0},{2,3},{3,2},{4,5},{5,4},{6,7},{7,6},{8,9},{9,8},{10,11... | collective-permute-start | bytes 786440 | tf_op jit(solution)/shard_map/ppermute | solution.py:216
  153.6 6.1 %collective-permute-start.6 = (f32[2,128,128]{2,1,0:T(8,128)S(1)}, f32[2,128,128]{2,1,0:T(8,128)S(1)}, u32[]{:S(2)}, u32[]{:S(2)}) collective-permute-start(f32[2,128,128]{2,1,0:T(8,128)S(1)} %get-tuple-element.60), channel_id=1, source_target_pairs={{0,6},{1,7},{2,0},{3,1},{4,2},{5,3},{6,4},{7,5},{8,14},{9,15},{10,... | collective-permute-start | bytes 393224 | tf_op jit(solution)/shard_map/ppermute | solution.py:220
  157.3 8.4 %collective-permute-start.4 = (f32[4,128,128]{2,1,0:T(8,128)S(1)}, f32[4,128,128]{2,1,0:T(8,128)S(1)}, u32[]{:S(2)}, u32[]{:S(2)}) collective-permute-start(f32[4,128,128]{2,1,0:T(8,128)S(1)} %pad_add_fusion.1), channel_id=1, source_target_pairs={{0,2},{1,3},{2,4},{3,5},{4,6},{5,7},{6,0},{7,1},{8,10},{9,11},{10,... | collective-permute-start | bytes 786440 | tf_op jit(solution)/shard_map/ppermute | solution.py:220
  159.7 7.9 %collective-permute-start.7 = (f32[4,128,128]{2,1,0:T(8,128)S(1)}, f32[4,128,128]{2,1,0:T(8,128)S(1)}, u32[]{:S(2)}, u32[]{:S(2)}) collective-permute-start(f32[4,128,128]{2,1,0:T(8,128)S(1)} %pad_add_fusion), channel_id=1, source_target_pairs={{0,6},{1,7},{2,0},{3,1},{4,2},{5,3},{6,4},{7,5},{8,14},{9,15},{10,... | collective-permute-start | bytes 786440 | tf_op jit(solution)/shard_map/ppermute | solution.py:220

commit v3 on v2

--- a/solution.py
+++ b/solution.py
@@ -93,10 +93,13 @@
     return ref.reshape((ref.shape[0] * ref.shape[1],) + ref.shape[2:])
 
 
-def first_body(bounds, left_at, right_at, table, ends, got, out):
-    out[...] = jnp.zeros(out.shape, out.dtype)
+def first_body(bounds, left_at, right_at, table, ends, got, out, acc, sem):
+    acc[...] = jnp.zeros(acc.shape, acc.dtype)
     flat = flatten(got)
-    contract(bounds, left_at, right_at, table, ends, flat, flat, out, 0)
+    contract(bounds, left_at, right_at, table, ends, flat, flat, acc, 0)
+    copy = pltpu.make_async_copy(acc, out, sem)
+    copy.start()
+    copy.wait()
 
 
 def second_body(first, bounds, left_at, right_at, table, ends, got, rest, before, other, mine, acc, old, sem):
@@ -143,24 +146,13 @@
     peers, kinds, cap = wanted.shape
     rows, slots = tri_amp.shape[0], tri_amp.shape[2]
     tile = amp_tiles.shape[1:]
-    cut = cap // 2
+    cut = cap - 3
     red = lax.axis_size("red")
     share = rows // red
     steps = red // 2
     me = lax.axis_index("red")
 
-    wanted, me = lax.optimization_barrier((wanted, me))
     asked = lax.all_to_all(wanted.reshape(peers, kinds * cap), "own", split_axis=0, concat_axis=0, tiled=True)
-    first_list = tuple((0, s) for s in range(cap)) + tuple((1, s) for s in range(cut))
-    second_list = tuple((1, s) for s in range(cut, cap))
-    asked, me = lax.optimization_barrier((asked, me))
-    send_first, send_second = pack((first_list, second_list), asked, (amp_tiles, int_tiles))
-    got_first = lax.all_to_all(send_first, "own", split_axis=0, concat_axis=0, tiled=True)
-    got_first, send_second, tri_amp, tri_int, tri_count, me = lax.optimization_barrier(
-        (got_first, send_second, tri_amp, tri_int, tri_count, me)
-    )
-    got_second = lax.all_to_all(send_second, "own", split_axis=0, concat_axis=0, tiled=True)
-
     amp_pos, int_pos = tri_amp[:, 0], tri_int[:, 0]
     count = tri_count[:, 0]
     alive = lax.broadcasted_iota(jnp.int32, (rows, slots), 1) < count[:, None]
@@ -185,14 +177,25 @@
     first_bounds = jnp.pad(first_end[rows - 1 :], (1, 0))
     second_bounds = jnp.pad(second_end[2 * share - 1 :: 2 * share], (1, 0))
 
+    tables = (left_at, right_at, first_bounds, first_table, first_ends, second_bounds, second_table, second_ends)
+    asked, tables = lax.optimization_barrier((asked, tables))
+    first_list = tuple((0, s) for s in range(cap)) + tuple((1, s) for s in range(cut))
+    second_list = tuple((1, s) for s in range(cut, cap))
+    send_first, send_second = pack((first_list, second_list), asked, (amp_tiles, int_tiles))
+    got_first = lax.all_to_all(send_first, "own", split_axis=0, concat_axis=0, tiled=True)
+    got_first, send_second, tables = lax.optimization_barrier((got_first, send_second, tables))
+    left_at, right_at, first_bounds, first_table, first_ends, second_bounds, second_table, second_ends = tables
+    got_second = lax.all_to_all(send_second, "own", split_axis=0, concat_axis=0, tiled=True)
+
     smem = pl.BlockSpec(memory_space=pltpu.SMEM)
     vmem = pl.BlockSpec(memory_space=pltpu.VMEM)
     params = pltpu.CompilerParams(vmem_limit_bytes=24 * 2**20)
     before = pl.pallas_call(
         first_body,
         in_specs=[smem] * 5 + [vmem],
-        out_specs=vmem,
-        out_shape=jax.ShapeDtypeStruct((rows,) + tile, jnp.float32),
+        out_specs=pl.BlockSpec(memory_space=pltpu.HBM),
+        out_shape=pltpu.HBM((rows,) + tile, jnp.float32),
+        scratch_shapes=[pltpu.VMEM((rows,) + tile, jnp.float32), pltpu.SemaphoreType.DMA(())],
         compiler_params=params,
     )(first_bounds, left_at, right_at, first_table, first_ends, got_first)
 

time: 171 us -> 178 us (1.041)
  the two profiles are of different devices: /device:TPU:1 before, /device:TPU:8 now
where the time goes in v3:
time: 178 us; the launch traced here: 177 us
  blocking collectives  83.5 us (47%)
  starting transfers between devices  32.1 us (18%)
  Pallas kernels  26.3 us (15%)
  waiting for transfers between devices  18.7 us (11%)
  local copies, waits for them, and re-layouts  10.1 us (6%)
  other arithmetic  6.24 us (4%)
    all_to_all x1, blocking collectives, body(): lax.all_to_all(send_first, 'own', split_axis=0, concat_axis=0, tiled=True)  83.5 us
    ppermute x4, waiting for transfers between devices, send(): lax.ppermute(value, 'red', [(i, (i // 2 + distance) % steps * 2 + i % 2)...  12 us
    pallas_call x1, Pallas kernels, body(): pl.pallas_call(first_body, in_specs=[smem] * 5 + [vmem], out_specs=pl.Blo...  10.9 us
    pallas_call x4, Pallas kernels, second(): pl.pallas_call(functools.partial(second_body, step * 2 * share), in_specs...  9.52 us
    ppermute x4, starting transfers between devices, met(): theirs = lax.ppermute(other, 'red', swap)  9.34 us
    ppermute x4, starting transfers between devices, send(): lax.ppermute(value, 'red', [(i, (i // 2 + distance) % steps * 2 + i % 2)...  8.53 us
    all_to_all x1, starting transfers between devices, body(): lax.all_to_all(wanted.reshape(peers, kinds * cap), 'own', split_axis=0, c...  8.41 us
    all_to_all x1, waiting for transfers between devices, body(): lax.all_to_all(send_second, 'own', split_axis=0, concat_axis=0, tiled=True)  6.72 us
  transfers between devices with their start and end apart: 10, of which 4 were waited for; matrix products, arithmetic and copies ran while one was open for 4% of the time, Pallas kernels for 10%

profile of v3, /device:TPU:8, one launch (start us, length us, event | category | flops | bytes accessed | tf_op | source)
XLA Modules:
  0.0 177.1 jit_solution(545691816054855152)
XLA Ops:
  0.0 1.4 copy.22
  1.4 8.4 %all-to-all-start = ((s32[16,1,16]{2,1,0:T(1,128)}), s32[16,1,16]{2,1,0:T(1,128)S(1)}, u32[]{:S(2)}, u32[]{:S(2)}) async-start(s32[16,1,16]{2,1,0:T(1,128)} %copy.22), calls=%async_computation | async-start | bytes 16384 | tf_op jit(solution)/shard_map/all_to_all | solution.py:155
  9.8 0.9 convert_reduce_fusion.2
  10.7 0.8 select_reduce_fusion.6
  11.6 0.1 select_reduce_fusion.5
  11.7 0.6 slice.24
  12.3 0.1 select_reduce_fusion
  12.4 0.6 slice.22
  13.0 0.1 select_reduce_fusion.3
  13.1 0.1 select_reduce_fusion.2
  13.3 0.8 multiply_add_fusion
  14.1 0.1 copy.23
  14.2 1.0 sort.14
  15.2 0.1 copy.24
  15.3 0.1 select_select_fusion
  15.4 0.6 compare_select_fusion.1
  16.0 0.6 compare_select_fusion
  16.6 0.7 pad.25.bounds
  17.3 0.1 slice.23
  17.4 0.1 pad.26.bounds
  17.5 0.0 all-to-all-done
  17.5 0.0 copy-start.2
  17.6 0.6 copy-done.2
  18.1 5.9 %shard_map.64 = (bf16[16,13,128,128]{3,2,1,0:T(8,128)(2,1)}, bf16[16,3,128,128]{3,2,1,0:T(8,128)(2,1)}) custom-call(s32[16,16]{1,0:T(8,128)} %bitcast.13, bf16[64,128,128]{2,1,0:T(8,128)(2,1)} %refs_0_.1, bf16[64,128,128]{2,1,0:T(8,128)(2,1)} %refs_1_.1), custom_call_target="tpu_custom_call" | custom-call | tf_op jit(solution)/shard_map/pallas_call | solution.py:32
  24.1 83.5 %all_to_all.22.got = bf16[16,13,128,128]{3,2,1,0:T(8,128)(2,1)} all-to-all(bf16[16,13,128,128]{3,2,1,0:T(8,128)(2,1)} %get-tuple-element.38), channel_id=1, replica_groups=mesh['own'=16,'red'=8] {'own'}, dimensions={0} | all-to-all | bytes 13631488 | tf_op jit(solution)/shard_map/all_to_all | solution.py:185
  107.5 5.8 %all-to-all-start.2 = ((bf16[16,3,128,128]{3,2,1,0:T(8,128)(2,1)}), bf16[16,3,128,128]{3,2,1,0:T(8,128)(2,1)S(1)}, u32[]{:S(2)}, u32[]{:S(2)}) async-start(bf16[16,3,128,128]{3,2,1,0:T(8,128)(2,1)} %get-tuple-element.54), calls=%async_computation.2 | async-start | bytes 3145728 | tf_op jit(solution)/shard_map/all_to_all | solution.py:188
  113.4 2.9 %copy-done = bf16[16,13,128,128]{3,2,1,0:T(8,128)(2,1)S(1)} copy-done((bf16[16,13,128,128]{3,2,1,0:T(8,128)(2,1)S(1)}, bf16[16,13,128,128]{3,2,1,0:T(8,128)(2,1)}, u32[]{:S(2)}) %copy-start) | copy-done | bytes 6815768
  116.3 10.9 %shard_map.65.before = f32[32,128,128]{2,1,0:T(8,128)} custom-call(s32[2]{0:T(128)S(1)} %pad.25.bounds, s32[32,68]{1,0:T(8,128)S(1)} %pad.23.left_at, s32[32,68]{1,0:T(8,128)S(1)} %pad.24.right_at, s32[3,520]{1,0:T(4,128)S(1)} %pad_add_fusion.2.table, s32[3,32]{1,0:T(4,128)S(1)} %get-tuple-element.57.ends, bf16[16,13,128,128]{3,2,1,0:T(8,128)(2,1)S(1)} %copy-done), custom_call_target="tpu_custom_call" | custom-call | tf_op jit(solution)/shard_map/pallas_call | solution.py:193
  127.2 6.7 %all-to-all-done.2.rest = bf16[16,3,128,128]{3,2,1,0:T(8,128)(2,1)S(1)} async-done(((bf16[16,3,128,128]{3,2,1,0:T(8,128)(2,1)}), bf16[16,3,128,128]{3,2,1,0:T(8,128)(2,1)S(1)}, u32[]{:S(2)}, u32[]{:S(2)}) %all-to-all-start.2) | async-done | bytes 1572896 | tf_op jit(solution)/shard_map/all_to_all | solution.py:188
  133.9 2.9 %copy-done.1 = bf16[16,13,128,128]{3,2,1,0:T(8,128)(2,1)S(1)} copy-done((bf16[16,13,128,128]{3,2,1,0:T(8,128)(2,1)S(1)}, bf16[16,13,128,128]{3,2,1,0:T(8,128)(2,1)}, u32[]{:S(2)}) %copy-start.1) | copy-done | bytes 6815768
  136.8 2.4 %shard_map.68 = (f32[4,128,128]{2,1,0:T(8,128)S(1)}, f32[4,128,128]{2,1,0:T(8,128)S(1)}) custom-call(s32[5]{0:T(128)S(1)} %pad.26.bounds, s32[32,68]{1,0:T(8,128)S(1)} %pad.23.left_at, s32[32,68]{1,0:T(8,128)S(1)} %pad.24.right_at, s32[3,520]{1,0:T(4,128)S(1)} %pad_add_fusion.3.table, s32[3,32]{1,0:T(4,128)S(1)} %get-tuple-element.52.ends, ...), custom_call_target="tpu_custom_call" | custom-call | tf_op jit(solution)/shard_map/pallas_call | solution.py:206
  139.2 6.5 %collective-permute-start.2 = (f32[4,128,128]{2,1,0:T(8,128)S(1)}, f32[4,128,128]{2,1,0:T(8,128)S(1)}, u32[]{:S(2)}, u32[]{:S(2)}) collective-permute-start(f32[4,128,128]{2,1,0:T(8,128)S(1)} %get-tuple-element.63), channel_id=1, source_target_pairs={{0,1},{1,0},{2,3},{3,2},{4,5},{5,4},{6,7},{7,6},{8,9},{9,8},{10,11... | collective-permute-start | bytes 786440 | tf_op jit(solution)/shard_map/ppermute | solution.py:219
  145.7 2.4 %shard_map.69 = (f32[4,128,128]{2,1,0:T(8,128)S(1)}, f32[4,128,128]{2,1,0:T(8,128)S(1)}) custom-call(s32[5]{0:T(128)S(1)} %pad.26.bounds, s32[32,68]{1,0:T(8,128)S(1)} %pad.23.left_at, s32[32,68]{1,0:T(8,128)S(1)} %pad.24.right_at, s32[3,520]{1,0:T(4,128)S(1)} %pad_add_fusion.3.table, s32[3,32]{1,0:T(4,128)S(1)} %get-tuple-element.52.ends, ...), custom_call_target="tpu_custom_call" | custom-call | tf_op jit(solution)/shard_map/pallas_call | solution.py:206
  148.1 1.0 collective-permute-start.5
  149.2 0.0 collective-permute-done.2
  149.2 5.2 %collective-permute-start.6 = (f32[2,128,128]{2,1,0:T(8,128)S(1)}, f32[2,128,128]{2,1,0:T(8,128)S(1)}, u32[]{:S(2)}, u32[]{:S(2)}) collective-permute-start(f32[2,128,128]{2,1,0:T(8,128)S(1)} %get-tuple-element.78), channel_id=1, source_target_pairs={{0,6},{1,7},{2,0},{3,1},{4,2},{5,3},{6,4},{7,5},{8,14},{9,15},{10,... | collective-permute-start | bytes 393224 | tf_op jit(solution)/shard_map/ppermute | solution.py:223
  154.4 2.4 %shard_map.67 = (f32[4,128,128]{2,1,0:T(8,128)S(1)}, f32[4,128,128]{2,1,0:T(8,128)S(1)}) custom-call(s32[5]{0:T(128)S(1)} %pad.26.bounds, s32[32,68]{1,0:T(8,128)S(1)} %pad.23.left_at, s32[32,68]{1,0:T(8,128)S(1)} %pad.24.right_at, s32[3,520]{1,0:T(4,128)S(1)} %pad_add_fusion.3.table, s32[3,32]{1,0:T(4,128)S(1)} %get-tuple-element.52.ends, ...), custom_call_target="tpu_custom_call" | custom-call | tf_op jit(solution)/shard_map/pallas_call | solution.py:206
  156.8 0.8 collective-permute-start.1
  157.5 2.4 %shard_map.66 = (f32[4,128,128]{2,1,0:T(8,128)S(1)}, f32[4,128,128]{2,1,0:T(8,128)S(1)}) custom-call(s32[5]{0:T(128)S(1)} %pad.26.bounds, s32[32,68]{1,0:T(8,128)S(1)} %pad.23.left_at, s32[32,68]{1,0:T(8,128)S(1)} %pad.24.right_at, s32[3,520]{1,0:T(4,128)S(1)} %pad_add_fusion.3.table, s32[3,32]{1,0:T(4,128)S(1)} %get-tuple-element.52.ends, ...), custom_call_target="tpu_custom_call" | custom-call | tf_op jit(solution)/shard_map/pallas_call | solution.py:206
  159.9 1.0 collective-permute-start
  160.9 0.0 collective-permute-start.3
  161.0 3.3 %collective-permute-start.7 = (f32[4,128,128]{2,1,0:T(8,128)S(1)}, f32[4,128,128]{2,1,0:T(8,128)S(1)}, u32[]{:S(2)}, u32[]{:S(2)}) collective-permute-start(f32[4,128,128]{2,1,0:T(8,128)S(1)} %pad_add_fusion), channel_id=1, source_target_pairs={{0,6},{1,7},{2,0},{3,1},{4,2},{5,3},{6,4},{7,5},{8,14},{9,15},{10,... | collective-permute-start | bytes 786440 | tf_op jit(solution)/shard_map/ppermute | solution.py:223
  164.3 0.0 collective-permute-done.1
  164.3 3.3 %collective-permute-done.3 = f32[2,128,128]{2,1,0:T(8,128)S(1)} collective-permute-done((f32[2,128,128]{2,1,0:T(8,128)S(1)}, f32[2,128,128]{2,1,0:T(8,128)S(1)}, u32[]{:S(2)}, u32[]{:S(2)}) %collective-permute-start.3) | collective-permute-done | bytes 131104 | tf_op jit(solution)/shard_map/ppermute | solution.py:223
  167.7 0.1 collective-permute-start.4
  167.7 2.1 %collective-permute-done.7 = f32[4,128,128]{2,1,0:T(8,128)S(1)} collective-permute-done((f32[4,128,128]{2,1,0:T(8,128)S(1)}, f32[4,128,128]{2,1,0:T(8,128)S(1)}, u32[]{:S(2)}, u32[]{:S(2)}) %collective-permute-start.7) | collective-permute-done | bytes 262176 | tf_op jit(solution)/shard_map/ppermute | solution.py:223
  169.8 6.6 %collective-permute-done.4 = f32[4,128,128]{2,1,0:T(8,128)S(1)} collective-permute-done((f32[4,128,128]{2,1,0:T(8,128)S(1)}, f32[4,128,128]{2,1,0:T(8,128)S(1)}, u32[]{:S(2)}, u32[]{:S(2)}) %collective-permute-start.4) | collective-permute-done | bytes 262176 | tf_op jit(solution)/shard_map/ppermute | solution.py:223
  176.4 0.8 add_add_fusion
  (23 shorter events, 0.2 us)
Async XLA Ops:
  1.4 16.2 %all-to-all-start = ((s32[16,1,16]{2,1,0:T(1,128)}), s32[16,1,16]{2,1,0:T(1,128)S(1)}, u32[]{:S(2)}, u32[]{:S(2)}) async-start(s32[16,1,16]{2,1,0:T(1,128)} %copy.22), calls=%async_computation | async-start | bytes 16384 | tf_op jit(solution)/shard_map/all_to_all | solution.py:155
  17.5 0.6 copy-start.2
  107.5 26.3 %all-to-all-start.2 = ((bf16[16,3,128,128]{3,2,1,0:T(8,128)(2,1)}), bf16[16,3,128,128]{3,2,1,0:T(8,128)(2,1)S(1)}, u32[]{:S(2)}, u32[]{:S(2)}) async-start(bf16[16,3,128,128]{3,2,1,0:T(8,128)(2,1)} %get-tuple-element.54), calls=%async_computation.2 | async-start | bytes 3145728 | tf_op jit(solution)/shard_map/all_to_all | solution.py:188
  113.4 2.9 %copy-start = (bf16[16,13,128,128]{3,2,1,0:T(8,128)(2,1)S(1)}, bf16[16,13,128,128]{3,2,1,0:T(8,128)(2,1)}, u32[]{:S(2)}) copy-start(bf16[16,13,128,128]{3,2,1,0:T(8,128)(2,1)} %all_to_all.22.got) | copy-start | bytes 20447236
  133.9 2.9 %copy-start.1 = (bf16[16,13,128,128]{3,2,1,0:T(8,128)(2,1)S(1)}, bf16[16,13,128,128]{3,2,1,0:T(8,128)(2,1)}, u32[]{:S(2)}) copy-start(bf16[16,13,128,128]{3,2,1,0:T(8,128)(2,1)} %all_to_all.22.got) | copy-start | bytes 20447236
  139.2 10.0 %collective-permute-start.2 = (f32[4,128,128]{2,1,0:T(8,128)S(1)}, f32[4,128,128]{2,1,0:T(8,128)S(1)}, u32[]{:S(2)}, u32[]{:S(2)}) collective-permute-start(f32[4,128,128]{2,1,0:T(8,128)S(1)} %get-tuple-element.63), channel_id=1, source_target_pairs={{0,1},{1,0},{2,3},{3,2},{4,5},{5,4},{6,7},{7,6},{8,9},{9,8},{10,11... | collective-permute-start | bytes 786440 | tf_op jit(solution)/shard_map/ppermute | solution.py:219
  148.1 12.8 %collective-permute-start.5 = (f32[4,128,128]{2,1,0:T(8,128)S(1)}, f32[4,128,128]{2,1,0:T(8,128)S(1)}, u32[]{:S(2)}, u32[]{:S(2)}) collective-permute-start(f32[4,128,128]{2,1,0:T(8,128)S(1)} %get-tuple-element.65), channel_id=1, source_target_pairs={{0,1},{1,0},{2,3},{3,2},{4,5},{5,4},{6,7},{7,6},{8,9},{9,8},{10,11... | collective-permute-start | bytes 786440 | tf_op jit(solution)/shard_map/ppermute | solution.py:219
  149.2 11.7 %collective-permute-start.6 = (f32[2,128,128]{2,1,0:T(8,128)S(1)}, f32[2,128,128]{2,1,0:T(8,128)S(1)}, u32[]{:S(2)}, u32[]{:S(2)}) collective-permute-start(f32[2,128,128]{2,1,0:T(8,128)S(1)} %get-tuple-element.78), channel_id=1, source_target_pairs={{0,6},{1,7},{2,0},{3,1},{4,2},{5,3},{6,4},{7,5},{8,14},{9,15},{10,... | collective-permute-start | bytes 393224 | tf_op jit(solution)/shard_map/ppermute | solution.py:223
  156.8 7.5 %collective-permute-start.1 = (f32[4,128,128]{2,1,0:T(8,128)S(1)}, f32[4,128,128]{2,1,0:T(8,128)S(1)}, u32[]{:S(2)}, u32[]{:S(2)}) collective-permute-start(f32[4,128,128]{2,1,0:T(8,128)S(1)} %get-tuple-element.61), channel_id=1, source_target_pairs={{0,1},{1,0},{2,3},{3,2},{4,5},{5,4},{6,7},{7,6},{8,9},{9,8},{10,11... | collective-permute-start | bytes 786440 | tf_op jit(solution)/shard_map/ppermute | solution.py:219
  159.9 7.8 %collective-permute-start = (f32[4,128,128]{2,1,0:T(8,128)S(1)}, f32[4,128,128]{2,1,0:T(8,128)S(1)}, u32[]{:S(2)}, u32[]{:S(2)}) collective-permute-start(f32[4,128,128]{2,1,0:T(8,128)S(1)} %get-tuple-element.59), channel_id=1, source_target_pairs={{0,1},{1,0},{2,3},{3,2},{4,5},{5,4},{6,7},{7,6},{8,9},{9,8},{10,11... | collective-permute-start | bytes 786440 | tf_op jit(solution)/shard_map/ppermute | solution.py:219
  160.9 6.7 %collective-permute-start.3 = (f32[2,128,128]{2,1,0:T(8,128)S(1)}, f32[2,128,128]{2,1,0:T(8,128)S(1)}, u32[]{:S(2)}, u32[]{:S(2)}) collective-permute-start(f32[2,128,128]{2,1,0:T(8,128)S(1)} %get-tuple-element.77), channel_id=1, source_target_pairs={{0,2},{1,3},{2,4},{3,5},{4,6},{5,7},{6,0},{7,1},{8,10},{9,11},{10,... | collective-permute-start | bytes 393224 | tf_op jit(solution)/shard_map/ppermute | solution.py:223
  161.0 8.8 %collective-permute-start.7 = (f32[4,128,128]{2,1,0:T(8,128)S(1)}, f32[4,128,128]{2,1,0:T(8,128)S(1)}, u32[]{:S(2)}, u32[]{:S(2)}) collective-permute-start(f32[4,128,128]{2,1,0:T(8,128)S(1)} %pad_add_fusion), channel_id=1, source_target_pairs={{0,6},{1,7},{2,0},{3,1},{4,2},{5,3},{6,4},{7,5},{8,14},{9,15},{10,... | collective-permute-start | bytes 786440 | tf_op jit(solution)/shard_map/ppermute | solution.py:223
  167.7 8.7 %collective-permute-start.4 = (f32[4,128,128]{2,1,0:T(8,128)S(1)}, f32[4,128,128]{2,1,0:T(8,128)S(1)}, u32[]{:S(2)}, u32[]{:S(2)}) collective-permute-start(f32[4,128,128]{2,1,0:T(8,128)S(1)} %pad_add_fusion.1), channel_id=1, source_target_pairs={{0,2},{1,3},{2,4},{3,5},{4,6},{5,7},{6,0},{7,1},{8,10},{9,11},{10,... | collective-permute-start | bytes 786440 | tf_op jit(solution)/shard_map/ppermute | solution.py:223

commit v4 on v2

--- a/solution.py
+++ b/solution.py
@@ -7,7 +7,7 @@
 from jax.experimental.pallas import tpu as pltpu
 from jax.sharding import PartitionSpec as P
 
-GROUP = 4
+GROUP = 8
 UNROLL = 4
 PACK_STEPS = 4
 
@@ -93,10 +93,13 @@
     return ref.reshape((ref.shape[0] * ref.shape[1],) + ref.shape[2:])
 
 
-def first_body(bounds, left_at, right_at, table, ends, got, out):
-    out[...] = jnp.zeros(out.shape, out.dtype)
+def first_body(bounds, left_at, right_at, table, ends, got, out, acc, sem):
+    acc[...] = jnp.zeros(acc.shape, acc.dtype)
     flat = flatten(got)
-    contract(bounds, left_at, right_at, table, ends, flat, flat, out, 0)
+    contract(bounds, left_at, right_at, table, ends, flat, flat, acc, 0)
+    copy = pltpu.make_async_copy(acc, out, sem)
+    copy.start()
+    copy.wait()
 
 
 def second_body(first, bounds, left_at, right_at, table, ends, got, rest, before, other, mine, acc, old, sem):
@@ -191,8 +194,9 @@
     before = pl.pallas_call(
         first_body,
         in_specs=[smem] * 5 + [vmem],
-        out_specs=vmem,
-        out_shape=jax.ShapeDtypeStruct((rows,) + tile, jnp.float32),
+        out_specs=pl.BlockSpec(memory_space=pltpu.HBM),
+        out_shape=pltpu.HBM((rows,) + tile, jnp.float32),
+        scratch_shapes=[pltpu.VMEM((rows,) + tile, jnp.float32), pltpu.SemaphoreType.DMA(())],
         compiler_params=params,
     )(first_bounds, left_at, right_at, first_table, first_ends, got_first)
 

time: 171 us -> 165 us (0.965)
  starting transfers between devices: 24.9 us -> 19.5 us
    ppermute x4, starting transfers between devices: 13.8 us -> 10.1 us  [met(): theirs = lax.ppermute(other, 'red', swap)]
    unnamed x12 -> x10, local copies, waits for them, and re-layouts: 6.91 us -> 5.57 us
  transfers between devices with their start and end apart: 9 -> 9, of which waited for: 4 -> 4; matrix products, arithmetic and copies ran while one was open for 3% -> 3% of each run, Pallas kernels for 9% -> 10%
where the time goes in v4:
time: 165 us; the launch traced here: 163 us
  blocking collectives  90.8 us (55%)
  Pallas kernels  24.9 us (15%)
  starting transfers between devices  19.5 us (12%)
  waiting for transfers between devices  15.3 us (9%)
  local copies, waits for them, and re-layouts  8.48 us (5%)
  other arithmetic  4.05 us (2%)
    all_to_all x1, blocking collectives, body(): lax.all_to_all(send_first, 'own', split_axis=0, concat_axis=0, tiled=True)  75.9 us
    all_to_all x1, blocking collectives, body(): lax.all_to_all(wanted.reshape(peers, kinds * cap), 'own', split_axis=0, c...  14.9 us
    ppermute x4, starting transfers between devices, met(): theirs = lax.ppermute(other, 'red', swap)  10.1 us
    pallas_call x4, Pallas kernels, second(): pl.pallas_call(functools.partial(second_body, step * 2 * share), in_specs...  9.68 us
    pallas_call x1, Pallas kernels, body(): pl.pallas_call(first_body, in_specs=[smem] * 5 + [vmem], out_specs=pl.Blo...  9.34 us
    all_to_all x1, waiting for transfers between devices, body(): lax.all_to_all(send_second, 'own', split_axis=0, concat_axis=0, tiled=True)  8.19 us
    ppermute x4, waiting for transfers between devices, send(): lax.ppermute(value, 'red', [(i, (i // 2 + distance) % steps * 2 + i % 2)...  7.06 us
    pallas_call x1, Pallas kernels, pack(): pl.pallas_call(functools.partial(pack_body, lists), grid=(PACK_STEPS,), i...  5.85 us
  transfers between devices with their start and end apart: 9, of which 4 were waited for; matrix products, arithmetic and copies ran while one was open for 3% of the time, Pallas kernels for 10%

profile of v4, /device:TPU:1, one launch (start us, length us, event | category | flops | bytes accessed | tf_op | source)
XLA Modules:
  0.0 163.2 jit_solution(14345707222933880758)
XLA Ops:
  0.0 0.8 copy.22
  0.8 14.9 %all_to_all.22 = s32[16,1,16]{2,1,0:T(1,128)} all-to-all(s32[16,1,16]{2,1,0:T(1,128)S(1)} %copy.22), channel_id=1, replica_groups=mesh['own'=16,'red'=8] {'own'}, dimensions={0} | all-to-all | bytes 2048 | tf_op jit(solution)/shard_map/all_to_all | solution.py:156
  15.7 5.9 %shard_map.64 = (bf16[16,12,128,128]{3,2,1,0:T(8,128)(2,1)}, bf16[16,4,128,128]{3,2,1,0:T(8,128)(2,1)}) custom-call(s32[16,16]{1,0:T(8,128)} %bitcast.12, bf16[64,128,128]{2,1,0:T(8,128)(2,1)} %refs_0_.1, bf16[64,128,128]{2,1,0:T(8,128)(2,1)} %refs_1_.1), custom_call_target="tpu_custom_call" | custom-call | tf_op jit(solution)/shard_map/pallas_call | solution.py:32
  21.6 75.9 %all_to_all.23.got = bf16[16,12,128,128]{3,2,1,0:T(8,128)(2,1)} all-to-all(bf16[16,12,128,128]{3,2,1,0:T(8,128)(2,1)} %get-tuple-element.30), channel_id=1, replica_groups=mesh['own'=16,'red'=8] {'own'}, dimensions={0} | all-to-all | bytes 12582912 | tf_op jit(solution)/shard_map/all_to_all | solution.py:161
  97.5 0.1 multiply_add_fusion
  97.5 0.2 convert_reduce_fusion.2
  97.7 3.7 %all-to-all-start.2 = ((bf16[16,4,128,128]{3,2,1,0:T(8,128)(2,1)}), bf16[16,4,128,128]{3,2,1,0:T(8,128)(2,1)S(1)}, u32[]{:S(2)}, u32[]{:S(2)}) async-start(bf16[16,4,128,128]{3,2,1,0:T(8,128)(2,1)} %get-tuple-element.39), calls=%async_computation.2 | async-start | bytes 4194304 | tf_op jit(solution)/shard_map/all_to_all | solution.py:165
  101.5 0.2 select_reduce_fusion.7
  101.7 0.1 select_reduce_fusion.5
  101.8 0.6 slice.23
  102.4 0.1 slice.22
  102.5 0.6 slice.24
  103.0 0.1 select_reduce_fusion
  103.2 0.1 select_reduce_fusion.2
  103.3 0.1 select_reduce_fusion.4
  103.4 0.6 pad.26.bounds
  104.0 0.1 copy.23
  104.1 1.0 sort.14
  105.2 0.1 copy.24
  105.2 0.1 select_select_fusion
  105.3 0.1 pad.23.bounds
  105.4 0.6 compare_select_fusion
  106.1 2.8 %copy-done = bf16[16,12,128,128]{3,2,1,0:T(8,128)(2,1)S(1)} copy-done((bf16[16,12,128,128]{3,2,1,0:T(8,128)(2,1)S(1)}, bf16[16,12,128,128]{3,2,1,0:T(8,128)(2,1)}, u32[]{:S(2)}) %copy-start) | copy-done | bytes 6291480
  108.8 9.3 %shard_map.65.before = f32[32,128,128]{2,1,0:T(8,128)} custom-call(s32[2]{0:T(128)S(1)} %pad.26.bounds, s32[32,72]{1,0:T(8,128)S(1)} %pad.24.left_at, s32[32,72]{1,0:T(8,128)S(1)} %pad.25.right_at, s32[3,264]{1,0:T(4,128)S(1)} %pad_add_fusion.3.table, s32[3,32]{1,0:T(4,128)S(1)} %get-tuple-element.63.ends, bf16[16,12,128,128]{3,2,1,0:T(8,128)(2,1)S(1)} %copy-done), custom_call_target="tpu_custom_call" | custom-call | tf_op jit(solution)/shard_map/pallas_call | solution.py:194
  118.2 0.6 compare_select_fusion.1
  118.8 8.2 %all-to-all-done.2.rest = bf16[16,4,128,128]{3,2,1,0:T(8,128)(2,1)S(1)} async-done(((bf16[16,4,128,128]{3,2,1,0:T(8,128)(2,1)}), bf16[16,4,128,128]{3,2,1,0:T(8,128)(2,1)S(1)}, u32[]{:S(2)}, u32[]{:S(2)}) %all-to-all-start.2) | async-done | bytes 2097184 | tf_op jit(solution)/shard_map/all_to_all | solution.py:165
  127.0 2.8 %copy-done.1 = bf16[16,12,128,128]{3,2,1,0:T(8,128)(2,1)S(1)} copy-done((bf16[16,12,128,128]{3,2,1,0:T(8,128)(2,1)S(1)}, bf16[16,12,128,128]{3,2,1,0:T(8,128)(2,1)}, u32[]{:S(2)}) %copy-start.1) | copy-done | bytes 6291480
  129.8 2.7 %shard_map.68 = (f32[4,128,128]{2,1,0:T(8,128)S(1)}, f32[4,128,128]{2,1,0:T(8,128)S(1)}) custom-call(s32[5]{0:T(128)S(1)} %pad.23.bounds, s32[32,72]{1,0:T(8,128)S(1)} %pad.24.left_at, s32[32,72]{1,0:T(8,128)S(1)} %pad.25.right_at, s32[3,264]{1,0:T(4,128)S(1)} %pad_add_fusion.2.table, s32[3,32]{1,0:T(4,128)S(1)} %get-tuple-element.64.ends, ...), custom_call_target="tpu_custom_call" | custom-call | tf_op jit(solution)/shard_map/pallas_call | solution.py:207
  132.5 5.9 %collective-permute-start.2 = (f32[4,128,128]{2,1,0:T(8,128)S(1)}, f32[4,128,128]{2,1,0:T(8,128)S(1)}, u32[]{:S(2)}, u32[]{:S(2)}) collective-permute-start(f32[4,128,128]{2,1,0:T(8,128)S(1)} %get-tuple-element.45), channel_id=1, source_target_pairs={{0,1},{1,0},{2,3},{3,2},{4,5},{5,4},{6,7},{7,6},{8,9},{9,8},{10,11... | collective-permute-start | bytes 786440 | tf_op jit(solution)/shard_map/ppermute | solution.py:220
  138.4 2.3 %shard_map.67 = (f32[4,128,128]{2,1,0:T(8,128)S(1)}, f32[4,128,128]{2,1,0:T(8,128)S(1)}) custom-call(s32[5]{0:T(128)S(1)} %pad.23.bounds, s32[32,72]{1,0:T(8,128)S(1)} %pad.24.left_at, s32[32,72]{1,0:T(8,128)S(1)} %pad.25.right_at, s32[3,264]{1,0:T(4,128)S(1)} %pad_add_fusion.2.table, s32[3,32]{1,0:T(4,128)S(1)} %get-tuple-element.64.ends, ...), custom_call_target="tpu_custom_call" | custom-call | tf_op jit(solution)/shard_map/pallas_call | solution.py:207
  140.7 1.4 collective-permute-start.1
  142.2 0.0 collective-permute-done.2
  142.2 0.4 collective-permute-start.3
  142.6 2.3 %shard_map.69 = (f32[4,128,128]{2,1,0:T(8,128)S(1)}, f32[4,128,128]{2,1,0:T(8,128)S(1)}) custom-call(s32[5]{0:T(128)S(1)} %pad.23.bounds, s32[32,72]{1,0:T(8,128)S(1)} %pad.24.left_at, s32[32,72]{1,0:T(8,128)S(1)} %pad.25.right_at, s32[3,264]{1,0:T(4,128)S(1)} %pad_add_fusion.2.table, s32[3,32]{1,0:T(4,128)S(1)} %get-tuple-element.64.ends, ...), custom_call_target="tpu_custom_call" | custom-call | tf_op jit(solution)/shard_map/pallas_call | solution.py:207
  144.9 1.7 %collective-permute-start.5 = (f32[4,128,128]{2,1,0:T(8,128)S(1)}, f32[4,128,128]{2,1,0:T(8,128)S(1)}, u32[]{:S(2)}, u32[]{:S(2)}) collective-permute-start(f32[4,128,128]{2,1,0:T(8,128)S(1)} %get-tuple-element.47), channel_id=1, source_target_pairs={{0,1},{1,0},{2,3},{3,2},{4,5},{5,4},{6,7},{7,6},{8,9},{9,8},{10,11... | collective-permute-start | bytes 786440 | tf_op jit(solution)/shard_map/ppermute | solution.py:220
  146.7 2.3 %shard_map.66 = (f32[4,128,128]{2,1,0:T(8,128)S(1)}, f32[4,128,128]{2,1,0:T(8,128)S(1)}) custom-call(s32[5]{0:T(128)S(1)} %pad.23.bounds, s32[32,72]{1,0:T(8,128)S(1)} %pad.24.left_at, s32[32,72]{1,0:T(8,128)S(1)} %pad.25.right_at, s32[3,264]{1,0:T(4,128)S(1)} %pad_add_fusion.2.table, s32[3,32]{1,0:T(4,128)S(1)} %get-tuple-element.64.ends, ...), custom_call_target="tpu_custom_call" | custom-call | tf_op jit(solution)/shard_map/pallas_call | solution.py:207
  149.0 1.0 collective-permute-start
  150.0 2.2 %collective-permute-start.6 = (f32[2,128,128]{2,1,0:T(8,128)S(1)}, f32[2,128,128]{2,1,0:T(8,128)S(1)}, u32[]{:S(2)}, u32[]{:S(2)}) collective-permute-start(f32[2,128,128]{2,1,0:T(8,128)S(1)} %get-tuple-element.60), channel_id=1, source_target_pairs={{0,6},{1,7},{2,0},{3,1},{4,2},{5,3},{6,4},{7,5},{8,14},{9,15},{10,... | collective-permute-start | bytes 393224 | tf_op jit(solution)/shard_map/ppermute | solution.py:224
  152.1 0.0 collective-permute-done.1
  152.1 0.0 collective-permute-done.3
  152.2 0.1 collective-permute-start.4
  152.2 0.0 collective-permute-done.5
  152.3 2.7 %collective-permute-done.6 = f32[2,128,128]{2,1,0:T(8,128)S(1)} collective-permute-done((f32[2,128,128]{2,1,0:T(8,128)S(1)}, f32[2,128,128]{2,1,0:T(8,128)S(1)}, u32[]{:S(2)}, u32[]{:S(2)}) %collective-permute-start.6) | collective-permute-done | bytes 131104 | tf_op jit(solution)/shard_map/ppermute | solution.py:224
  155.0 3.1 %collective-permute-start.7 = (f32[4,128,128]{2,1,0:T(8,128)S(1)}, f32[4,128,128]{2,1,0:T(8,128)S(1)}, u32[]{:S(2)}, u32[]{:S(2)}) collective-permute-start(f32[4,128,128]{2,1,0:T(8,128)S(1)} %pad_add_fusion), channel_id=1, source_target_pairs={{0,6},{1,7},{2,0},{3,1},{4,2},{5,3},{6,4},{7,5},{8,14},{9,15},{10,... | collective-permute-start | bytes 786440 | tf_op jit(solution)/shard_map/ppermute | solution.py:224
  158.1 0.0 collective-permute-done
  158.1 2.5 %collective-permute-done.4 = f32[4,128,128]{2,1,0:T(8,128)S(1)} collective-permute-done((f32[4,128,128]{2,1,0:T(8,128)S(1)}, f32[4,128,128]{2,1,0:T(8,128)S(1)}, u32[]{:S(2)}, u32[]{:S(2)}) %collective-permute-start.4) | collective-permute-done | bytes 262176 | tf_op jit(solution)/shard_map/ppermute | solution.py:224
  160.6 1.8 %collective-permute-done.7 = f32[4,128,128]{2,1,0:T(8,128)S(1)} collective-permute-done((f32[4,128,128]{2,1,0:T(8,128)S(1)}, f32[4,128,128]{2,1,0:T(8,128)S(1)}, u32[]{:S(2)}, u32[]{:S(2)}) %collective-permute-start.7) | collective-permute-done | bytes 262176 | tf_op jit(solution)/shard_map/ppermute | solution.py:224
  162.4 0.8 add_add_fusion
  (26 shorter events, 0.2 us)
Async XLA Ops:
  21.5 75.9 %copy-start.2 = (s32[32,1,64]{2,1,0:T(1,128)S(1)}, s32[32,1,64]{2,1,0:T(1,128)}, u32[]{:S(2)}) copy-start(s32[32,1,64]{2,1,0:T(1,128)} %param.10) | copy-start | bytes 24580
  21.5 75.9 %copy-start.3 = (s32[32,1,64]{2,1,0:T(1,128)S(1)}, s32[32,1,64]{2,1,0:T(1,128)}, u32[]{:S(2)}) copy-start(s32[32,1,64]{2,1,0:T(1,128)} %param.9) | copy-start | bytes 24580
  21.5 75.9 %copy-start.4 = (s32[32,1]{0,1:T(1,128)S(1)}, s32[32,1]{0,1:T(1,128)}, u32[]{:S(2)}) copy-start(s32[32,1]{0,1:T(1,128)} %param.11) | copy-start | bytes 388
  97.7 29.3 %all-to-all-start.2 = ((bf16[16,4,128,128]{3,2,1,0:T(8,128)(2,1)}), bf16[16,4,128,128]{3,2,1,0:T(8,128)(2,1)S(1)}, u32[]{:S(2)}, u32[]{:S(2)}) async-start(bf16[16,4,128,128]{3,2,1,0:T(8,128)(2,1)} %get-tuple-element.39), calls=%async_computation.2 | async-start | bytes 4194304 | tf_op jit(solution)/shard_map/all_to_all | solution.py:165
  106.1 2.8 %copy-start = (bf16[16,12,128,128]{3,2,1,0:T(8,128)(2,1)S(1)}, bf16[16,12,128,128]{3,2,1,0:T(8,128)(2,1)}, u32[]{:S(2)}) copy-start(bf16[16,12,128,128]{3,2,1,0:T(8,128)(2,1)} %all_to_all.23.got) | copy-start | bytes 18874372
  127.0 2.8 %copy-start.1 = (bf16[16,12,128,128]{3,2,1,0:T(8,128)(2,1)S(1)}, bf16[16,12,128,128]{3,2,1,0:T(8,128)(2,1)}, u32[]{:S(2)}) copy-start(bf16[16,12,128,128]{3,2,1,0:T(8,128)(2,1)} %all_to_all.23.got) | copy-start | bytes 18874372
  132.5 9.7 %collective-permute-start.2 = (f32[4,128,128]{2,1,0:T(8,128)S(1)}, f32[4,128,128]{2,1,0:T(8,128)S(1)}, u32[]{:S(2)}, u32[]{:S(2)}) collective-permute-start(f32[4,128,128]{2,1,0:T(8,128)S(1)} %get-tuple-element.45), channel_id=1, source_target_pairs={{0,1},{1,0},{2,3},{3,2},{4,5},{5,4},{6,7},{7,6},{8,9},{9,8},{10,11... | collective-permute-start | bytes 786440 | tf_op jit(solution)/shard_map/ppermute | solution.py:220
  140.7 11.4 %collective-permute-start.1 = (f32[4,128,128]{2,1,0:T(8,128)S(1)}, f32[4,128,128]{2,1,0:T(8,128)S(1)}, u32[]{:S(2)}, u32[]{:S(2)}) collective-permute-start(f32[4,128,128]{2,1,0:T(8,128)S(1)} %get-tuple-element.43), channel_id=1, source_target_pairs={{0,1},{1,0},{2,3},{3,2},{4,5},{5,4},{6,7},{7,6},{8,9},{9,8},{10,11... | collective-permute-start | bytes 786440 | tf_op jit(solution)/shard_map/ppermute | solution.py:220
  142.2 9.9 %collective-permute-start.3 = (f32[2,128,128]{2,1,0:T(8,128)S(1)}, f32[2,128,128]{2,1,0:T(8,128)S(1)}, u32[]{:S(2)}, u32[]{:S(2)}) collective-permute-start(f32[2,128,128]{2,1,0:T(8,128)S(1)} %get-tuple-element.59), channel_id=1, source_target_pairs={{0,2},{1,3},{2,4},{3,5},{4,6},{5,7},{6,0},{7,1},{8,10},{9,11},{10,... | collective-permute-start | bytes 393224 | tf_op jit(solution)/shard_map/ppermute | solution.py:224
  144.9 7.3 %collective-permute-start.5 = (f32[4,128,128]{2,1,0:T(8,128)S(1)}, f32[4,128,128]{2,1,0:T(8,128)S(1)}, u32[]{:S(2)}, u32[]{:S(2)}) collective-permute-start(f32[4,128,128]{2,1,0:T(8,128)S(1)} %get-tuple-element.47), channel_id=1, source_target_pairs={{0,1},{1,0},{2,3},{3,2},{4,5},{5,4},{6,7},{7,6},{8,9},{9,8},{10,11... | collective-permute-start | bytes 786440 | tf_op jit(solution)/shard_map/ppermute | solution.py:220
  149.0 9.1 %collective-permute-start = (f32[4,128,128]{2,1,0:T(8,128)S(1)}, f32[4,128,128]{2,1,0:T(8,128)S(1)}, u32[]{:S(2)}, u32[]{:S(2)}) collective-permute-start(f32[4,128,128]{2,1,0:T(8,128)S(1)} %get-tuple-element.41), channel_id=1, source_target_pairs={{0,1},{1,0},{2,3},{3,2},{4,5},{5,4},{6,7},{7,6},{8,9},{9,8},{10,11... | collective-permute-start | bytes 786440 | tf_op jit(solution)/shard_map/ppermute | solution.py:220
  150.0 5.0 %collective-permute-start.6 = (f32[2,128,128]{2,1,0:T(8,128)S(1)}, f32[2,128,128]{2,1,0:T(8,128)S(1)}, u32[]{:S(2)}, u32[]{:S(2)}) collective-permute-start(f32[2,128,128]{2,1,0:T(8,128)S(1)} %get-tuple-element.60), channel_id=1, source_target_pairs={{0,6},{1,7},{2,0},{3,1},{4,2},{5,3},{6,4},{7,5},{8,14},{9,15},{10,... | collective-permute-start | bytes 393224 | tf_op jit(solution)/shard_map/ppermute | solution.py:224
  152.2 8.4 %collective-permute-start.4 = (f32[4,128,128]{2,1,0:T(8,128)S(1)}, f32[4,128,128]{2,1,0:T(8,128)S(1)}, u32[]{:S(2)}, u32[]{:S(2)}) collective-permute-start(f32[4,128,128]{2,1,0:T(8,128)S(1)} %pad_add_fusion.1), channel_id=1, source_target_pairs={{0,2},{1,3},{2,4},{3,5},{4,6},{5,7},{6,0},{7,1},{8,10},{9,11},{10,... | collective-permute-start | bytes 786440 | tf_op jit(solution)/shard_map/ppermute | solution.py:224
  155.0 7.5 %collective-permute-start.7 = (f32[4,128,128]{2,1,0:T(8,128)S(1)}, f32[4,128,128]{2,1,0:T(8,128)S(1)}, u32[]{:S(2)}, u32[]{:S(2)}) collective-permute-start(f32[4,128,128]{2,1,0:T(8,128)S(1)} %pad_add_fusion), channel_id=1, source_target_pairs={{0,6},{1,7},{2,0},{3,1},{4,2},{5,3},{6,4},{7,5},{8,14},{9,15},{10,... | collective-permute-start | bytes 786440 | tf_op jit(solution)/shard_map/ppermute | solution.py:224

commit v5 on v4

--- a/solution.py
+++ b/solution.py
@@ -9,7 +9,7 @@
 
 GROUP = 8
 UNROLL = 4
-PACK_STEPS = 4
+PACK_STEPS = 8
 
 
 def pack_body(lists, asked, *refs):
@@ -28,7 +28,7 @@
 def pack(lists, asked, stores):
     peers = asked.shape[0]
     tile = stores[0].shape[1:]
-    whole = pl.BlockSpec(stores[0].shape, lambda i: (0, 0, 0))
+    whole = pl.BlockSpec(memory_space=pltpu.VMEM)
     return pl.pallas_call(
         functools.partial(pack_body, lists),
         grid=(PACK_STEPS,),
@@ -37,6 +37,7 @@
             pl.BlockSpec((peers // PACK_STEPS, len(picks)) + tile, lambda i: (i, 0, 0, 0)) for picks in lists
         ],
         out_shape=[jax.ShapeDtypeStruct((peers, len(picks)) + tile, stores[0].dtype) for picks in lists],
+        compiler_params=pltpu.CompilerParams(vmem_limit_bytes=24 * 2**20),
     )(asked, *stores)
 
 
@@ -114,6 +115,16 @@
         out[...] = acc[span] + old[span]
 
 
+def load_body(first, bounds, left_at, right_at, table, ends, got, rest, before, other, mine, amp, acc, old, sems):
+    cap = got.shape[1] - rest.shape[1]
+    copy = pltpu.make_async_copy(got.at[:, pl.ds(0, cap)], amp.at[:, pl.ds(0, cap)], sems.at[1])
+    copy.start()
+    copy.wait()
+    second_body(
+        first, bounds, left_at, right_at, table, ends, amp, rest, before, other, mine, acc, old, sems.at[0]
+    )
+
+
 def group_table(order, start, stop, slots):
     rows = start.shape[0]
     at = order[:, None] == jnp.arange(rows)[None, :]
@@ -157,7 +168,8 @@
     first_list = tuple((0, s) for s in range(cap)) + tuple((1, s) for s in range(cut))
     second_list = tuple((1, s) for s in range(cut, cap))
     asked, me = lax.optimization_barrier((asked, me))
-    send_first, send_second = pack((first_list, second_list), asked, (amp_tiles, int_tiles))
+    stores = tuple(pltpu.with_memory_space_constraint(store, pltpu.VMEM) for store in (amp_tiles, int_tiles))
+    send_first, send_second = pack((first_list, second_list), asked, stores)
     got_first = lax.all_to_all(send_first, "own", split_axis=0, concat_axis=0, tiled=True)
     got_first, send_second, tri_amp, tri_int, tri_count, me = lax.optimization_barrier(
         (got_first, send_second, tri_amp, tri_int, tri_count, me)
@@ -202,21 +214,29 @@
 
     before = pltpu.with_memory_space_constraint(before, pltpu.HBM)
 
-    def second(step):
+    def second(step, amp=None):
         half = jax.ShapeDtypeStruct((share,) + tile, jnp.float32)
+        load = amp is None
+        sems = pltpu.SemaphoreType.DMA((2,)) if load else pltpu.SemaphoreType.DMA(())
+        hbm = pl.BlockSpec(memory_space=pltpu.HBM)
         return pl.pallas_call(
-            functools.partial(second_body, step * 2 * share),
-            in_specs=[smem] * 5 + [vmem] * 2 + [pl.BlockSpec(memory_space=pltpu.HBM)],
-            out_specs=[vmem, vmem],
-            out_shape=[half, half],
-            scratch_shapes=[pltpu.VMEM((2 * share,) + tile, jnp.float32)] * 2 + [pltpu.SemaphoreType.DMA(())],
+            functools.partial(load_body if load else second_body, step * 2 * share),
+            in_specs=[smem] * 5 + [hbm if load else vmem, vmem, hbm],
+            out_specs=[vmem] * (3 if load else 2),
+            out_shape=[half, half] + ([jax.ShapeDtypeStruct(got_first.shape, got_first.dtype)] if load else []),
+            scratch_shapes=[pltpu.VMEM((2 * share,) + tile, jnp.float32)] * 2 + [sems],
             compiler_params=params,
-        )(second_bounds, left_at, right_at, second_table, second_ends, got_first, got_second, before)
-
+        )(
+            second_bounds, left_at, right_at, second_table, second_ends, got_hbm if load else amp, got_second, before
+        )
+
+    got_hbm = pltpu.with_memory_space_constraint(got_first, pltpu.HBM)
+    held = []
     swap = [(i, i ^ 1) for i in range(red)]
 
     def met(step, spans=(slice(None),), extra=0.0):
-        other, mine = second(step)
+        other, mine, *amp = second(step, *held)
+        held.extend(amp)
         theirs = lax.ppermute(other, "red", swap)
         return [mine[span] + theirs[span] + extra for span in spans]
 

time: 165 us -> 165 us (level)
  waiting for transfers between devices: 15.3 us -> 19.2 us
  Pallas kernels: 24.9 us -> 22.7 us
    ppermute x4, waiting for transfers between devices: 7.06 us -> 11.5 us  [send(): lax.ppermute(value, 'red', [(i, (i // 2 + distance) % steps * 2 + i % 2)...]
    pallas_call x1, Pallas kernels: 5.85 us -> 1.46 us  [pack(): pl.pallas_call(functools.partial(pack_body, lists), grid=(PACK_STEPS,), i...]
    pallas_call x4, Pallas kernels: 9.68 us -> 11.9 us  [second(): pl.pallas_call(functools.partial(load_body if load else second_body, step...]
    unnamed x10 -> x14, local copies, waits for them, and re-layouts: 5.57 us -> 5.97 us
where the time goes in v5:
time: 165 us; the launch traced here: 164 us
  blocking collectives  89.4 us (54%)
  Pallas kernels  22.7 us (14%)
  starting transfers between devices  19.2 us (12%)
  waiting for transfers between devices  19.2 us (12%)
  local copies, waits for them, and re-layouts  8.93 us (5%)
  other arithmetic  4.18 us (3%)
    all_to_all x1, blocking collectives, body(): lax.all_to_all(send_first, 'own', split_axis=0, concat_axis=0, tiled=True)  74.6 us
    all_to_all x1, blocking collectives, body(): lax.all_to_all(wanted.reshape(peers, kinds * cap), 'own', split_axis=0, c...  14.8 us
    pallas_call x4, Pallas kernels, second(): pl.pallas_call(functools.partial(load_body if load else second_body, step...  11.9 us
    ppermute x4, waiting for transfers between devices, send(): lax.ppermute(value, 'red', [(i, (i // 2 + distance) % steps * 2 + i % 2)...  11.5 us
    ppermute x4, starting transfers between devices, met(): theirs = lax.ppermute(other, 'red', swap)  10 us
    pallas_call x1, Pallas kernels, body(): pl.pallas_call(first_body, in_specs=[smem] * 5 + [vmem], out_specs=pl.Blo...  9.4 us
    all_to_all x1, waiting for transfers between devices, body(): lax.all_to_all(send_second, 'own', split_axis=0, concat_axis=0, tiled=True)  7.7 us
    unnamed x14, local copies, waits for them, and re-layouts  5.97 us
  transfers between devices with their start and end apart: 9, of which 4 were waited for; matrix products, arithmetic and copies ran while one was open for 3% of the time, Pallas kernels for 10%

profile of v5, /device:TPU:1, one launch (start us, length us, event | category | flops | bytes accessed | tf_op | source)
XLA Modules:
  0.0 164.0 jit_solution(18043431375401911449)
XLA Ops:
  0.0 0.8 copy.22
  0.8 14.8 %all_to_all.22 = s32[16,1,16]{2,1,0:T(1,128)S(1)} all-to-all(s32[16,1,16]{2,1,0:T(1,128)S(1)} %copy.22), channel_id=1, replica_groups=mesh['own'=16,'red'=8] {'own'}, dimensions={0} | all-to-all | bytes 2048 | tf_op jit(solution)/shard_map/all_to_all | solution.py:167
  15.6 1.6 copy-done.1
  17.2 1.6 copy-done.2
  18.8 1.5 shard_map.64
  20.2 74.6 %all_to_all.23.got = bf16[16,12,128,128]{3,2,1,0:T(8,128)(2,1)} all-to-all(bf16[16,12,128,128]{3,2,1,0:T(8,128)(2,1)S(1)} %get-tuple-element.31), channel_id=1, replica_groups=mesh['own'=16,'red'=8] {'own'}, dimensions={0} | all-to-all | bytes 12582912 | tf_op jit(solution)/shard_map/all_to_all | solution.py:173
  94.9 3.9 %all-to-all-start.2 = ((bf16[16,4,128,128]{3,2,1,0:T(8,128)(2,1)}), bf16[16,4,128,128]{3,2,1,0:T(8,128)(2,1)S(1)}, u32[]{:S(2)}, u32[]{:S(2)}) async-start(bf16[16,4,128,128]{3,2,1,0:T(8,128)(2,1)} %copy-done.3), calls=%async_computation.2 | async-start | bytes 4194304 | tf_op jit(solution)/shard_map/all_to_all | solution.py:177
  98.8 0.1 multiply_add_fusion
  98.9 0.2 convert_reduce_fusion.2
  99.1 0.2 select_reduce_fusion.7
  99.3 0.1 select_reduce_fusion.5
  99.4 0.7 slice.23
  100.0 0.1 slice.22
  100.1 0.6 slice.24
  100.7 0.6 pad.26.bounds
  101.3 0.1 pad.23.bounds
  101.4 0.1 select_reduce_fusion.2
  101.5 0.1 select_reduce_fusion
  101.6 0.1 select_reduce_fusion.4
  101.8 0.1 copy.23
  101.8 1.0 sort.14
  102.9 0.1 copy.24
  102.9 0.1 select_select_fusion
  103.0 0.6 compare_select_fusion
  103.7 2.8 %copy-done = bf16[16,12,128,128]{3,2,1,0:T(8,128)(2,1)S(1)} copy-done((bf16[16,12,128,128]{3,2,1,0:T(8,128)(2,1)S(1)}, bf16[16,12,128,128]{3,2,1,0:T(8,128)(2,1)}, u32[]{:S(2)}) %copy-start) | copy-done | bytes 6291480
  106.5 9.4 %shard_map.65.before = f32[32,128,128]{2,1,0:T(8,128)} custom-call(s32[2]{0:T(128)S(1)} %pad.26.bounds, s32[32,72]{1,0:T(8,128)S(1)} %pad.24.left_at, s32[32,72]{1,0:T(8,128)S(1)} %pad.25.right_at, s32[3,264]{1,0:T(4,128)S(1)} %pad_add_fusion.3.table, s32[3,32]{1,0:T(4,128)S(1)} %get-tuple-element.65.ends, bf16[16,12,128,128]{3,2,1,0:T(8,128)(2,1)S(1)} %copy-done), custom_call_target="tpu_custom_call" | custom-call | tf_op jit(solution)/shard_map/pallas_call | solution.py:206
  115.9 0.7 compare_select_fusion.1
  116.6 7.7 %all-to-all-done.2.rest = bf16[16,4,128,128]{3,2,1,0:T(8,128)(2,1)S(1)} async-done(((bf16[16,4,128,128]{3,2,1,0:T(8,128)(2,1)}), bf16[16,4,128,128]{3,2,1,0:T(8,128)(2,1)S(1)}, u32[]{:S(2)}, u32[]{:S(2)}) %all-to-all-start.2) | async-done | bytes 2097184 | tf_op jit(solution)/shard_map/all_to_all | solution.py:177
  124.3 4.9 %shard_map.66 = (f32[4,128,128]{2,1,0:T(8,128)S(1)}, f32[4,128,128]{2,1,0:T(8,128)S(1)}, bf16[16,12,128,128]{3,2,1,0:T(8,128)(2,1)S(1)}) custom-call(s32[5]{0:T(128)S(1)} %pad.23.bounds, s32[32,72]{1,0:T(8,128)S(1)} %pad.24.left_at, s32[32,72]{1,0:T(8,128)S(1)} %pad.25.right_at, s32[3,264]{1,0:T(4,128)S(1)} %pad_add_fusion.2.table, ...), custom_call_target="tpu_custom_call" | custom-call | tf_op jit(solution)/shard_map/pallas_call | solution.py:222
  129.2 5.8 %collective-permute-start.2 = (f32[4,128,128]{2,1,0:T(8,128)S(1)}, f32[4,128,128]{2,1,0:T(8,128)S(1)}, u32[]{:S(2)}, u32[]{:S(2)}) collective-permute-start(f32[4,128,128]{2,1,0:T(8,128)S(1)} %get-tuple-element.47), channel_id=1, source_target_pairs={{0,1},{1,0},{2,3},{3,2},{4,5},{5,4},{6,7},{7,6},{8,9},{9,8},{10,11... | collective-permute-start | bytes 786440 | tf_op jit(solution)/shard_map/ppermute | solution.py:240
  135.1 2.3 %shard_map.69 = (f32[4,128,128]{2,1,0:T(8,128)S(1)}, f32[4,128,128]{2,1,0:T(8,128)S(1)}) custom-call(s32[5]{0:T(128)S(1)} %pad.23.bounds, s32[32,72]{1,0:T(8,128)S(1)} %pad.24.left_at, s32[32,72]{1,0:T(8,128)S(1)} %pad.25.right_at, s32[3,264]{1,0:T(4,128)S(1)} %pad_add_fusion.2.table, s32[3,32]{1,0:T(4,128)S(1)} %get-tuple-element.66.ends, ...), custom_call_target="tpu_custom_call" | custom-call | tf_op jit(solution)/shard_map/pallas_call | solution.py:222
  137.4 1.0 collective-permute-start.5
  138.4 0.0 collective-permute-done.2
  138.4 2.6 %collective-permute-start.6 = (f32[2,128,128]{2,1,0:T(8,128)S(1)}, f32[2,128,128]{2,1,0:T(8,128)S(1)}, u32[]{:S(2)}, u32[]{:S(2)}) collective-permute-start(f32[2,128,128]{2,1,0:T(8,128)S(1)} %get-tuple-element.62), channel_id=1, source_target_pairs={{0,6},{1,7},{2,0},{3,1},{4,2},{5,3},{6,4},{7,5},{8,14},{9,15},{10,... | collective-permute-start | bytes 393224 | tf_op jit(solution)/shard_map/ppermute | solution.py:244
  141.0 2.3 %shard_map.68 = (f32[4,128,128]{2,1,0:T(8,128)S(1)}, f32[4,128,128]{2,1,0:T(8,128)S(1)}) custom-call(s32[5]{0:T(128)S(1)} %pad.23.bounds, s32[32,72]{1,0:T(8,128)S(1)} %pad.24.left_at, s32[32,72]{1,0:T(8,128)S(1)} %pad.25.right_at, s32[3,264]{1,0:T(4,128)S(1)} %pad_add_fusion.2.table, s32[3,32]{1,0:T(4,128)S(1)} %get-tuple-element.66.ends, ...), custom_call_target="tpu_custom_call" | custom-call | tf_op jit(solution)/shard_map/pallas_call | solution.py:222
  143.3 2.2 %collective-permute-start.1 = (f32[4,128,128]{2,1,0:T(8,128)S(1)}, f32[4,128,128]{2,1,0:T(8,128)S(1)}, u32[]{:S(2)}, u32[]{:S(2)}) collective-permute-start(f32[4,128,128]{2,1,0:T(8,128)S(1)} %get-tuple-element.45), channel_id=1, source_target_pairs={{0,1},{1,0},{2,3},{3,2},{4,5},{5,4},{6,7},{7,6},{8,9},{9,8},{10,11... | collective-permute-start | bytes 786440 | tf_op jit(solution)/shard_map/ppermute | solution.py:240
  145.5 2.3 %shard_map.67 = (f32[4,128,128]{2,1,0:T(8,128)S(1)}, f32[4,128,128]{2,1,0:T(8,128)S(1)}) custom-call(s32[5]{0:T(128)S(1)} %pad.23.bounds, s32[32,72]{1,0:T(8,128)S(1)} %pad.24.left_at, s32[32,72]{1,0:T(8,128)S(1)} %pad.25.right_at, s32[3,264]{1,0:T(4,128)S(1)} %pad_add_fusion.2.table, s32[3,32]{1,0:T(4,128)S(1)} %get-tuple-element.66.ends, ...), custom_call_target="tpu_custom_call" | custom-call | tf_op jit(solution)/shard_map/pallas_call | solution.py:222
  147.8 1.0 collective-permute-start
  148.8 0.0 collective-permute-start.3
  148.8 0.0 collective-permute-done.5
  148.8 0.0 collective-permute-done.6
  148.8 2.7 %collective-permute-start.7 = (f32[4,128,128]{2,1,0:T(8,128)S(1)}, f32[4,128,128]{2,1,0:T(8,128)S(1)}, u32[]{:S(2)}, u32[]{:S(2)}) collective-permute-start(f32[4,128,128]{2,1,0:T(8,128)S(1)} %pad_add_fusion), channel_id=1, source_target_pairs={{0,6},{1,7},{2,0},{3,1},{4,2},{5,3},{6,4},{7,5},{8,14},{9,15},{10,... | collective-permute-start | bytes 786440 | tf_op jit(solution)/shard_map/ppermute | solution.py:244
  151.6 0.0 collective-permute-done.1
  151.6 3.4 %collective-permute-done.3 = f32[2,128,128]{2,1,0:T(8,128)S(1)} collective-permute-done((f32[2,128,128]{2,1,0:T(8,128)S(1)}, f32[2,128,128]{2,1,0:T(8,128)S(1)}, u32[]{:S(2)}, u32[]{:S(2)}) %collective-permute-start.3) | collective-permute-done | bytes 131104 | tf_op jit(solution)/shard_map/ppermute | solution.py:244
  155.0 0.1 collective-permute-start.4
  155.1 1.8 %collective-permute-done.7 = f32[4,128,128]{2,1,0:T(8,128)S(1)} collective-permute-done((f32[4,128,128]{2,1,0:T(8,128)S(1)}, f32[4,128,128]{2,1,0:T(8,128)S(1)}, u32[]{:S(2)}, u32[]{:S(2)}) %collective-permute-start.7) | collective-permute-done | bytes 262176 | tf_op jit(solution)/shard_map/ppermute | solution.py:244
  156.9 6.3 %collective-permute-done.4 = f32[4,128,128]{2,1,0:T(8,128)S(1)} collective-permute-done((f32[4,128,128]{2,1,0:T(8,128)S(1)}, f32[4,128,128]{2,1,0:T(8,128)S(1)}, u32[]{:S(2)}, u32[]{:S(2)}) %collective-permute-start.4) | collective-permute-done | bytes 262176 | tf_op jit(solution)/shard_map/ppermute | solution.py:244
  163.2 0.8 add_add_fusion
  (30 shorter events, 0.3 us)
Async XLA Ops:
  15.6 1.6 copy-start.1
  17.2 1.6 copy-start.2
  20.2 74.6 %copy-start.3 = (bf16[16,4,128,128]{3,2,1,0:T(8,128)(2,1)}, bf16[16,4,128,128]{3,2,1,0:T(8,128)(2,1)S(1)}, u32[]{:S(2)}) copy-start(bf16[16,4,128,128]{3,2,1,0:T(8,128)(2,1)S(1)} %get-tuple-element.40) | copy-start | bytes 6291460
  94.9 3.9 %copy-start.4 = (s32[32,1,64]{2,1,0:T(1,128)S(1)}, s32[32,1,64]{2,1,0:T(1,128)}, u32[]{:S(2)}) copy-start(s32[32,1,64]{2,1,0:T(1,128)} %param.10) | copy-start | bytes 24580
  94.9 3.9 %copy-start.5 = (s32[32,1,64]{2,1,0:T(1,128)S(1)}, s32[32,1,64]{2,1,0:T(1,128)}, u32[]{:S(2)}) copy-start(s32[32,1,64]{2,1,0:T(1,128)} %param.9) | copy-start | bytes 24580
  94.9 3.9 %copy-start.6 = (s32[32,1]{0,1:T(1,128)S(1)}, s32[32,1]{0,1:T(1,128)}, u32[]{:S(2)}) copy-start(s32[32,1]{0,1:T(1,128)} %param.11) | copy-start | bytes 388
  94.9 29.4 %all-to-all-start.2 = ((bf16[16,4,128,128]{3,2,1,0:T(8,128)(2,1)}), bf16[16,4,128,128]{3,2,1,0:T(8,128)(2,1)S(1)}, u32[]{:S(2)}, u32[]{:S(2)}) async-start(bf16[16,4,128,128]{3,2,1,0:T(8,128)(2,1)} %copy-done.3), calls=%async_computation.2 | async-start | bytes 4194304 | tf_op jit(solution)/shard_map/all_to_all | solution.py:177
  103.7 2.8 %copy-start = (bf16[16,12,128,128]{3,2,1,0:T(8,128)(2,1)S(1)}, bf16[16,12,128,128]{3,2,1,0:T(8,128)(2,1)}, u32[]{:S(2)}) copy-start(bf16[16,12,128,128]{3,2,1,0:T(8,128)(2,1)} %all_to_all.23.got) | copy-start | bytes 18874372
  129.2 9.2 %collective-permute-start.2 = (f32[4,128,128]{2,1,0:T(8,128)S(1)}, f32[4,128,128]{2,1,0:T(8,128)S(1)}, u32[]{:S(2)}, u32[]{:S(2)}) collective-permute-start(f32[4,128,128]{2,1,0:T(8,128)S(1)} %get-tuple-element.47), channel_id=1, source_target_pairs={{0,1},{1,0},{2,3},{3,2},{4,5},{5,4},{6,7},{7,6},{8,9},{9,8},{10,11... | collective-permute-start | bytes 786440 | tf_op jit(solution)/shard_map/ppermute | solution.py:240
  137.4 11.4 %collective-permute-start.5 = (f32[4,128,128]{2,1,0:T(8,128)S(1)}, f32[4,128,128]{2,1,0:T(8,128)S(1)}, u32[]{:S(2)}, u32[]{:S(2)}) collective-permute-start(f32[4,128,128]{2,1,0:T(8,128)S(1)} %get-tuple-element.49), channel_id=1, source_target_pairs={{0,1},{1,0},{2,3},{3,2},{4,5},{5,4},{6,7},{7,6},{8,9},{9,8},{10,11... | collective-permute-start | bytes 786440 | tf_op jit(solution)/shard_map/ppermute | solution.py:240
  138.4 10.4 %collective-permute-start.6 = (f32[2,128,128]{2,1,0:T(8,128)S(1)}, f32[2,128,128]{2,1,0:T(8,128)S(1)}, u32[]{:S(2)}, u32[]{:S(2)}) collective-permute-start(f32[2,128,128]{2,1,0:T(8,128)S(1)} %get-tuple-element.62), channel_id=1, source_target_pairs={{0,6},{1,7},{2,0},{3,1},{4,2},{5,3},{6,4},{7,5},{8,14},{9,15},{10,... | collective-permute-start | bytes 393224 | tf_op jit(solution)/shard_map/ppermute | solution.py:244
  143.3 8.3 %collective-permute-start.1 = (f32[4,128,128]{2,1,0:T(8,128)S(1)}, f32[4,128,128]{2,1,0:T(8,128)S(1)}, u32[]{:S(2)}, u32[]{:S(2)}) collective-permute-start(f32[4,128,128]{2,1,0:T(8,128)S(1)} %get-tuple-element.45), channel_id=1, source_target_pairs={{0,1},{1,0},{2,3},{3,2},{4,5},{5,4},{6,7},{7,6},{8,9},{9,8},{10,11... | collective-permute-start | bytes 786440 | tf_op jit(solution)/shard_map/ppermute | solution.py:240
  147.8 7.3 %collective-permute-start = (f32[4,128,128]{2,1,0:T(8,128)S(1)}, f32[4,128,128]{2,1,0:T(8,128)S(1)}, u32[]{:S(2)}, u32[]{:S(2)}) collective-permute-start(f32[4,128,128]{2,1,0:T(8,128)S(1)} %get-tuple-element.43), channel_id=1, source_target_pairs={{0,1},{1,0},{2,3},{3,2},{4,5},{5,4},{6,7},{7,6},{8,9},{9,8},{10,11... | collective-permute-start | bytes 786440 | tf_op jit(solution)/shard_map/ppermute | solution.py:240
  148.8 6.2 %collective-permute-start.3 = (f32[2,128,128]{2,1,0:T(8,128)S(1)}, f32[2,128,128]{2,1,0:T(8,128)S(1)}, u32[]{:S(2)}, u32[]{:S(2)}) collective-permute-start(f32[2,128,128]{2,1,0:T(8,128)S(1)} %get-tuple-element.61), channel_id=1, source_target_pairs={{0,2},{1,3},{2,4},{3,5},{4,6},{5,7},{6,0},{7,1},{8,10},{9,11},{10,... | collective-permute-start | bytes 393224 | tf_op jit(solution)/shard_map/ppermute | solution.py:244
  148.8 8.0 %collective-permute-start.7 = (f32[4,128,128]{2,1,0:T(8,128)S(1)}, f32[4,128,128]{2,1,0:T(8,128)S(1)}, u32[]{:S(2)}, u32[]{:S(2)}) collective-permute-start(f32[4,128,128]{2,1,0:T(8,128)S(1)} %pad_add_fusion), channel_id=1, source_target_pairs={{0,6},{1,7},{2,0},{3,1},{4,2},{5,3},{6,4},{7,5},{8,14},{9,15},{10,... | collective-permute-start | bytes 786440 | tf_op jit(solution)/shard_map/ppermute | solution.py:244
  155.0 8.2 %collective-permute-start.4 = (f32[4,128,128]{2,1,0:T(8,128)S(1)}, f32[4,128,128]{2,1,0:T(8,128)S(1)}, u32[]{:S(2)}, u32[]{:S(2)}) collective-permute-start(f32[4,128,128]{2,1,0:T(8,128)S(1)} %pad_add_fusion.1), channel_id=1, source_target_pairs={{0,2},{1,3},{2,4},{3,5},{4,6},{5,7},{6,0},{7,1},{8,10},{9,11},{10,... | collective-permute-start | bytes 786440 | tf_op jit(solution)/shard_map/ppermute | solution.py:244

commit v6 on v5

--- a/solution.py
+++ b/solution.py
@@ -10,10 +10,29 @@
 GROUP = 8
 UNROLL = 4
 PACK_STEPS = 8
-
-
-def pack_body(lists, asked, *refs):
-    stores, outs = refs[:2], refs[2:]
+PARTS = 4
+
+
+def copy_parts(pairs, sems):
+    copies = []
+    for number, (source, target) in enumerate(pairs):
+        size = source.shape[0] // PARTS
+        for i in range(PARTS):
+            span = pl.ds(i * size, size)
+            copies.append(pltpu.make_async_copy(source.at[span], target.at[span], sems.at[number * PARTS + i]))
+    for copy in copies:
+        copy.start()
+    for copy in copies:
+        copy.wait()
+
+
+def pack_body(lists, asked, first_store, second_store, first_out, second_out, first_held, second_held, sems):
+    stores, outs = (first_held, second_held), (first_out, second_out)
+
+    @pl.when(pl.program_id(0) == 0)
+    def _():
+        copy_parts(((first_store, first_held), (second_store, second_held)), sems)
+
     cap = asked.shape[1] // 2
     last = stores[0].shape[0] - 1
     peers = outs[0].shape[0]
@@ -28,7 +47,7 @@
 def pack(lists, asked, stores):
     peers = asked.shape[0]
     tile = stores[0].shape[1:]
-    whole = pl.BlockSpec(memory_space=pltpu.VMEM)
+    whole = pl.BlockSpec(memory_space=pltpu.HBM)
     return pl.pallas_call(
         functools.partial(pack_body, lists),
         grid=(PACK_STEPS,),
@@ -37,6 +56,8 @@
             pl.BlockSpec((peers // PACK_STEPS, len(picks)) + tile, lambda i: (i, 0, 0, 0)) for picks in lists
         ],
         out_shape=[jax.ShapeDtypeStruct((peers, len(picks)) + tile, stores[0].dtype) for picks in lists],
+        scratch_shapes=[pltpu.VMEM(store.shape, store.dtype) for store in stores]
+        + [pltpu.SemaphoreType.DMA((2 * PARTS,))],
         compiler_params=pltpu.CompilerParams(vmem_limit_bytes=24 * 2**20),
     )(asked, *stores)
 
@@ -50,9 +71,10 @@
     )
 
 
-def contract(bounds, left_at, right_at, table, ends, left, right, acc, first):
+def contract(bounds, left_at, right_at, table, ends, left, right, acc, first, zero):
     places = acc.shape[0]
-    begin, finish = bounds[first // places], bounds[first // places + 1]
+    begin = bounds[first - 1] if first else 0
+    finish = bounds[first + places - 1]
 
     def full_step(i, carry):
         sums = []
@@ -78,8 +100,7 @@
             base = stop - ends[2, place] % GROUP
             lefts, rights = [], []
             for j in range(GROUP):
-                tile = left[left_at[row, base + j]]
-                lefts.append(jnp.where(base + j < stop, tile, jnp.zeros_like(tile)))
+                lefts.append(left[jnp.where(base + j < stop, left_at[row, base + j], zero)])
                 rights.append(right[right_at[row, base + j]])
             sums.append(group_dot(lefts, rights))
         for u in range(UNROLL):
@@ -94,13 +115,14 @@
     return ref.reshape((ref.shape[0] * ref.shape[1],) + ref.shape[2:])
 
 
-def first_body(bounds, left_at, right_at, table, ends, got, out, acc, sem):
+def first_body(bounds, left_at, right_at, table, ends, got, out, acc, buf, sems):
+    holders, width = got.shape[0], got.shape[1]
     acc[...] = jnp.zeros(acc.shape, acc.dtype)
-    flat = flatten(got)
-    contract(bounds, left_at, right_at, table, ends, flat, flat, acc, 0)
-    copy = pltpu.make_async_copy(acc, out, sem)
-    copy.start()
-    copy.wait()
+    copy_parts(((got, buf.at[pl.ds(0, holders)]),), sems)
+    buf[holders, 0] = jnp.zeros(buf.shape[2:], buf.dtype)
+    flat = flatten(buf)
+    contract(bounds, left_at, right_at, table, ends, flat, flat, acc, 0, holders * width)
+    copy_parts(((acc, out),), sems)
 
 
 def second_body(first, bounds, left_at, right_at, table, ends, got, rest, before, other, mine, acc, old, sem):
@@ -108,7 +130,7 @@
     copy = pltpu.make_async_copy(before.at[pl.ds(first, places)], old, sem)
     copy.start()
     acc[...] = jnp.zeros(acc.shape, acc.dtype)
-    contract(bounds, left_at, right_at, table, ends, flatten(got), flatten(rest), acc, first)
+    contract(bounds, left_at, right_at, table, ends, flatten(got), flatten(rest), acc, first, got.shape[1] - rest.shape[1])
     copy.wait()
     for half, out in enumerate((other, mine)):
         span = pl.ds(half * (places // 2), places // 2)
@@ -117,11 +139,10 @@
 
 def load_body(first, bounds, left_at, right_at, table, ends, got, rest, before, other, mine, amp, acc, old, sems):
     cap = got.shape[1] - rest.shape[1]
-    copy = pltpu.make_async_copy(got.at[:, pl.ds(0, cap)], amp.at[:, pl.ds(0, cap)], sems.at[1])
-    copy.start()
-    copy.wait()
+    copy_parts(((got.at[:, pl.ds(0, cap)], amp.at[:, pl.ds(0, cap)]),), sems)
+    amp[0, cap] = jnp.zeros(amp.shape[2:], amp.dtype)
     second_body(
-        first, bounds, left_at, right_at, table, ends, amp, rest, before, other, mine, acc, old, sems.at[0]
+        first, bounds, left_at, right_at, table, ends, amp, rest, before, other, mine, acc, old, sems.at[PARTS]
     )
 
 
@@ -168,7 +189,7 @@
     first_list = tuple((0, s) for s in range(cap)) + tuple((1, s) for s in range(cut))
     second_list = tuple((1, s) for s in range(cut, cap))
     asked, me = lax.optimization_barrier((asked, me))
-    stores = tuple(pltpu.with_memory_space_constraint(store, pltpu.VMEM) for store in (amp_tiles, int_tiles))
+    stores = tuple(pltpu.with_memory_space_constraint(store, pltpu.HBM) for store in (amp_tiles, int_tiles))
     send_first, send_second = pack((first_list, second_list), asked, stores)
     got_first = lax.all_to_all(send_first, "own", split_axis=0, concat_axis=0, tiled=True)
     got_first, send_second, tri_amp, tri_int, tri_count, me = lax.optimization_barrier(
@@ -195,30 +216,33 @@
     place = jnp.arange(rows, dtype=jnp.int32)
     step, side = place // (2 * share), (place // share) % 2
     order = (((me // 2 + step) % steps) * 2 + jnp.where(side == 0, 1 - me % 2, me % 2)) * share + place % share
-    first_end, first_table, first_ends = group_table(order, jnp.zeros_like(low), low, slots)
-    second_end, second_table, second_ends = group_table(order, low, count, slots)
-    first_bounds = jnp.pad(first_end[rows - 1 :], (1, 0))
-    second_bounds = jnp.pad(second_end[2 * share - 1 :: 2 * share], (1, 0))
+    first_bounds, first_table, first_ends = group_table(order, jnp.zeros_like(low), low, slots)
+    second_bounds, second_table, second_ends = group_table(order, low, count, slots)
 
     smem = pl.BlockSpec(memory_space=pltpu.SMEM)
     vmem = pl.BlockSpec(memory_space=pltpu.VMEM)
     params = pltpu.CompilerParams(vmem_limit_bytes=24 * 2**20)
+    hbm = pl.BlockSpec(memory_space=pltpu.HBM)
+    got_hbm = pltpu.with_memory_space_constraint(got_first, pltpu.HBM)
     before = pl.pallas_call(
         first_body,
-        in_specs=[smem] * 5 + [vmem],
-        out_specs=pl.BlockSpec(memory_space=pltpu.HBM),
+        in_specs=[smem] * 5 + [hbm],
+        out_specs=hbm,
         out_shape=pltpu.HBM((rows,) + tile, jnp.float32),
-        scratch_shapes=[pltpu.VMEM((rows,) + tile, jnp.float32), pltpu.SemaphoreType.DMA(())],
+        scratch_shapes=[
+            pltpu.VMEM((rows,) + tile, jnp.float32),
+            pltpu.VMEM((peers + 1, width) + tile, got_first.dtype),
+            pltpu.SemaphoreType.DMA((PARTS,)),
+        ],
         compiler_params=params,
-    )(first_bounds, left_at, right_at, first_table, first_ends, got_first)
+    )(first_bounds, left_at, right_at, first_table, first_ends, got_hbm)
 
     before = pltpu.with_memory_space_constraint(before, pltpu.HBM)
 
     def second(step, amp=None):
         half = jax.ShapeDtypeStruct((share,) + tile, jnp.float32)
         load = amp is None
-        sems = pltpu.SemaphoreType.DMA((2,)) if load else pltpu.SemaphoreType.DMA(())
-        hbm = pl.BlockSpec(memory_space=pltpu.HBM)
+        sems = pltpu.SemaphoreType.DMA((PARTS + 1,)) if load else pltpu.SemaphoreType.DMA(())
         return pl.pallas_call(
             functools.partial(load_body if load else second_body, step * 2 * share),
             in_specs=[smem] * 5 + [hbm if load else vmem, vmem, hbm],
@@ -230,7 +254,6 @@
             second_bounds, left_at, right_at, second_table, second_ends, got_hbm if load else amp, got_second, before
         )
 
-    got_hbm = pltpu.with_memory_space_constraint(got_first, pltpu.HBM)
     held = []
     swap = [(i, i ^ 1) for i in range(red)]
 

time: 165 us -> 164 us (level)
  local copies, waits for them, and re-layouts: 8.93 us -> 2.16 us
  Pallas kernels: 22.7 us -> 27.4 us
    unnamed x14 -> x8, local copies, waits for them, and re-layouts: 5.97 us -> 0.02 us
    pallas_call x1, Pallas kernels: 9.4 us -> 11.8 us  [body(): pl.pallas_call(first_body, in_specs=[smem] * 5 + [hbm], out_specs=hbm, ou...]
    pallas_call x1, Pallas kernels: 1.46 us -> 3.8 us  [pack(): pl.pallas_call(functools.partial(pack_body, lists), grid=(PACK_STEPS,), i...]
  transfers between devices with their start and end apart: 9 -> 9, of which waited for: 4 -> 4; matrix products, arithmetic and copies ran while one was open for 3% -> 3% of each run, Pallas kernels for 10% -> 12%
where the time goes in v6:
time: 164 us; the launch traced here: 163 us
  blocking collectives  89.4 us (55%)
  Pallas kernels  27.4 us (17%)
  waiting for transfers between devices  20.4 us (12%)
  starting transfers between devices  19 us (12%)
  other arithmetic  4.15 us (3%)
  local copies, waits for them, and re-layouts  2.16 us (1%)
    all_to_all x1, blocking collectives, body(): lax.all_to_all(send_first, 'own', split_axis=0, concat_axis=0, tiled=True)  74.6 us
    all_to_all x1, blocking collectives, body(): lax.all_to_all(wanted.reshape(peers, kinds * cap), 'own', split_axis=0, c...  14.8 us
    pallas_call x1, Pallas kernels, body(): pl.pallas_call(first_body, in_specs=[smem] * 5 + [hbm], out_specs=hbm, ou...  11.8 us
    pallas_call x4, Pallas kernels, second(): pl.pallas_call(functools.partial(load_body if load else second_body, step...  11.8 us
    ppermute x4, waiting for transfers between devices, send(): lax.ppermute(value, 'red', [(i, (i // 2 + distance) % steps * 2 + i % 2)...  11.5 us
    ppermute x4, starting transfers between devices, met(): theirs = lax.ppermute(other, 'red', swap)  9.8 us
    all_to_all x1, waiting for transfers between devices, body(): lax.all_to_all(send_second, 'own', split_axis=0, concat_axis=0, tiled=True)  8.88 us
    ppermute x4, starting transfers between devices, send(): lax.ppermute(value, 'red', [(i, (i // 2 + distance) % steps * 2 + i % 2)...  5.36 us
  transfers between devices with their start and end apart: 9, of which 4 were waited for; matrix products, arithmetic and copies ran while one was open for 3% of the time, Pallas kernels for 12%

profile of v6, /device:TPU:1, one launch (start us, length us, event | category | flops | bytes accessed | tf_op | source)
XLA Modules:
  0.0 162.9 jit_solution(16865400273317145002)
XLA Ops:
  0.0 0.8 copy.22
  0.8 14.8 %all_to_all.22 = s32[16,1,16]{2,1,0:T(1,128)S(1)} all-to-all(s32[16,1,16]{2,1,0:T(1,128)S(1)} %copy.22), channel_id=1, replica_groups=mesh['own'=16,'red'=8] {'own'}, dimensions={0} | all-to-all | bytes 2048 | tf_op jit(solution)/shard_map/all_to_all | solution.py:188
  15.6 3.8 %shard_map.64 = (bf16[16,12,128,128]{3,2,1,0:T(8,128)(2,1)S(1)}, bf16[16,4,128,128]{3,2,1,0:T(8,128)(2,1)S(1)}) custom-call(s32[16,16]{1,0:T(8,128)S(1)} %bitcast.12, bf16[64,128,128]{2,1,0:T(8,128)(2,1)} %first_store.1, bf16[64,128,128]{2,1,0:T(8,128)(2,1)} %second_store.1), custom_call_target="tpu_custom_call" | custom-call | tf_op jit(solution)/shard_map/pallas_call | solution.py:51
  19.4 0.0 copy-start
  19.4 74.6 %all_to_all.23.got = bf16[16,12,128,128]{3,2,1,0:T(8,128)(2,1)} all-to-all(bf16[16,12,128,128]{3,2,1,0:T(8,128)(2,1)S(1)} %get-tuple-element.31), channel_id=1, replica_groups=mesh['own'=16,'red'=8] {'own'}, dimensions={0} | all-to-all | bytes 12582912 | tf_op jit(solution)/shard_map/all_to_all | solution.py:194
  94.0 0.0 copy-done
  94.0 3.9 %all-to-all-start.2 = ((bf16[16,4,128,128]{3,2,1,0:T(8,128)(2,1)}), bf16[16,4,128,128]{3,2,1,0:T(8,128)(2,1)S(1)}, u32[]{:S(2)}, u32[]{:S(2)}) async-start(bf16[16,4,128,128]{3,2,1,0:T(8,128)(2,1)} %copy-done), calls=%async_computation.2 | async-start | bytes 4194304 | tf_op jit(solution)/shard_map/all_to_all | solution.py:198
  97.9 0.0 copy-done.1
  97.9 0.0 copy-done.2
  97.9 0.0 copy-done.3
  97.9 0.1 multiply_add_fusion
  98.0 0.2 convert_reduce_fusion.2
  98.2 0.2 select_reduce_fusion.7
  98.4 0.1 select_reduce_fusion.5
  98.5 0.7 slice.18
  99.2 0.6 slice.19
  99.7 0.1 select_reduce_fusion
  99.9 0.1 select_reduce_fusion.2
  100.0 0.1 select_reduce_fusion.4
  100.1 0.1 copy.23
  100.2 1.0 sort.14
  101.2 0.1 copy.24
  101.3 0.1 select_select_fusion
  101.4 0.6 compare_select_fusion
  102.0 11.8 %shard_map.65.before = f32[32,128,128]{2,1,0:T(8,128)} custom-call(s32[32]{0:T(128)S(1)} %get-tuple-element.69.bounds, s32[32,72]{1,0:T(8,128)S(1)} %pad.15.left_at, s32[32,72]{1,0:T(8,128)S(1)} %pad.16.right_at, s32[3,264]{1,0:T(4,128)S(1)} %pad_add_fusion.3.table, s32[3,32]{1,0:T(4,128)S(1)} %get-tuple-element.65.ends, ...), custom_call_target="tpu_custom_call" | custom-call | tf_op jit(solution)/shard_map/pallas_call | solution.py:227
  113.9 0.7 compare_select_fusion.1
  114.6 8.9 %all-to-all-done.2.rest = bf16[16,4,128,128]{3,2,1,0:T(8,128)(2,1)S(1)} async-done(((bf16[16,4,128,128]{3,2,1,0:T(8,128)(2,1)}), bf16[16,4,128,128]{3,2,1,0:T(8,128)(2,1)S(1)}, u32[]{:S(2)}, u32[]{:S(2)}) %all-to-all-start.2) | async-done | bytes 2097184 | tf_op jit(solution)/shard_map/all_to_all | solution.py:198
  123.4 4.9 %shard_map.66 = (f32[4,128,128]{2,1,0:T(8,128)S(1)}, f32[4,128,128]{2,1,0:T(8,128)S(1)}, bf16[16,12,128,128]{3,2,1,0:T(8,128)(2,1)S(1)}) custom-call(s32[32]{0:T(128)S(1)} %get-tuple-element.70.bounds, s32[32,72]{1,0:T(8,128)S(1)} %pad.15.left_at, s32[32,72]{1,0:T(8,128)S(1)} %pad.16.right_at, s32[3,264]{1,0:T(4,128)S(1)} %pad_add_fusion.2.table, ...), custom_call_target="tpu_custom_call" | custom-call | tf_op jit(solution)/shard_map/pallas_call | solution.py:246
  128.3 5.8 %collective-permute-start.2 = (f32[4,128,128]{2,1,0:T(8,128)S(1)}, f32[4,128,128]{2,1,0:T(8,128)S(1)}, u32[]{:S(2)}, u32[]{:S(2)}) collective-permute-start(f32[4,128,128]{2,1,0:T(8,128)S(1)} %get-tuple-element.47), channel_id=1, source_target_pairs={{0,1},{1,0},{2,3},{3,2},{4,5},{5,4},{6,7},{7,6},{8,9},{9,8},{10,11... | collective-permute-start | bytes 786440 | tf_op jit(solution)/shard_map/ppermute | solution.py:263
  134.2 2.3 %shard_map.69 = (f32[4,128,128]{2,1,0:T(8,128)S(1)}, f32[4,128,128]{2,1,0:T(8,128)S(1)}) custom-call(s32[32]{0:T(128)S(1)} %get-tuple-element.70.bounds, s32[32,72]{1,0:T(8,128)S(1)} %pad.15.left_at, s32[32,72]{1,0:T(8,128)S(1)} %pad.16.right_at, s32[3,264]{1,0:T(4,128)S(1)} %pad_add_fusion.2.table, s32[3,32]{1,0:T(4,128)S(1)} %get-tuple-element.66.ends, ...), custom_call_target="tpu_custom_call" | custom-call | tf_op jit(solution)/shard_map/pallas_call | solution.py:246
  136.5 0.9 collective-permute-start.5
  137.4 0.0 collective-permute-done.2
  137.4 2.5 %collective-permute-start.6 = (f32[2,128,128]{2,1,0:T(8,128)S(1)}, f32[2,128,128]{2,1,0:T(8,128)S(1)}, u32[]{:S(2)}, u32[]{:S(2)}) collective-permute-start(f32[2,128,128]{2,1,0:T(8,128)S(1)} %get-tuple-element.62), channel_id=1, source_target_pairs={{0,6},{1,7},{2,0},{3,1},{4,2},{5,3},{6,4},{7,5},{8,14},{9,15},{10,... | collective-permute-start | bytes 393224 | tf_op jit(solution)/shard_map/ppermute | solution.py:267
  140.0 2.3 %shard_map.68 = (f32[4,128,128]{2,1,0:T(8,128)S(1)}, f32[4,128,128]{2,1,0:T(8,128)S(1)}) custom-call(s32[32]{0:T(128)S(1)} %get-tuple-element.70.bounds, s32[32,72]{1,0:T(8,128)S(1)} %pad.15.left_at, s32[32,72]{1,0:T(8,128)S(1)} %pad.16.right_at, s32[3,264]{1,0:T(4,128)S(1)} %pad_add_fusion.2.table, s32[3,32]{1,0:T(4,128)S(1)} %get-tuple-element.66.ends, ...), custom_call_target="tpu_custom_call" | custom-call | tf_op jit(solution)/shard_map/pallas_call | solution.py:246
  142.3 2.1 %collective-permute-start.1 = (f32[4,128,128]{2,1,0:T(8,128)S(1)}, f32[4,128,128]{2,1,0:T(8,128)S(1)}, u32[]{:S(2)}, u32[]{:S(2)}) collective-permute-start(f32[4,128,128]{2,1,0:T(8,128)S(1)} %get-tuple-element.45), channel_id=1, source_target_pairs={{0,1},{1,0},{2,3},{3,2},{4,5},{5,4},{6,7},{7,6},{8,9},{9,8},{10,11... | collective-permute-start | bytes 786440 | tf_op jit(solution)/shard_map/ppermute | solution.py:263
  144.4 2.3 %shard_map.67 = (f32[4,128,128]{2,1,0:T(8,128)S(1)}, f32[4,128,128]{2,1,0:T(8,128)S(1)}) custom-call(s32[32]{0:T(128)S(1)} %get-tuple-element.70.bounds, s32[32,72]{1,0:T(8,128)S(1)} %pad.15.left_at, s32[32,72]{1,0:T(8,128)S(1)} %pad.16.right_at, s32[3,264]{1,0:T(4,128)S(1)} %pad_add_fusion.2.table, s32[3,32]{1,0:T(4,128)S(1)} %get-tuple-element.66.ends, ...), custom_call_target="tpu_custom_call" | custom-call | tf_op jit(solution)/shard_map/pallas_call | solution.py:246
  146.8 0.9 collective-permute-start
  147.7 0.0 collective-permute-start.3
  147.7 0.0 collective-permute-done.5
  147.7 0.0 collective-permute-done.6
  147.7 2.7 %collective-permute-start.7 = (f32[4,128,128]{2,1,0:T(8,128)S(1)}, f32[4,128,128]{2,1,0:T(8,128)S(1)}, u32[]{:S(2)}, u32[]{:S(2)}) collective-permute-start(f32[4,128,128]{2,1,0:T(8,128)S(1)} %pad_add_fusion), channel_id=1, source_target_pairs={{0,6},{1,7},{2,0},{3,1},{4,2},{5,3},{6,4},{7,5},{8,14},{9,15},{10,... | collective-permute-start | bytes 786440 | tf_op jit(solution)/shard_map/ppermute | solution.py:267
  150.5 0.0 collective-permute-done.1
  150.5 3.4 %collective-permute-done.3 = f32[2,128,128]{2,1,0:T(8,128)S(1)} collective-permute-done((f32[2,128,128]{2,1,0:T(8,128)S(1)}, f32[2,128,128]{2,1,0:T(8,128)S(1)}, u32[]{:S(2)}, u32[]{:S(2)}) %collective-permute-start.3) | collective-permute-done | bytes 131104 | tf_op jit(solution)/shard_map/ppermute | solution.py:267
  153.9 0.1 collective-permute-start.4
  154.0 0.0 collective-permute-done
  154.0 1.8 %collective-permute-done.7 = f32[4,128,128]{2,1,0:T(8,128)S(1)} collective-permute-done((f32[4,128,128]{2,1,0:T(8,128)S(1)}, f32[4,128,128]{2,1,0:T(8,128)S(1)}, u32[]{:S(2)}, u32[]{:S(2)}) %collective-permute-start.7) | collective-permute-done | bytes 262176 | tf_op jit(solution)/shard_map/ppermute | solution.py:267
  155.8 6.3 %collective-permute-done.4 = f32[4,128,128]{2,1,0:T(8,128)S(1)} collective-permute-done((f32[4,128,128]{2,1,0:T(8,128)S(1)}, f32[4,128,128]{2,1,0:T(8,128)S(1)}, u32[]{:S(2)}, u32[]{:S(2)}) %collective-permute-start.4) | collective-permute-done | bytes 262176 | tf_op jit(solution)/shard_map/ppermute | solution.py:267
  162.1 0.8 add_add_fusion
  (21 shorter events, 0.2 us)
Async XLA Ops:
  19.4 74.6 %copy-start = (bf16[16,4,128,128]{3,2,1,0:T(8,128)(2,1)}, bf16[16,4,128,128]{3,2,1,0:T(8,128)(2,1)S(1)}, u32[]{:S(2)}) copy-start(bf16[16,4,128,128]{3,2,1,0:T(8,128)(2,1)S(1)} %get-tuple-element.40) | copy-start | bytes 6291460
  94.0 3.9 %copy-start.1 = (s32[32,1,64]{2,1,0:T(1,128)S(1)}, s32[32,1,64]{2,1,0:T(1,128)}, u32[]{:S(2)}) copy-start(s32[32,1,64]{2,1,0:T(1,128)} %param.10) | copy-start | bytes 24580
  94.0 3.9 %copy-start.2 = (s32[32,1,64]{2,1,0:T(1,128)S(1)}, s32[32,1,64]{2,1,0:T(1,128)}, u32[]{:S(2)}) copy-start(s32[32,1,64]{2,1,0:T(1,128)} %param.9) | copy-start | bytes 24580
  94.0 3.9 %copy-start.3 = (s32[32,1]{0,1:T(1,128)S(1)}, s32[32,1]{0,1:T(1,128)}, u32[]{:S(2)}) copy-start(s32[32,1]{0,1:T(1,128)} %param.11) | copy-start | bytes 388
  94.0 29.4 %all-to-all-start.2 = ((bf16[16,4,128,128]{3,2,1,0:T(8,128)(2,1)}), bf16[16,4,128,128]{3,2,1,0:T(8,128)(2,1)S(1)}, u32[]{:S(2)}, u32[]{:S(2)}) async-start(bf16[16,4,128,128]{3,2,1,0:T(8,128)(2,1)} %copy-done), calls=%async_computation.2 | async-start | bytes 4194304 | tf_op jit(solution)/shard_map/all_to_all | solution.py:198
  128.3 9.1 %collective-permute-start.2 = (f32[4,128,128]{2,1,0:T(8,128)S(1)}, f32[4,128,128]{2,1,0:T(8,128)S(1)}, u32[]{:S(2)}, u32[]{:S(2)}) collective-permute-start(f32[4,128,128]{2,1,0:T(8,128)S(1)} %get-tuple-element.47), channel_id=1, source_target_pairs={{0,1},{1,0},{2,3},{3,2},{4,5},{5,4},{6,7},{7,6},{8,9},{9,8},{10,11... | collective-permute-start | bytes 786440 | tf_op jit(solution)/shard_map/ppermute | solution.py:263
  136.5 11.2 %collective-permute-start.5 = (f32[4,128,128]{2,1,0:T(8,128)S(1)}, f32[4,128,128]{2,1,0:T(8,128)S(1)}, u32[]{:S(2)}, u32[]{:S(2)}) collective-permute-start(f32[4,128,128]{2,1,0:T(8,128)S(1)} %get-tuple-element.49), channel_id=1, source_target_pairs={{0,1},{1,0},{2,3},{3,2},{4,5},{5,4},{6,7},{7,6},{8,9},{9,8},{10,11... | collective-permute-start | bytes 786440 | tf_op jit(solution)/shard_map/ppermute | solution.py:263
  137.4 10.2 %collective-permute-start.6 = (f32[2,128,128]{2,1,0:T(8,128)S(1)}, f32[2,128,128]{2,1,0:T(8,128)S(1)}, u32[]{:S(2)}, u32[]{:S(2)}) collective-permute-start(f32[2,128,128]{2,1,0:T(8,128)S(1)} %get-tuple-element.62), channel_id=1, source_target_pairs={{0,6},{1,7},{2,0},{3,1},{4,2},{5,3},{6,4},{7,5},{8,14},{9,15},{10,... | collective-permute-start | bytes 393224 | tf_op jit(solution)/shard_map/ppermute | solution.py:267
  142.3 8.1 %collective-permute-start.1 = (f32[4,128,128]{2,1,0:T(8,128)S(1)}, f32[4,128,128]{2,1,0:T(8,128)S(1)}, u32[]{:S(2)}, u32[]{:S(2)}) collective-permute-start(f32[4,128,128]{2,1,0:T(8,128)S(1)} %get-tuple-element.45), channel_id=1, source_target_pairs={{0,1},{1,0},{2,3},{3,2},{4,5},{5,4},{6,7},{7,6},{8,9},{9,8},{10,11... | collective-permute-start | bytes 786440 | tf_op jit(solution)/shard_map/ppermute | solution.py:263
  146.8 7.2 %collective-permute-start = (f32[4,128,128]{2,1,0:T(8,128)S(1)}, f32[4,128,128]{2,1,0:T(8,128)S(1)}, u32[]{:S(2)}, u32[]{:S(2)}) collective-permute-start(f32[4,128,128]{2,1,0:T(8,128)S(1)} %get-tuple-element.43), channel_id=1, source_target_pairs={{0,1},{1,0},{2,3},{3,2},{4,5},{5,4},{6,7},{7,6},{8,9},{9,8},{10,11... | collective-permute-start | bytes 786440 | tf_op jit(solution)/shard_map/ppermute | solution.py:263
  147.7 6.2 %collective-permute-start.3 = (f32[2,128,128]{2,1,0:T(8,128)S(1)}, f32[2,128,128]{2,1,0:T(8,128)S(1)}, u32[]{:S(2)}, u32[]{:S(2)}) collective-permute-start(f32[2,128,128]{2,1,0:T(8,128)S(1)} %get-tuple-element.61), channel_id=1, source_target_pairs={{0,2},{1,3},{2,4},{3,5},{4,6},{5,7},{6,0},{7,1},{8,10},{9,11},{10,... | collective-permute-start | bytes 393224 | tf_op jit(solution)/shard_map/ppermute | solution.py:267
  147.7 8.0 %collective-permute-start.7 = (f32[4,128,128]{2,1,0:T(8,128)S(1)}, f32[4,128,128]{2,1,0:T(8,128)S(1)}, u32[]{:S(2)}, u32[]{:S(2)}) collective-permute-start(f32[4,128,128]{2,1,0:T(8,128)S(1)} %pad_add_fusion), channel_id=1, source_target_pairs={{0,6},{1,7},{2,0},{3,1},{4,2},{5,3},{6,4},{7,5},{8,14},{9,15},{10,... | collective-permute-start | bytes 786440 | tf_op jit(solution)/shard_map/ppermute | solution.py:267
  153.9 8.2 %collective-permute-start.4 = (f32[4,128,128]{2,1,0:T(8,128)S(1)}, f32[4,128,128]{2,1,0:T(8,128)S(1)}, u32[]{:S(2)}, u32[]{:S(2)}) collective-permute-start(f32[4,128,128]{2,1,0:T(8,128)S(1)} %pad_add_fusion.1), channel_id=1, source_target_pairs={{0,2},{1,3},{2,4},{3,5},{4,6},{5,7},{6,0},{7,1},{8,10},{9,11},{10,... | collective-permute-start | bytes 786440 | tf_op jit(solution)/shard_map/ppermute | solution.py:267

commit v7 on v6

--- a/solution.py
+++ b/solution.py
@@ -55,7 +55,10 @@
         out_specs=[
             pl.BlockSpec((peers // PACK_STEPS, len(picks)) + tile, lambda i: (i, 0, 0, 0)) for picks in lists
         ],
-        out_shape=[jax.ShapeDtypeStruct((peers, len(picks)) + tile, stores[0].dtype) for picks in lists],
+        out_shape=[
+            jax.ShapeDtypeStruct((peers, len(lists[0])) + tile, stores[0].dtype),
+            pltpu.HBM((peers, len(lists[1])) + tile, stores[0].dtype),
+        ],
         scratch_shapes=[pltpu.VMEM(store.shape, store.dtype) for store in stores]
         + [pltpu.SemaphoreType.DMA((2 * PARTS,))],
         compiler_params=pltpu.CompilerParams(vmem_limit_bytes=24 * 2**20),

time: 164 us -> 166 us (1.012)
  Pallas kernels: 27.4 us -> 29.9 us
    pallas_call x1, Pallas kernels: 3.8 us -> 6.23 us  [pack(): pl.pallas_call(functools.partial(pack_body, lists), grid=(PACK_STEPS,), i...]
  transfers between devices with their start and end apart: 9 -> 9, of which waited for: 4 -> 4; matrix products, arithmetic and copies ran while one was open for 3% -> 3% of each run, Pallas kernels for 12% -> 11%
where the time goes in v7:
time: 166 us; the launch traced here: 165 us
  blocking collectives  89.4 us (54%)
  Pallas kernels  29.9 us (18%)
  waiting for transfers between devices  20.4 us (12%)
  starting transfers between devices  19 us (11%)
  other arithmetic  4.15 us (3%)
  local copies, waits for them, and re-layouts  2.16 us (1%)
    all_to_all x1, blocking collectives, body(): lax.all_to_all(send_first, 'own', split_axis=0, concat_axis=0, tiled=True)  74.6 us
    all_to_all x1, blocking collectives, body(): lax.all_to_all(wanted.reshape(peers, kinds * cap), 'own', split_axis=0, c...  14.8 us
    pallas_call x4, Pallas kernels, second(): pl.pallas_call(functools.partial(load_body if load else second_body, step...  11.8 us
    pallas_call x1, Pallas kernels, body(): pl.pallas_call(first_body, in_specs=[smem] * 5 + [hbm], out_specs=hbm, ou...  11.8 us
    ppermute x4, waiting for transfers between devices, send(): lax.ppermute(value, 'red', [(i, (i // 2 + distance) % steps * 2 + i % 2)...  11.5 us
    ppermute x4, starting transfers between devices, met(): theirs = lax.ppermute(other, 'red', swap)  9.79 us
    all_to_all x1, waiting for transfers between devices, body(): lax.all_to_all(send_second, 'own', split_axis=0, concat_axis=0, tiled=True)  8.88 us
    pallas_call x1, Pallas kernels, pack(): pl.pallas_call(functools.partial(pack_body, lists), grid=(PACK_STEPS,), i...  6.23 us
  transfers between devices with their start and end apart: 9, of which 4 were waited for; matrix products, arithmetic and copies ran while one was open for 3% of the time, Pallas kernels for 11%

profile of v7, /device:TPU:1, one launch (start us, length us, event | category | flops | bytes accessed | tf_op | source)
XLA Modules:
  0.0 165.3 jit_solution(3274199140465832613)
XLA Ops:
  0.0 0.8 copy.22
  0.8 14.8 %all_to_all.22 = s32[16,1,16]{2,1,0:T(1,128)S(1)} all-to-all(s32[16,1,16]{2,1,0:T(1,128)S(1)} %copy.22), channel_id=1, replica_groups=mesh['own'=16,'red'=8] {'own'}, dimensions={0} | all-to-all | bytes 2048 | tf_op jit(solution)/shard_map/all_to_all | solution.py:191
  15.6 6.2 %shard_map.64 = (bf16[16,12,128,128]{3,2,1,0:T(8,128)(2,1)S(1)}, bf16[16,4,128,128]{3,2,1,0:T(8,128)(2,1)}) custom-call(s32[16,16]{1,0:T(8,128)S(1)} %bitcast.12, bf16[64,128,128]{2,1,0:T(8,128)(2,1)} %first_store.1, bf16[64,128,128]{2,1,0:T(8,128)(2,1)} %second_store.1), custom_call_target="tpu_custom_call" | custom-call | tf_op jit(solution)/shard_map/pallas_call | solution.py:51
  21.8 74.6 %all_to_all.23.got = bf16[16,12,128,128]{3,2,1,0:T(8,128)(2,1)} all-to-all(bf16[16,12,128,128]{3,2,1,0:T(8,128)(2,1)S(1)} %get-tuple-element.31), channel_id=1, replica_groups=mesh['own'=16,'red'=8] {'own'}, dimensions={0} | all-to-all | bytes 12582912 | tf_op jit(solution)/shard_map/all_to_all | solution.py:197
  96.4 0.0 copy-start
  96.4 0.0 copy-start.1
  96.5 3.8 %all-to-all-start.2 = ((bf16[16,4,128,128]{3,2,1,0:T(8,128)(2,1)}), bf16[16,4,128,128]{3,2,1,0:T(8,128)(2,1)S(1)}, u32[]{:S(2)}, u32[]{:S(2)}) async-start(bf16[16,4,128,128]{3,2,1,0:T(8,128)(2,1)} %get-tuple-element.40), calls=%async_computation.2 | async-start | bytes 4194304 | tf_op jit(solution)/shard_map/all_to_all | solution.py:201
  100.3 0.0 copy-done
  100.3 0.0 copy-done.1
  100.3 0.0 copy-done.2
  100.3 0.1 multiply_add_fusion
  100.4 0.2 convert_reduce_fusion.2
  100.6 0.2 select_reduce_fusion.7
  100.8 0.1 select_reduce_fusion.5
  100.9 0.7 slice.18
  101.6 0.6 slice.19
  102.1 0.1 select_reduce_fusion
  102.3 0.1 select_reduce_fusion.2
  102.4 0.1 select_reduce_fusion.4
  102.5 0.1 copy.23
  102.6 1.0 sort.14
  103.6 0.1 copy.24
  103.7 0.1 select_select_fusion
  103.8 0.6 compare_select_fusion
  104.4 11.8 %shard_map.65.before = f32[32,128,128]{2,1,0:T(8,128)} custom-call(s32[32]{0:T(128)S(1)} %get-tuple-element.69.bounds, s32[32,72]{1,0:T(8,128)S(1)} %pad.15.left_at, s32[32,72]{1,0:T(8,128)S(1)} %pad.16.right_at, s32[3,264]{1,0:T(4,128)S(1)} %pad_add_fusion.3.table, s32[3,32]{1,0:T(4,128)S(1)} %get-tuple-element.65.ends, ...), custom_call_target="tpu_custom_call" | custom-call | tf_op jit(solution)/shard_map/pallas_call | solution.py:230
  116.3 0.7 compare_select_fusion.1
  117.0 8.9 %all-to-all-done.2.rest = bf16[16,4,128,128]{3,2,1,0:T(8,128)(2,1)S(1)} async-done(((bf16[16,4,128,128]{3,2,1,0:T(8,128)(2,1)}), bf16[16,4,128,128]{3,2,1,0:T(8,128)(2,1)S(1)}, u32[]{:S(2)}, u32[]{:S(2)}) %all-to-all-start.2) | async-done | bytes 2097184 | tf_op jit(solution)/shard_map/all_to_all | solution.py:201
  125.8 4.9 %shard_map.66 = (f32[4,128,128]{2,1,0:T(8,128)S(1)}, f32[4,128,128]{2,1,0:T(8,128)S(1)}, bf16[16,12,128,128]{3,2,1,0:T(8,128)(2,1)S(1)}) custom-call(s32[32]{0:T(128)S(1)} %get-tuple-element.70.bounds, s32[32,72]{1,0:T(8,128)S(1)} %pad.15.left_at, s32[32,72]{1,0:T(8,128)S(1)} %pad.16.right_at, s32[3,264]{1,0:T(4,128)S(1)} %pad_add_fusion.2.table, ...), custom_call_target="tpu_custom_call" | custom-call | tf_op jit(solution)/shard_map/pallas_call | solution.py:249
  130.7 5.8 %collective-permute-start.2 = (f32[4,128,128]{2,1,0:T(8,128)S(1)}, f32[4,128,128]{2,1,0:T(8,128)S(1)}, u32[]{:S(2)}, u32[]{:S(2)}) collective-permute-start(f32[4,128,128]{2,1,0:T(8,128)S(1)} %get-tuple-element.47), channel_id=1, source_target_pairs={{0,1},{1,0},{2,3},{3,2},{4,5},{5,4},{6,7},{7,6},{8,9},{9,8},{10,11... | collective-permute-start | bytes 786440 | tf_op jit(solution)/shard_map/ppermute | solution.py:266
  136.6 2.3 %shard_map.69 = (f32[4,128,128]{2,1,0:T(8,128)S(1)}, f32[4,128,128]{2,1,0:T(8,128)S(1)}) custom-call(s32[32]{0:T(128)S(1)} %get-tuple-element.70.bounds, s32[32,72]{1,0:T(8,128)S(1)} %pad.15.left_at, s32[32,72]{1,0:T(8,128)S(1)} %pad.16.right_at, s32[3,264]{1,0:T(4,128)S(1)} %pad_add_fusion.2.table, s32[3,32]{1,0:T(4,128)S(1)} %get-tuple-element.66.ends, ...), custom_call_target="tpu_custom_call" | custom-call | tf_op jit(solution)/shard_map/pallas_call | solution.py:249
  138.9 0.9 collective-permute-start.5
  139.8 0.0 collective-permute-done.2
  139.8 2.5 %collective-permute-start.6 = (f32[2,128,128]{2,1,0:T(8,128)S(1)}, f32[2,128,128]{2,1,0:T(8,128)S(1)}, u32[]{:S(2)}, u32[]{:S(2)}) collective-permute-start(f32[2,128,128]{2,1,0:T(8,128)S(1)} %get-tuple-element.62), channel_id=1, source_target_pairs={{0,6},{1,7},{2,0},{3,1},{4,2},{5,3},{6,4},{7,5},{8,14},{9,15},{10,... | collective-permute-start | bytes 393224 | tf_op jit(solution)/shard_map/ppermute | solution.py:270
  142.4 2.3 %shard_map.68 = (f32[4,128,128]{2,1,0:T(8,128)S(1)}, f32[4,128,128]{2,1,0:T(8,128)S(1)}) custom-call(s32[32]{0:T(128)S(1)} %get-tuple-element.70.bounds, s32[32,72]{1,0:T(8,128)S(1)} %pad.15.left_at, s32[32,72]{1,0:T(8,128)S(1)} %pad.16.right_at, s32[3,264]{1,0:T(4,128)S(1)} %pad_add_fusion.2.table, s32[3,32]{1,0:T(4,128)S(1)} %get-tuple-element.66.ends, ...), custom_call_target="tpu_custom_call" | custom-call | tf_op jit(solution)/shard_map/pallas_call | solution.py:249
  144.7 2.1 %collective-permute-start.1 = (f32[4,128,128]{2,1,0:T(8,128)S(1)}, f32[4,128,128]{2,1,0:T(8,128)S(1)}, u32[]{:S(2)}, u32[]{:S(2)}) collective-permute-start(f32[4,128,128]{2,1,0:T(8,128)S(1)} %get-tuple-element.45), channel_id=1, source_target_pairs={{0,1},{1,0},{2,3},{3,2},{4,5},{5,4},{6,7},{7,6},{8,9},{9,8},{10,11... | collective-permute-start | bytes 786440 | tf_op jit(solution)/shard_map/ppermute | solution.py:266
  146.8 2.3 %shard_map.67 = (f32[4,128,128]{2,1,0:T(8,128)S(1)}, f32[4,128,128]{2,1,0:T(8,128)S(1)}) custom-call(s32[32]{0:T(128)S(1)} %get-tuple-element.70.bounds, s32[32,72]{1,0:T(8,128)S(1)} %pad.15.left_at, s32[32,72]{1,0:T(8,128)S(1)} %pad.16.right_at, s32[3,264]{1,0:T(4,128)S(1)} %pad_add_fusion.2.table, s32[3,32]{1,0:T(4,128)S(1)} %get-tuple-element.66.ends, ...), custom_call_target="tpu_custom_call" | custom-call | tf_op jit(solution)/shard_map/pallas_call | solution.py:249
  149.2 0.9 collective-permute-start
  150.1 0.0 collective-permute-start.3
  150.1 0.0 collective-permute-done.5
  150.1 0.0 collective-permute-done.6
  150.1 2.7 %collective-permute-start.7 = (f32[4,128,128]{2,1,0:T(8,128)S(1)}, f32[4,128,128]{2,1,0:T(8,128)S(1)}, u32[]{:S(2)}, u32[]{:S(2)}) collective-permute-start(f32[4,128,128]{2,1,0:T(8,128)S(1)} %pad_add_fusion), channel_id=1, source_target_pairs={{0,6},{1,7},{2,0},{3,1},{4,2},{5,3},{6,4},{7,5},{8,14},{9,15},{10,... | collective-permute-start | bytes 786440 | tf_op jit(solution)/shard_map/ppermute | solution.py:270
  152.9 0.0 collective-permute-done.1
  152.9 3.4 %collective-permute-done.3 = f32[2,128,128]{2,1,0:T(8,128)S(1)} collective-permute-done((f32[2,128,128]{2,1,0:T(8,128)S(1)}, f32[2,128,128]{2,1,0:T(8,128)S(1)}, u32[]{:S(2)}, u32[]{:S(2)}) %collective-permute-start.3) | collective-permute-done | bytes 131104 | tf_op jit(solution)/shard_map/ppermute | solution.py:270
  156.3 0.1 collective-permute-start.4
  156.4 0.0 collective-permute-done
  156.4 1.8 %collective-permute-done.7 = f32[4,128,128]{2,1,0:T(8,128)S(1)} collective-permute-done((f32[4,128,128]{2,1,0:T(8,128)S(1)}, f32[4,128,128]{2,1,0:T(8,128)S(1)}, u32[]{:S(2)}, u32[]{:S(2)}) %collective-permute-start.7) | collective-permute-done | bytes 262176 | tf_op jit(solution)/shard_map/ppermute | solution.py:270
  158.2 6.3 %collective-permute-done.4 = f32[4,128,128]{2,1,0:T(8,128)S(1)} collective-permute-done((f32[4,128,128]{2,1,0:T(8,128)S(1)}, f32[4,128,128]{2,1,0:T(8,128)S(1)}, u32[]{:S(2)}, u32[]{:S(2)}) %collective-permute-start.4) | collective-permute-done | bytes 262176 | tf_op jit(solution)/shard_map/ppermute | solution.py:270
  164.5 0.8 add_add_fusion
  (19 shorter events, 0.2 us)
Async XLA Ops:
  96.4 3.9 %copy-start = (s32[32,1,64]{2,1,0:T(1,128)S(1)}, s32[32,1,64]{2,1,0:T(1,128)}, u32[]{:S(2)}) copy-start(s32[32,1,64]{2,1,0:T(1,128)} %param.10) | copy-start | bytes 24580
  96.4 3.9 %copy-start.1 = (s32[32,1,64]{2,1,0:T(1,128)S(1)}, s32[32,1,64]{2,1,0:T(1,128)}, u32[]{:S(2)}) copy-start(s32[32,1,64]{2,1,0:T(1,128)} %param.9) | copy-start | bytes 24580
  96.5 3.9 %copy-start.2 = (s32[32,1]{0,1:T(1,128)S(1)}, s32[32,1]{0,1:T(1,128)}, u32[]{:S(2)}) copy-start(s32[32,1]{0,1:T(1,128)} %param.11) | copy-start | bytes 388
  96.5 29.4 %all-to-all-start.2 = ((bf16[16,4,128,128]{3,2,1,0:T(8,128)(2,1)}), bf16[16,4,128,128]{3,2,1,0:T(8,128)(2,1)S(1)}, u32[]{:S(2)}, u32[]{:S(2)}) async-start(bf16[16,4,128,128]{3,2,1,0:T(8,128)(2,1)} %get-tuple-element.40), calls=%async_computation.2 | async-start | bytes 4194304 | tf_op jit(solution)/shard_map/all_to_all | solution.py:201
  130.7 9.1 %collective-permute-start.2 = (f32[4,128,128]{2,1,0:T(8,128)S(1)}, f32[4,128,128]{2,1,0:T(8,128)S(1)}, u32[]{:S(2)}, u32[]{:S(2)}) collective-permute-start(f32[4,128,128]{2,1,0:T(8,128)S(1)} %get-tuple-element.47), channel_id=1, source_target_pairs={{0,1},{1,0},{2,3},{3,2},{4,5},{5,4},{6,7},{7,6},{8,9},{9,8},{10,11... | collective-permute-start | bytes 786440 | tf_op jit(solution)/shard_map/ppermute | solution.py:266
  138.9 11.2 %collective-permute-start.5 = (f32[4,128,128]{2,1,0:T(8,128)S(1)}, f32[4,128,128]{2,1,0:T(8,128)S(1)}, u32[]{:S(2)}, u32[]{:S(2)}) collective-permute-start(f32[4,128,128]{2,1,0:T(8,128)S(1)} %get-tuple-element.49), channel_id=1, source_target_pairs={{0,1},{1,0},{2,3},{3,2},{4,5},{5,4},{6,7},{7,6},{8,9},{9,8},{10,11... | collective-permute-start | bytes 786440 | tf_op jit(solution)/shard_map/ppermute | solution.py:266
  139.8 10.2 %collective-permute-start.6 = (f32[2,128,128]{2,1,0:T(8,128)S(1)}, f32[2,128,128]{2,1,0:T(8,128)S(1)}, u32[]{:S(2)}, u32[]{:S(2)}) collective-permute-start(f32[2,128,128]{2,1,0:T(8,128)S(1)} %get-tuple-element.62), channel_id=1, source_target_pairs={{0,6},{1,7},{2,0},{3,1},{4,2},{5,3},{6,4},{7,5},{8,14},{9,15},{10,... | collective-permute-start | bytes 393224 | tf_op jit(solution)/shard_map/ppermute | solution.py:270
  144.7 8.1 %collective-permute-start.1 = (f32[4,128,128]{2,1,0:T(8,128)S(1)}, f32[4,128,128]{2,1,0:T(8,128)S(1)}, u32[]{:S(2)}, u32[]{:S(2)}) collective-permute-start(f32[4,128,128]{2,1,0:T(8,128)S(1)} %get-tuple-element.45), channel_id=1, source_target_pairs={{0,1},{1,0},{2,3},{3,2},{4,5},{5,4},{6,7},{7,6},{8,9},{9,8},{10,11... | collective-permute-start | bytes 786440 | tf_op jit(solution)/shard_map/ppermute | solution.py:266
  149.2 7.2 %collective-permute-start = (f32[4,128,128]{2,1,0:T(8,128)S(1)}, f32[4,128,128]{2,1,0:T(8,128)S(1)}, u32[]{:S(2)}, u32[]{:S(2)}) collective-permute-start(f32[4,128,128]{2,1,0:T(8,128)S(1)} %get-tuple-element.43), channel_id=1, source_target_pairs={{0,1},{1,0},{2,3},{3,2},{4,5},{5,4},{6,7},{7,6},{8,9},{9,8},{10,11... | collective-permute-start | bytes 786440 | tf_op jit(solution)/shard_map/ppermute | solution.py:266
  150.1 6.2 %collective-permute-start.3 = (f32[2,128,128]{2,1,0:T(8,128)S(1)}, f32[2,128,128]{2,1,0:T(8,128)S(1)}, u32[]{:S(2)}, u32[]{:S(2)}) collective-permute-start(f32[2,128,128]{2,1,0:T(8,128)S(1)} %get-tuple-element.61), channel_id=1, source_target_pairs={{0,2},{1,3},{2,4},{3,5},{4,6},{5,7},{6,0},{7,1},{8,10},{9,11},{10,... | collective-permute-start | bytes 393224 | tf_op jit(solution)/shard_map/ppermute | solution.py:270
  150.1 8.0 %collective-permute-start.7 = (f32[4,128,128]{2,1,0:T(8,128)S(1)}, f32[4,128,128]{2,1,0:T(8,128)S(1)}, u32[]{:S(2)}, u32[]{:S(2)}) collective-permute-start(f32[4,128,128]{2,1,0:T(8,128)S(1)} %pad_add_fusion), channel_id=1, source_target_pairs={{0,6},{1,7},{2,0},{3,1},{4,2},{5,3},{6,4},{7,5},{8,14},{9,15},{10,... | collective-permute-start | bytes 786440 | tf_op jit(solution)/shard_map/ppermute | solution.py:270
  156.3 8.2 %collective-permute-start.4 = (f32[4,128,128]{2,1,0:T(8,128)S(1)}, f32[4,128,128]{2,1,0:T(8,128)S(1)}, u32[]{:S(2)}, u32[]{:S(2)}) collective-permute-start(f32[4,128,128]{2,1,0:T(8,128)S(1)} %pad_add_fusion.1), channel_id=1, source_target_pairs={{0,2},{1,3},{2,4},{3,5},{4,6},{5,7},{6,0},{7,1},{8,10},{9,11},{10,... | collective-permute-start | bytes 786440 | tf_op jit(solution)/shard_map/ppermute | solution.py:270
